TPU v7x, 32 devices: a whole 2x2x4 slice. The times are simulated.
32 devices in a mesh: groups: 2 (over x), row: 8 (over z, y), col: 2 (over core).
Axes of the slice: x: 2, y: 2, z: 4, core: 2. Of those that a mesh axis runs over, the one named last changes fastest.
Arguments:
- inverse: float32 [16, 2, 128, 2048], P('groups', 'col', None, 'row'), parts along dimension 0, as said below
- features: float32 [16384, 1024], P(('groups', 'row')), parts along dimension 0, may hold values from -6 to 6
- residual: float32 [16384, 256], P(('groups', 'row')), parts along dimension 0, may hold values from -6 to 6
- block_ids: int32 [4096], P(('groups', 'row')), parts along dimension 0, may hold values from 0 to 8191, as said below
Outputs:
- updated: float32 [16384, 256], P(('groups', 'row'), 'col'), parts along dimension 0
There are 2 independent parts, one for each index of `groups`. A program takes and returns all parts, laid end to end along the dimension named above; each array names one. Nothing has to cross between parts.
Inputs may be any that keep to these rules, and one draw needn't show every extreme that they name: `block_ids`: the ids at block positions a * 256 to (a + 1) * 256 - 1 are distinct and lie in a * 1024 to (a + 1) * 1024 - 1. `inverse`: read as a [2048, 2048] matrix, each row is a positive scale between 0.3 and 3.4 times an identity row plus small independent entries.
All inputs are finite; a program needn't handle non-finite values.
Results may differ from a plain program's by a relative error of at most 0.000084.
Values sent between devices are 32-bit elements; how exact they have to be, the bound alone decides.
No kernel may reach another device: no remote copies, remote signals or barrier semaphores. Data moves between devices by JAX's collectives and lax.ppermute only.
A program may use at most 128 MiB of HBM per device.

v0:
```python
import jax
import jax.numpy as jnp
from jax import lax
from jax.sharding import PartitionSpec as P


def kernel_apply(features, block_x, block_corr):
    gram = jnp.dot(
        features, block_x.T, precision=lax.Precision.HIGHEST, preferred_element_type=jnp.float32
    )
    kern = (gram / block_x.shape[1] + 0.5) ** 2
    return jnp.dot(
        kern, block_corr, precision=lax.Precision.HIGHEST, preferred_element_type=jnp.float32
    )


def on_device(inverse, features, residual, block_ids):
    rows_here = features.shape[0]
    local_ids = block_ids - lax.axis_index("row") * rows_here
    block_res = jnp.take(residual, local_ids, axis=0)
    half_count = block_ids.shape[0] // lax.axis_size("col")
    own_ids = lax.dynamic_slice_in_dim(local_ids, lax.axis_index("col") * half_count, half_count)
    block_x = jnp.take(features, own_ids, axis=0)
    inv_rows = inverse.reshape(-1, inverse.shape[-1])
    partial_value = jnp.dot(
        inv_rows, block_res, precision=lax.Precision.HIGHEST, preferred_element_type=jnp.float32
    )
    corr_whole = lax.psum(partial_value, "row")
    change = kernel_apply(features, lax.all_gather(block_x, "row", axis=0, tiled=True), corr_whole)
    summed = lax.psum_scatter(change, "col", scatter_dimension=1, tiled=True)
    width = summed.shape[1]
    own_res = lax.dynamic_slice_in_dim(residual, lax.axis_index("col") * width, width, 1)
    return own_res - summed


def solution(mesh):
    return jax.shard_map(
        on_device,
        mesh=mesh,
        in_specs=(
            P("groups", "col", None, "row"),
            P(("groups", "row"), None),
            P(("groups", "row"), None),
            P(("groups", "row")),
        ),
        out_specs=P(("groups", "row"), "col"),
        check_vma=False,
    )
```

profile of v0, /device:TPU:25, one launch (start us, length us, event | category | flops | bytes accessed | tf_op | source)
XLA Modules:
  0.0 193.3 jit_solution(6805193917286604821)
XLA Ops:
  6.5 0.0 copy-start
  6.5 0.0 copy-start.1
  6.5 0.0 all-gather.2.cloned.1.call-start
  6.5 0.8 compare_and_fusion
  7.4 0.1 compare_and_fusion.1
  7.5 3.2 %gather_fusion = f32[128,1024]{1,0:T(8,128)S(1)} fusion(f32[1024,1024]{1,0:T(8,128)} %param.5, s32[1024]{0:T(1024)S(1)} %pad_clamp_fusion.1), kind=kCustom, calls=%fused_computation | custom fusion | bytes 1049088 | tf_op jit(solution)/shard_map/jit(_take)/gather | solution.py:23
  10.7 0.9 broadcast_select_fusion
  11.6 0.0 all-gather.2.cloned.1.call-update
  11.6 0.0 all-reduce.2.cloned.1.call-start
  11.7 0.0 copy-done.1
  11.7 1.0 gather_fusion.1
  12.7 0.0 copy-done
  12.7 2.9 %convolution_bitcast_fusion = f32[1024,256]{0,1:T(8,128)} fusion(f32[1024,256]{1,0:T(8,128)S(1)} %bitcast.7, f32[256,256]{1,0:T(8,128)S(1)} %gather_fusion.1, pred[256]{0:T(512)(128)(4,1)S(1)} %get-tuple-element.7), kind=kOutput, calls=%fused_computation.8 | convolution fusion | flops 805371904 | bytes 2359552 | tf_op jit(solution)/shard_map/dot_general | solution.py:25
  15.6 0.0 all-reduce.2.cloned.1.call-update
  15.6 0.0 reduce-scatter.2.cloned.1.call-start
  15.7 68.3 %all-gather.2.cloned.1.call-done = f32[1024,1024]{1,0:T(8,128)} async-done(((f32[128,1024]{1,0:T(8,128)}), f32[1024,1024]{1,0:T(8,128)}) %all-gather.2.cloned.1.call-update) | async-done | bytes 4194320 | tf_op jit(solution)/shard_map/all_gather | solution.py:29
  84.0 17.6 %fusion.12 = f32[1024,1024]{1,0:T(8,128)} fusion(f32[1024,1024]{1,0:T(8,128)} %all-gather.2.cloned.1.call-done, f32[1024,1024]{1,0:T(8,128)} %param.5), kind=kOutput, calls=%fused_computation.24 | convolution fusion | flops 12884901888 | bytes 12582912 | tf_op jit(solution)/shard_map/dot_general | solution.py:8
  101.6 62.1 %all-reduce.2.cloned.1.call-done = f32[1024,256]{0,1:T(8,128)} async-done(((f32[1024,256]{0,1:T(8,128)}), f32[1024,256]{0,1:T(8,128)}) %all-reduce.2.cloned.1.call-update) | async-done | bytes 1048592 | tf_op jit(solution)/shard_map/psum | solution.py:28
  163.7 10.2 %fusion = f32[1024,256]{1,0:T(8,128)} fusion(f32[1024,256]{0,1:T(8,128)} %all-reduce.2.cloned.1.call-done, f32[1024,1024]{1,0:T(8,128)} %fusion.12), kind=kOutput, calls=%fused_computation.2 | convolution fusion | flops 3224371200 | bytes 6291456 | tf_op jit(solution)/shard_map/dot_general | solution.py:12
  173.8 0.0 reduce-scatter.2.cloned.1.call-update
  173.9 11.0 %reduce-scatter.2.cloned.1.call-done = f32[1024,128]{1,0:T(8,128)} async-done(((f32[1024,256]{1,0:T(8,128)}), f32[1024,128]{1,0:T(8,128)}) %reduce-scatter.2.cloned.1.call-update) | async-done | bytes 524304 | tf_op jit(solution)/shard_map/reduce_scatter | solution.py:30
  184.9 1.9 dynamic-slice_subtract_fusion
  (3 shorter events, 0.0 us)
Async XLA Ops:
  6.5 6.1 %copy-start = (f32[8,1,128,256]{3,2,1,0:T(8,128)S(1)}, f32[8,1,128,256]{3,2,1,0:T(8,128)}, u32[]{:S(2)}) copy-start(f32[8,1,128,256]{3,2,1,0:T(8,128)} %param.4) | copy-start | bytes 3145732
  6.5 5.2 %copy-start.1 = (f32[1024,256]{1,0:T(8,128)S(1)}, f32[1024,256]{1,0:T(8,128)}, u32[]{:S(2)}) copy-start(f32[1024,256]{1,0:T(8,128)} %param.6) | copy-start | bytes 3145732
  6.5 77.4 %all-gather.2.cloned.1.call-start = ((), (), s32[]{:S(2)}) async-start(), calls=%async_computation.1 | async-start | bytes 4718592 | tf_op jit(solution)/shard_map/all_gather | solution.py:29
  11.6 152.0 %all-reduce.2.cloned.1.call-start = ((), (), s32[]{:S(2)}) async-start(), calls=%async_computation.2 | async-start | bytes 2097152 | tf_op jit(solution)/shard_map/psum | solution.py:28
  15.6 169.3 %reduce-scatter.2.cloned.1.call-start = ((), (), s32[]{:S(2)}) async-start(), calls=%async_computation.3 | async-start | bytes 1572864 | tf_op jit(solution)/shard_map/reduce_scatter | solution.py:30
Sparse Core Ops, SparseCore 0:
  11.7 72.1 all-gather.1
  87.5 76.1 all-reduce.1
  174.0 10.8 reduce-scatter.1
where the time goes:
time: 195 us; the launch traced here: 193 us
  waiting for transfers between devices  142 us (73%)
  matrix products  30.6 us (16%)
  between operations  13.2 us (7%)
  local copies, waits for them, and re-layouts  4.21 us (2%)
  other arithmetic  3.74 us (2%)
    all_gather x1, waiting for transfers between devices, on_device(): lax.all_gather(block_x, 'row', axis=0, tiled=True)  68.3 us
    psum x1, waiting for transfers between devices, on_device(): corr_whole = lax.psum(partial_value, 'row')  62.1 us
    dot_general x1, matrix products, kernel_apply(): jnp.dot(features, block_x.T, precision=lax.Precision.HIGHEST, preferred_e...  17.6 us
    reduce_scatter x1, waiting for transfers between devices, on_device(): summed = lax.psum_scatter(change, 'col', scatter_dimension=1, tiled=True)  11 us
    dot_general x1, matrix products, kernel_apply(): jnp.dot(kern, block_corr, precision=lax.Precision.HIGHEST, preferred_elem...  10.2 us
  transfers between devices with their start and end apart: 3, of which 3 were waited for; matrix products, arithmetic and copies ran while one was open for 11% of the time, Pallas kernels for 0%

commit v1 on v0

v1 whole, which is shorter than its diff:
```python
import numpy as np
import jax
import jax.numpy as jnp
from jax import lax
from jax.sharding import PartitionSpec as P

HIGH = lax.Precision.HIGH


def dot(a, b, dims=(((1,), (0,)), ((), ()))):
    return lax.dot_general(a, b, dims, precision=HIGH, preferred_element_type=jnp.float32)


def line_streams(own, depth, width):
    def shift(x, sources, step):
        pairs = [((z * width + y), ((z + step) * width + y)) for z in sources for y in range(width)]
        return lax.ppermute(x, "row", pairs)

    def across(x, places):
        pairs = [(z * width + y, z * width + (width - 1 - y)) for z in places for y in range(width)]
        return lax.ppermute(x, "row", pairs)

    got, crossed = {}, {}
    up = down = own
    crossed[0] = across(own, range(depth)) if width > 1 else None
    for s in range(1, depth):
        up = got[-s] = shift(up, range(s - 1, depth - 1), 1)
        down = got[s] = shift(down, range(1, depth - s + 1), -1)
        if width > 1:
            crossed[-s] = across(up, range(s, depth))
            crossed[s] = across(down, range(0, depth - s))
    return got, crossed


def arrivals(depth):
    table = []
    for z in range(depth):
        order = [(s, -s) for s in range(1, depth) if z - s >= 0] + [(s, s) for s in range(1, depth) if z + s < depth]
        table.append([off for _, off in sorted(order, key=lambda e: (e[0], e[1] > 0))])
    return np.array(table, np.int32).reshape(depth, depth - 1)


def pick(z, column, parts):
    out = None
    for off in sorted(set(column.tolist())):
        here = parts[off]
        if out is None:
            out = here
        else:
            mask = jnp.asarray((column == off))[z]
            out = jnp.where(mask, here, out)
    return out


def reduce_all(blocks, bits):
    n = len(blocks)
    pairs_of = {b: [(r, r ^ b) for r in range(n)] for b in bits}
    live = {k: blocks[k] for k in range(n)}
    for b in bits:
        send = [k for k in sorted(live) if k & b]
        moved = lax.ppermute(jnp.concatenate([live[k] for k in send], 0), "row", pairs_of[b])
        rows = live[send[0]].shape[0]
        live = {k ^ b: live[k ^ b] + moved[i * rows:(i + 1) * rows] for i, k in enumerate(send)}
    for b in reversed(bits):
        have = sorted(live)
        moved = lax.ppermute(jnp.concatenate([live[k] for k in have], 0), "row", pairs_of[b])
        rows = live[have[0]].shape[0]
        for i, k in enumerate(have):
            live[k ^ b] = moved[i * rows:(i + 1) * rows]
    return jnp.stack([live[k] for k in range(n)])


def on_device(inverse, features, residual, block_ids):
    n = lax.axis_size("row")
    me, col = lax.axis_index("row"), lax.axis_index("col")
    cols = lax.axis_size("col")
    width = 2 if n % 2 == 0 else 1
    depth = n // width
    z, y = me // width, me % width
    rows_here, feats = features.shape
    local_ids = block_ids - me * rows_here
    half = block_ids.shape[0] // cols
    own_ids = lax.dynamic_slice_in_dim(local_ids, col * half, half)
    own_x = jnp.take(features, own_ids, axis=0, mode="clip")
    block_res = jnp.take(residual, local_ids, axis=0, mode="clip")

    partial = dot(inverse.reshape(-1, inverse.shape[-1]), block_res).reshape(n, half, -1)
    relative = jnp.take(partial, me ^ jnp.arange(n), axis=0, mode="clip")
    rhs = partial.shape[-1] // cols
    bits = [1 << i for i in range(n.bit_length() - 1)]
    orders = [bits[1:] + bits[:1], bits]
    sums = []
    for h in range(cols):
        part = relative[:, :, h * rhs:(h + 1) * rhs]
        sums.append(reduce_all([part[k] for k in range(n)], orders[h % 2]))

    got, crossed = line_streams(own_x, depth, width)
    table = arrivals(depth)
    got[0] = own_x

    def kern(xs):
        gram = dot(features, jnp.concatenate(xs, 0), (((1,), (1,)), ((), ())))
        return (gram / feats + 0.5) ** 2

    kerns, owners = [], []
    for j in range(-1, depth - 1):
        column = np.zeros(depth, np.int32) if j < 0 else table[:, j]
        xs = [pick(z, column, got)]
        place = z + jnp.asarray(column)[z]
        owners.append(place * width + y)
        if width > 1:
            xs.append(pick(z, column, crossed))
            owners.append(place * width + (width - 1 - y))
        kerns.append(kern(xs))
    kernel = jnp.concatenate(kerns, 1)
    order = jnp.stack(owners) ^ me
    corr = [jnp.take(s, order, axis=0, mode="clip").reshape(-1, rhs) for s in sums]
    other = jnp.where(col == 0, corr[1], corr[0])
    mine = jnp.where(col == 0, corr[0], corr[1])
    theirs = lax.ppermute(dot(kernel, other), "col", [(c, cols - 1 - c) for c in range(cols)])
    own_res = lax.dynamic_slice_in_dim(residual, col * rhs, rhs, 1)
    return own_res - (dot(kernel, mine) + theirs)


def solution(mesh):
    return jax.shard_map(
        on_device,
        mesh=mesh,
        in_specs=(
            P("groups", "col", None, "row"),
            P(("groups", "row"), None),
            P(("groups", "row"), None),
            P(("groups", "row")),
        ),
        out_specs=P(("groups", "row"), "col"),
        check_vma=False,
    )
```

time: 195 us -> 139 us (0.71)
  waiting for transfers between devices: 142 us -> 56.6 us
  starting transfers between devices: 0.09 us -> 34.6 us
  between operations: 13.2 us -> 2.44 us
  matrix products: 30.6 us -> 20.6 us
  local copies, waits for them, and re-layouts: 4.21 us -> 12.8 us
  other arithmetic: 3.74 us -> 11.3 us
    all_gather x1 -> x0, waiting for transfers between devices: 68.3 us -> none  [on_device(): lax.all_gather(block_x, 'row', axis=0, tiled=True)]
    psum x1 -> x0, waiting for transfers between devices: 62.1 us -> none  [on_device(): corr_whole = lax.psum(partial_value, 'row')]
    ppermute x0 -> x26, waiting for transfers between devices: none -> 56.6 us  [the longest x6 27.4 us: reduce_all(): lax.ppermute(jnp.concatenate([live[k] for k in have], 0), 'row', pairs_of...]
    ppermute x0 -> x26, starting transfers between devices: none -> 34.6 us  [the longest x7 12.4 us: across(): return lax.ppermute(x, 'row', pairs)]
    reduce_scatter x1 -> x0, waiting for transfers between devices: 11 us -> none  [on_device(): summed = lax.psum_scatter(change, 'col', scatter_dimension=1, tiled=True)]
    dot_general x3 -> x7, matrix products: 30.6 us -> 20.6 us  [dot(): lax.dot_general(a, b, dims, precision=HIGH, preferred_element_type=jnp.fl...]
    select_n x2 -> x3, other arithmetic: 0.9 us -> 8.74 us  [the longest x2 8.67 us: pick(): out = jnp.where(mask, here, out)]
    dynamic_slice x0 -> x8, local copies, waits for them, and re-layouts: none -> 4.98 us  [the longest x4 3.05 us: pick(): mask = jnp.asarray(column == off)[z]]
  transfers between devices with their start and end apart: 3 -> 26, of which waited for: 3 -> 10; matrix products, arithmetic and copies ran while one was open for 11% -> 15% of each run, Pallas kernels for 0% -> 0%
where the time goes in v1:
time: 139 us; the launch traced here: 138 us
  waiting for transfers between devices  56.6 us (41%)
  starting transfers between devices  34.6 us (25%)
  matrix products  20.6 us (15%)
  local copies, waits for them, and re-layouts  12.8 us (9%)
  other arithmetic  11.3 us (8%)
  between operations  2.44 us (2%)
    ppermute x6, waiting for transfers between devices, reduce_all(): lax.ppermute(jnp.concatenate([live[k] for k in have], 0), 'row', pairs_of...  27.4 us
    dot_general x7, matrix products, dot(): lax.dot_general(a, b, dims, precision=HIGH, preferred_element_type=jnp.fl...  20.6 us
    ppermute x6, waiting for transfers between devices, reduce_all(): lax.ppermute(jnp.concatenate([live[k] for k in send], 0), 'row', pairs_of...  15.3 us
    ppermute x7, starting transfers between devices, across(): return lax.ppermute(x, 'row', pairs)  12.4 us
    ppermute x6, starting transfers between devices, shift(): return lax.ppermute(x, 'row', pairs)  8.86 us
    select_n x2, other arithmetic, pick(): out = jnp.where(mask, here, out)  8.67 us
    ppermute x7, waiting for transfers between devices, across(): return lax.ppermute(x, 'row', pairs)  7.73 us
    ppermute x6, starting transfers between devices, reduce_all(): lax.ppermute(jnp.concatenate([live[k] for k in have], 0), 'row', pairs_of...  6.24 us
  transfers between devices with their start and end apart: 26, of which 10 were waited for; matrix products, arithmetic and copies ran while one was open for 15% of the time, Pallas kernels for 0%

profile of v1, /device:TPU:25, one launch (start us, length us, event | category | flops | bytes accessed | tf_op | source)
XLA Modules:
  0.0 138.4 jit_solution(5988152468576482206)
XLA Ops:
  0.8 2.2 %gather_fusion.1 = f32[256,256]{1,0:T(8,128)S(1)} fusion(f32[1024,256]{1,0:T(8,128)} %param.22, s32[1024]{0:T(1024)S(1)} %get-tuple-element.32), kind=kCustom, calls=%fused_computation.1 | custom fusion | bytes 525312 | tf_op jit(solution)/shard_map/jit(_take)/gather | solution.py:85
  5.4 7.0 %collective-permute-done.13 = f32[512,128]{1,0:T(8,128)S(1)} collective-permute-done((f32[512,128]{1,0:T(8,128)S(1)}, f32[512,128]{1,0:T(8,128)S(1)}, u32[]{:S(2)}, u32[]{:S(2)}) %collective-permute-start.13) | collective-permute-done | bytes 262176 | tf_op jit(solution)/shard_map/ppermute | solution.py:61
  12.6 8.3 %collective-permute-done.14 = f32[256,128]{1,0:T(8,128)S(1)} collective-permute-done((f32[256,128]{1,0:T(8,128)S(1)}, f32[256,128]{1,0:T(8,128)S(1)}, u32[]{:S(2)}, u32[]{:S(2)}) %collective-permute-start.14) | collective-permute-done | bytes 131104 | tf_op jit(solution)/shard_map/ppermute | solution.py:61
  20.9 1.3 collective-permute-start.15
  22.3 3.2 %gather_fusion = f32[128,1024]{1,0:T(8,128)S(1)} fusion(f32[1024,1024]{1,0:T(8,128)} %param.21, s32[1024]{0:T(1024)S(1)} %pad_clamp_fusion.3), kind=kCustom, calls=%fused_computation | custom fusion | bytes 1049088 | tf_op jit(solution)/shard_map/jit(_take)/gather | solution.py:84
  25.5 2.1 %collective-permute-start.1 = (f32[128,1024]{1,0:T(8,128)S(1)}, f32[128,1024]{1,0:T(8,128)}, u32[]{:S(2)}, u32[]{:S(2)}) collective-permute-start(f32[128,1024]{1,0:T(8,128)S(1)} %gather_fusion), channel_id=1, source_target_pairs={{4,0},{6,2},{8,4},{10,6},{12,8},{14,10},{5,1},{7,3},{9,5},{11,7},{... | collective-permute-start | bytes 1572872 | tf_op jit(solution)/shard_map/ppermute | solution.py:17
  39.4 7.3 %collective-permute-done.16 = f32[128,128]{1,0:T(8,128)S(1)} collective-permute-done((f32[128,128]{1,0:T(8,128)S(1)}, f32[128,128]{1,0:T(8,128)S(1)}, u32[]{:S(2)}, u32[]{:S(2)}) %collective-permute-start.16) | collective-permute-done | bytes 65568 | tf_op jit(solution)/shard_map/ppermute | solution.py:66
  47.1 1.5 %collective-permute-start.5 = (f32[128,1024]{1,0:T(8,128)}, f32[128,1024]{1,0:T(8,128)}, u32[]{:S(2)}, u32[]{:S(2)}) collective-permute-start(f32[128,1024]{1,0:T(8,128)} %collective-permute-done.1), channel_id=1, source_target_pairs={{4,0},{6,2},{8,4},{10,6},{5,1},{7,3},{9,5},{11,7},{20,16},{22,18},... | collective-permute-start | bytes 1572872 | tf_op jit(solution)/shard_map/ppermute | solution.py:17
  48.6 6.4 %collective-permute-done.17 = f32[256,128]{1,0:T(8,128)S(1)} collective-permute-done((f32[256,128]{1,0:T(8,128)S(1)}, f32[256,128]{1,0:T(8,128)S(1)}, u32[]{:S(2)}, u32[]{:S(2)}) %collective-permute-start.17) | collective-permute-done | bytes 131104 | tf_op jit(solution)/shard_map/ppermute | solution.py:66
  55.0 1.5 %collective-permute-start.3 = (f32[128,1024]{1,0:T(8,128)}, f32[128,1024]{1,0:T(8,128)}, u32[]{:S(2)}, u32[]{:S(2)}) collective-permute-start(f32[128,1024]{1,0:T(8,128)} %collective-permute-done.1), channel_id=1, source_target_pairs={{0,2},{2,0},{4,6},{6,4},{8,10},{10,8},{1,3},{3,1},{5,7},{7,5},{9,1... | collective-permute-start | bytes 1572872 | tf_op jit(solution)/shard_map/ppermute | solution.py:21
  56.7 5.3 %fusion.13 = f32[1024,256]{0,1:T(8,128)} fusion(f32[1024,1024]{1,0:T(8,128)} %param.21, f32[128,1024]{1,0:T(8,128)} %collective-permute-done, f32[128,1024]{1,0:T(8,128)S(1)} %gather_fusion), kind=kOutput, calls=%fused_computation.24 | convolution fusion | flops 1611661312 | bytes 6291456 | tf_op jit(solution)/shard_map/dot_general | solution.py:11
  61.9 1.3 collective-permute-start.6
  63.2 2.9 %collective-permute-start.4 = (f32[128,1024]{1,0:T(8,128)}, f32[128,1024]{1,0:T(8,128)}, u32[]{:S(2)}, u32[]{:S(2)}) collective-permute-start(f32[128,1024]{1,0:T(8,128)} %collective-permute-done.2), channel_id=1, source_target_pairs={{4,6},{6,4},{8,10},{10,8},{12,14},{14,12},{5,7},{7,5},{9,11},{11,9... | collective-permute-start | bytes 1572872 | tf_op jit(solution)/shard_map/ppermute | solution.py:21
  66.2 4.4 %collective-permute-start.22 = (f32[128,128]{1,0:T(8,128)S(1)}, f32[128,128]{1,0:T(8,128)S(1)}, u32[]{:S(2)}, u32[]{:S(2)}) collective-permute-start(f32[128,128]{1,0:T(8,128)S(1)} %get-tuple-element.8), channel_id=1, source_target_pairs={{0,8},{2,10},{4,12},{6,14},{8,0},{10,2},{12,4},{14,6},{1,9},{3,11}... | collective-permute-start | bytes 196616 | tf_op jit(solution)/shard_map/ppermute | solution.py:66
  70.6 7.9 %collective-permute-done.22 = f32[128,128]{1,0:T(8,128)S(1)} collective-permute-done((f32[128,128]{1,0:T(8,128)S(1)}, f32[128,128]{1,0:T(8,128)S(1)}, u32[]{:S(2)}, u32[]{:S(2)}) %collective-permute-start.22) | collective-permute-done | bytes 65568 | tf_op jit(solution)/shard_map/ppermute | solution.py:66
  78.7 4.4 %collective-permute-done.23 = f32[256,128]{1,0:T(8,128)S(1)} collective-permute-done((f32[256,128]{1,0:T(8,128)S(1)}, f32[256,128]{1,0:T(8,128)S(1)}, u32[]{:S(2)}, u32[]{:S(2)}) %collective-permute-start.23) | collective-permute-done | bytes 131104 | tf_op jit(solution)/shard_map/ppermute | solution.py:66
  84.8 1.5 %collective-permute-start.9 = (f32[128,1024]{1,0:T(8,128)}, f32[128,1024]{1,0:T(8,128)}, u32[]{:S(2)}, u32[]{:S(2)}) collective-permute-start(f32[128,1024]{1,0:T(8,128)} %collective-permute-done.5), channel_id=1, source_target_pairs={{4,0},{6,2},{5,1},{7,3},{20,16},{22,18},{21,17},{23,19}} | collective-permute-start | bytes 1572872 | tf_op jit(solution)/shard_map/ppermute | solution.py:17
  87.0 1.4 %collective-permute-done.24 = f32[512,128]{1,0:T(8,128)S(1)} collective-permute-done((f32[512,128]{1,0:T(8,128)S(1)}, f32[512,128]{1,0:T(8,128)S(1)}, u32[]{:S(2)}, u32[]{:S(2)}) %collective-permute-start.24) | collective-permute-done | bytes 262176 | tf_op jit(solution)/shard_map/ppermute | solution.py:66
  88.4 1.3 collective-permute-start.10
  90.4 2.9 %collective-permute-start.8 = (f32[128,1024]{1,0:T(8,128)}, f32[128,1024]{1,0:T(8,128)S(1)}, u32[]{:S(2)}, u32[]{:S(2)}) collective-permute-start(f32[128,1024]{1,0:T(8,128)} %collective-permute-done.6), channel_id=1, source_target_pairs={{8,10},{10,8},{12,14},{14,12},{9,11},{11,9},{13,15},{15,13},{24,26... | collective-permute-start | bytes 1572872 | tf_op jit(solution)/shard_map/ppermute | solution.py:21
  94.0 4.6 %collective-permute-done.10 = f32[128,1024]{1,0:T(8,128)} collective-permute-done((f32[128,1024]{1,0:T(8,128)}, f32[128,1024]{1,0:T(8,128)}, u32[]{:S(2)}, u32[]{:S(2)}) %collective-permute-start.10) | collective-permute-done | bytes 524320 | tf_op jit(solution)/shard_map/ppermute | solution.py:17
  98.6 3.1 %collective-permute-start.12 = (f32[128,1024]{1,0:T(8,128)}, f32[128,1024]{1,0:T(8,128)S(1)}, u32[]{:S(2)}, u32[]{:S(2)}) collective-permute-start(f32[128,1024]{1,0:T(8,128)} %collective-permute-done.10), channel_id=1, source_target_pairs={{12,14},{14,12},{13,15},{15,13},{28,30},{30,28},{29,31},{31,29}} | collective-permute-start | bytes 1572872 | tf_op jit(solution)/shard_map/ppermute | solution.py:21
  101.8 4.7 %select_select_fusion.3 = (f32[128,1024]{1,0:T(8,128)S(1)}, f32[128,1024]{1,0:T(8,128)S(1)}, f32[128,1024]{1,0:T(8,128)S(1)}) fusion(f32[128,1024]{1,0:T(8,128)} %collective-permute-done.5, f32[128,1024]{1,0:T(8,128)} %collective-permute-done.1, f32[128,1024]{1,0:T(8,128)} %collective-permute-done.6, pred[]{:T(512)} %bitcast.3, pred[]{:T(512)} %bitcast.1, ...), kind=kLoop, calls=%fused_computation.42 | loop fusion | flops 786432 | bytes 4718596 | tf_op jit(solution)/shard_map/jit(_where)/select_n | solution.py:51
  106.6 7.7 %collective-permute-done.12 = f32[128,1024]{1,0:T(8,128)S(1)} collective-permute-done((f32[128,1024]{1,0:T(8,128)}, f32[128,1024]{1,0:T(8,128)S(1)}, u32[]{:S(2)}, u32[]{:S(2)}) %collective-permute-start.12) | collective-permute-done | bytes 524320 | tf_op jit(solution)/shard_map/ppermute | solution.py:21
  114.3 4.0 %select_select_fusion.2 = (f32[128,1024]{1,0:T(8,128)S(1)}, f32[128,1024]{1,0:T(8,128)S(1)}, f32[128,1024]{1,0:T(8,128)S(1)}) fusion(f32[128,1024]{1,0:T(8,128)S(1)} %collective-permute-done.7, f32[128,1024]{1,0:T(8,128)} %collective-permute-done.3, f32[128,1024]{1,0:T(8,128)S(1)} %collective-permute-done.8, pred[]{:T(512)} %bitcast.3, pred[]{:T(512)} %bitcast.1, ...), kind=kLoop, calls=%fused_computation.41 | loop fusion | flops 786432 | bytes 4718596 | tf_op jit(solution)/shard_map/jit(_where)/select_n | solution.py:51
  118.3 2.2 %fusion.7 = f32[1024,256]{0,1:T(8,128)S(1)} fusion(f32[1024,1024]{1,0:T(8,128)S(1)} %copy-done.1, f32[128,1024]{1,0:T(8,128)S(1)} %get-tuple-element.17, f32[128,1024]{1,0:T(8,128)S(1)} %get-tuple-element.15), kind=kOutput, calls=%fused_computation.16 | convolution fusion | flops 1611661312 | bytes 6291456 | tf_op jit(solution)/shard_map/dot_general | solution.py:11
  120.4 2.2 %fusion.4 = f32[1024,256]{0,1:T(8,128)S(1)} fusion(f32[1024,1024]{1,0:T(8,128)S(1)} %copy-done.1, f32[128,1024]{1,0:T(8,128)S(1)} %get-tuple-element.18, f32[128,1024]{1,0:T(8,128)S(1)} %get-tuple-element.16), kind=kOutput, calls=%fused_computation.12 | convolution fusion | flops 1611661312 | bytes 6291456 | tf_op jit(solution)/shard_map/dot_general | solution.py:11
  122.6 2.2 %fusion.10 = f32[1024,256]{0,1:T(8,128)S(1)} fusion(f32[1024,1024]{1,0:T(8,128)S(1)} %copy-done.1, f32[128,1024]{1,0:T(8,128)S(1)} %get-tuple-element.28, f32[128,1024]{1,0:T(8,128)S(1)} %get-tuple-element.27), kind=kOutput, calls=%fused_computation.20 | convolution fusion | flops 1611661312 | bytes 6291456 | tf_op jit(solution)/shard_map/dot_general | solution.py:11
  124.8 3.5 %fusion = f32[1024,128]{1,0:T(8,128)S(1)} fusion(f32[1024,128]{1,0:T(8,128)S(1)} %bitcast.146, f32[1024,256]{0,1:T(8,128)S(1)} %fusion.4, f32[1024,256]{0,1:T(8,128)S(1)} %fusion.7, f32[1024,256]{0,1:T(8,128)S(1)} %fusion.10, f32[1024,256]{0,1:T(8,128)S(1)} %copy-done.3), kind=kOutput, calls=%fused_computation.6 | convolution fusion | flops 808452096 | bytes 5242880 | tf_op jit(solution)/shard_map/dot_general | solution.py:11
  128.3 4.2 %collective-permute-start.25 = (f32[1024,128]{1,0:T(8,128)S(1)}, f32[1024,128]{1,0:T(8,128)S(1)}, u32[]{:S(2)}, u32[]{:S(2)}) collective-permute-start(f32[1024,128]{1,0:T(8,128)S(1)} %fusion), channel_id=1, source_target_pairs={{0,1},{1,0},{2,3},{3,2},{4,5},{5,4},{6,7},{7,6},{8,9},{9,8},{10,11... | collective-permute-start | bytes 1572872 | tf_op jit(solution)/shard_map/ppermute | solution.py:120
  132.5 1.5 %collective-permute-done.25 = f32[1024,128]{1,0:T(8,128)S(1)} collective-permute-done((f32[1024,128]{1,0:T(8,128)S(1)}, f32[1024,128]{1,0:T(8,128)S(1)}, u32[]{:S(2)}, u32[]{:S(2)}) %collective-permute-start.25) | collective-permute-done | bytes 524320 | tf_op jit(solution)/shard_map/ppermute | solution.py:120
  134.1 4.3 %fusion.15 = f32[1024,128]{1,0:T(8,128)} fusion(f32[1024,128]{1,0:T(8,128)S(1)} %collective-permute-done.25, f32[1024,128]{1,0:T(8,128)S(1)} %bitcast.145, f32[1024,256]{0,1:T(8,128)S(1)} %fusion.4, f32[1024,256]{0,1:T(8,128)S(1)} %fusion.7, f32[1024,256]{0,1:T(8,128)S(1)} %fusion.10, f32[1024,256]{0,1:T(8,128)S(1)} %copy-done.3, ...), kind=kOutput, calls=%fused_computation.26 | convolution fusion | flops 808714240 | bytes 6291460 | tf_op jit(solution)/shard_map/dot_general | solution.py:11
  (103 shorter events, 17.8 us)
Async XLA Ops:
  4.4 25.1 %copy-start.10 = (s32[4]{0:T(128)S(1)}, s32[4]{0:T(128)}, u32[]{:S(2)}) copy-start(s32[4]{0:T(128)} %constant.73.clone) | copy-start | bytes 52
  4.4 26.2 %copy-start.9 = (s32[4]{0:T(128)S(1)}, s32[4]{0:T(128)}, u32[]{:S(2)}) copy-start(s32[4]{0:T(128)} %constant.70.clone) | copy-start | bytes 52
  4.4 27.5 %copy-start.8 = (s32[4]{0:T(128)S(1)}, s32[4]{0:T(128)}, u32[]{:S(2)}) copy-start(s32[4]{0:T(128)} %constant.68.clone) | copy-start | bytes 52
  5.0 32.0 %copy-start.7 = (pred[4]{0:T(512)(128)(4,1)S(1)}, pred[4]{0:T(512)(128)(4,1)}, u32[]{:S(2)}) copy-start(pred[4]{0:T(512)(128)(4,1)} %constant.71.clone) | copy-start | bytes 16
  5.1 32.6 %copy-start.6 = (pred[4]{0:T(512)(128)(4,1)S(1)}, pred[4]{0:T(512)(128)(4,1)}, u32[]{:S(2)}) copy-start(pred[4]{0:T(512)(128)(4,1)} %constant.69.clone) | copy-start | bytes 16
  5.1 33.2 %copy-start.5 = (pred[4]{0:T(512)(128)(4,1)S(1)}, pred[4]{0:T(512)(128)(4,1)}, u32[]{:S(2)}) copy-start(pred[4]{0:T(512)(128)(4,1)} %constant.67.clone) | copy-start | bytes 16
  5.1 7.3 %collective-permute-start.13 = (f32[512,128]{1,0:T(8,128)S(1)}, f32[512,128]{1,0:T(8,128)S(1)}, u32[]{:S(2)}, u32[]{:S(2)}) collective-permute-start(f32[512,128]{1,0:T(8,128)S(1)} %pad_maximum_fusion.7), channel_id=1, source_target_pairs={{0,4},{2,6},{4,0},{6,2},{8,12},{10,14},{12,8},{14,10},{1,5},{3,7},... | collective-permute-start | bytes 786440 | tf_op jit(solution)/shard_map/ppermute | solution.py:61
  12.4 8.5 %collective-permute-start.14 = (f32[256,128]{1,0:T(8,128)S(1)}, f32[256,128]{1,0:T(8,128)S(1)}, u32[]{:S(2)}, u32[]{:S(2)}) collective-permute-start(f32[256,128]{1,0:T(8,128)S(1)} %pad_maximum_fusion.11), channel_id=1, source_target_pairs={{0,8},{2,10},{4,12},{6,14},{8,0},{10,2},{12,4},{14,6},{1,9},{3,11}... | collective-permute-start | bytes 393224 | tf_op jit(solution)/shard_map/ppermute | solution.py:61
  20.9 12.3 %collective-permute-start.15 = (f32[128,128]{1,0:T(8,128)S(1)}, f32[128,128]{1,0:T(8,128)S(1)}, u32[]{:S(2)}, u32[]{:S(2)}) collective-permute-start(f32[128,128]{1,0:T(8,128)S(1)} %slice_add_fusion.6), channel_id=1, source_target_pairs={{0,2},{2,0},{4,6},{6,4},{8,10},{10,8},{12,14},{14,12},{1,3},{3,1},... | collective-permute-start | bytes 196616 | tf_op jit(solution)/shard_map/ppermute | solution.py:61
  25.5 21.6 %collective-permute-start.1 = (f32[128,1024]{1,0:T(8,128)S(1)}, f32[128,1024]{1,0:T(8,128)}, u32[]{:S(2)}, u32[]{:S(2)}) collective-permute-start(f32[128,1024]{1,0:T(8,128)S(1)} %gather_fusion), channel_id=1, source_target_pairs={{4,0},{6,2},{8,4},{10,6},{12,8},{14,10},{5,1},{7,3},{9,5},{11,7},{... | collective-permute-start | bytes 1572872 | tf_op jit(solution)/shard_map/ppermute | solution.py:17
  27.6 29.0 %collective-permute-start = (f32[128,1024]{1,0:T(8,128)S(1)}, f32[128,1024]{1,0:T(8,128)}, u32[]{:S(2)}, u32[]{:S(2)}) collective-permute-start(f32[128,1024]{1,0:T(8,128)S(1)} %gather_fusion), channel_id=1, source_target_pairs={{0,2},{2,0},{4,6},{6,4},{8,10},{10,8},{12,14},{14,12},{1,3},{3,1},... | collective-permute-start | bytes 1572872 | tf_op jit(solution)/shard_map/ppermute | solution.py:21
  28.2 33.8 %collective-permute-start.2 = (f32[128,1024]{1,0:T(8,128)S(1)}, f32[128,1024]{1,0:T(8,128)}, u32[]{:S(2)}, u32[]{:S(2)}) collective-permute-start(f32[128,1024]{1,0:T(8,128)S(1)} %gather_fusion), channel_id=1, source_target_pairs={{0,4},{2,6},{4,8},{6,10},{8,12},{10,14},{1,5},{3,7},{5,9},{7,11},{... | collective-permute-start | bytes 1572872 | tf_op jit(solution)/shard_map/ppermute | solution.py:17
  34.9 11.9 %collective-permute-start.19 = (f32[512,128]{1,0:T(8,128)}, f32[512,128]{1,0:T(8,128)S(1)}, u32[]{:S(2)}, u32[]{:S(2)}) collective-permute-start(f32[512,128]{1,0:T(8,128)} %pad_maximum_fusion.9), channel_id=1, source_target_pairs={{0,2},{2,0},{4,6},{6,4},{8,10},{10,8},{12,14},{14,12},{1,3},{3,1},... | collective-permute-start | bytes 786440 | tf_op jit(solution)/shard_map/ppermute | solution.py:61
  38.9 7.9 %collective-permute-start.16 = (f32[128,128]{1,0:T(8,128)S(1)}, f32[128,128]{1,0:T(8,128)S(1)}, u32[]{:S(2)}, u32[]{:S(2)}) collective-permute-start(f32[128,128]{1,0:T(8,128)S(1)} %get-tuple-element.6), channel_id=1, source_target_pairs={{0,2},{2,0},{4,6},{6,4},{8,10},{10,8},{12,14},{14,12},{1,3},{3,1},... | collective-permute-start | bytes 196616 | tf_op jit(solution)/shard_map/ppermute | solution.py:66
  46.8 8.2 %collective-permute-start.17 = (f32[256,128]{1,0:T(8,128)S(1)}, f32[256,128]{1,0:T(8,128)S(1)}, u32[]{:S(2)}, u32[]{:S(2)}) collective-permute-start(f32[256,128]{1,0:T(8,128)S(1)} %pad_maximum_fusion.12), channel_id=1, source_target_pairs={{0,8},{2,10},{4,12},{6,14},{8,0},{10,2},{12,4},{14,6},{1,9},{3,11}... | collective-permute-start | bytes 393224 | tf_op jit(solution)/shard_map/ppermute | solution.py:66
  46.9 9.6 %collective-permute-start.20 = (f32[256,128]{1,0:T(8,128)S(1)}, f32[256,128]{1,0:T(8,128)S(1)}, u32[]{:S(2)}, u32[]{:S(2)}) collective-permute-start(f32[256,128]{1,0:T(8,128)S(1)} %pad_maximum_fusion.13), channel_id=1, source_target_pairs={{0,4},{2,6},{4,0},{6,2},{8,12},{10,14},{12,8},{14,10},{1,5},{3,7},... | collective-permute-start | bytes 393224 | tf_op jit(solution)/shard_map/ppermute | solution.py:61
  47.1 37.7 %collective-permute-start.5 = (f32[128,1024]{1,0:T(8,128)}, f32[128,1024]{1,0:T(8,128)}, u32[]{:S(2)}, u32[]{:S(2)}) collective-permute-start(f32[128,1024]{1,0:T(8,128)} %collective-permute-done.1), channel_id=1, source_target_pairs={{4,0},{6,2},{8,4},{10,6},{5,1},{7,3},{9,5},{11,7},{20,16},{22,18},... | collective-permute-start | bytes 1572872 | tf_op jit(solution)/shard_map/ppermute | solution.py:17
  55.0 35.4 %collective-permute-start.3 = (f32[128,1024]{1,0:T(8,128)}, f32[128,1024]{1,0:T(8,128)}, u32[]{:S(2)}, u32[]{:S(2)}) collective-permute-start(f32[128,1024]{1,0:T(8,128)} %collective-permute-done.1), channel_id=1, source_target_pairs={{0,2},{2,0},{4,6},{6,4},{8,10},{10,8},{1,3},{3,1},{5,7},{7,5},{9,1... | collective-permute-start | bytes 1572872 | tf_op jit(solution)/shard_map/ppermute | solution.py:21
  56.5 9.7 %collective-permute-start.18 = (f32[512,128]{1,0:T(8,128)S(1)}, f32[512,128]{1,0:T(8,128)S(1)}, u32[]{:S(2)}, u32[]{:S(2)}) collective-permute-start(f32[512,128]{1,0:T(8,128)S(1)} %pad_maximum_fusion.8), channel_id=1, source_target_pairs={{0,4},{2,6},{4,0},{6,2},{8,12},{10,14},{12,8},{14,10},{1,5},{3,7},... | collective-permute-start | bytes 786440 | tf_op jit(solution)/shard_map/ppermute | solution.py:66
  56.6 6.7 %collective-permute-start.21 = (f32[128,128]{1,0:T(8,128)S(1)}, f32[128,128]{1,0:T(8,128)S(1)}, u32[]{:S(2)}, u32[]{:S(2)}) collective-permute-start(f32[128,128]{1,0:T(8,128)S(1)} %slice_add_fusion), channel_id=1, source_target_pairs={{0,8},{2,10},{4,12},{6,14},{8,0},{10,2},{12,4},{14,6},{1,9},{3,11}... | collective-permute-start | bytes 196616 | tf_op jit(solution)/shard_map/ppermute | solution.py:61
  61.9 24.3 %collective-permute-start.6 = (f32[128,1024]{1,0:T(8,128)}, f32[128,1024]{1,0:T(8,128)}, u32[]{:S(2)}, u32[]{:S(2)}) collective-permute-start(f32[128,1024]{1,0:T(8,128)} %collective-permute-done.2), channel_id=1, source_target_pairs={{4,8},{6,10},{8,12},{10,14},{5,9},{7,11},{9,13},{11,15},{20,24},{2... | collective-permute-start | bytes 1572872 | tf_op jit(solution)/shard_map/ppermute | solution.py:17
  63.2 43.3 %collective-permute-start.4 = (f32[128,1024]{1,0:T(8,128)}, f32[128,1024]{1,0:T(8,128)}, u32[]{:S(2)}, u32[]{:S(2)}) collective-permute-start(f32[128,1024]{1,0:T(8,128)} %collective-permute-done.2), channel_id=1, source_target_pairs={{4,6},{6,4},{8,10},{10,8},{12,14},{14,12},{5,7},{7,5},{9,11},{11,9... | collective-permute-start | bytes 1572872 | tf_op jit(solution)/shard_map/ppermute | solution.py:21
  66.2 12.4 %collective-permute-start.22 = (f32[128,128]{1,0:T(8,128)S(1)}, f32[128,128]{1,0:T(8,128)S(1)}, u32[]{:S(2)}, u32[]{:S(2)}) collective-permute-start(f32[128,128]{1,0:T(8,128)S(1)} %get-tuple-element.8), channel_id=1, source_target_pairs={{0,8},{2,10},{4,12},{6,14},{8,0},{10,2},{12,4},{14,6},{1,9},{3,11}... | collective-permute-start | bytes 196616 | tf_op jit(solution)/shard_map/ppermute | solution.py:66
  78.6 4.5 %collective-permute-start.23 = (f32[256,128]{1,0:T(8,128)S(1)}, f32[256,128]{1,0:T(8,128)S(1)}, u32[]{:S(2)}, u32[]{:S(2)}) collective-permute-start(f32[256,128]{1,0:T(8,128)S(1)} %pad_maximum_fusion.14), channel_id=1, source_target_pairs={{0,4},{2,6},{4,0},{6,2},{8,12},{10,14},{12,8},{14,10},{1,5},{3,7},... | collective-permute-start | bytes 393224 | tf_op jit(solution)/shard_map/ppermute | solution.py:66
  83.1 5.3 %collective-permute-start.24 = (f32[512,128]{1,0:T(8,128)S(1)}, f32[512,128]{1,0:T(8,128)S(1)}, u32[]{:S(2)}, u32[]{:S(2)}) collective-permute-start(f32[512,128]{1,0:T(8,128)S(1)} %pad_maximum_fusion.10), channel_id=1, source_target_pairs={{0,2},{2,0},{4,6},{6,4},{8,10},{10,8},{12,14},{14,12},{1,3},{3,1},... | collective-permute-start | bytes 786440 | tf_op jit(solution)/shard_map/ppermute | solution.py:66
  84.8 8.5 %collective-permute-start.9 = (f32[128,1024]{1,0:T(8,128)}, f32[128,1024]{1,0:T(8,128)}, u32[]{:S(2)}, u32[]{:S(2)}) collective-permute-start(f32[128,1024]{1,0:T(8,128)} %collective-permute-done.5), channel_id=1, source_target_pairs={{4,0},{6,2},{5,1},{7,3},{20,16},{22,18},{21,17},{23,19}} | collective-permute-start | bytes 1572872 | tf_op jit(solution)/shard_map/ppermute | solution.py:17
  86.3 20.3 %collective-permute-start.7 = (f32[128,1024]{1,0:T(8,128)}, f32[128,1024]{1,0:T(8,128)S(1)}, u32[]{:S(2)}, u32[]{:S(2)}) collective-permute-start(f32[128,1024]{1,0:T(8,128)} %collective-permute-done.5), channel_id=1, source_target_pairs={{0,2},{2,0},{4,6},{6,4},{1,3},{3,1},{5,7},{7,5},{16,18},{18,16},{2... | collective-permute-start | bytes 1572872 | tf_op jit(solution)/shard_map/ppermute | solution.py:21
  88.4 10.2 %collective-permute-start.10 = (f32[128,1024]{1,0:T(8,128)}, f32[128,1024]{1,0:T(8,128)}, u32[]{:S(2)}, u32[]{:S(2)}) collective-permute-start(f32[128,1024]{1,0:T(8,128)} %collective-permute-done.6), channel_id=1, source_target_pairs={{8,12},{10,14},{9,13},{11,15},{24,28},{26,30},{25,29},{27,31}} | collective-permute-start | bytes 1572872 | tf_op jit(solution)/shard_map/ppermute | solution.py:17
  90.4 16.2 %collective-permute-start.8 = (f32[128,1024]{1,0:T(8,128)}, f32[128,1024]{1,0:T(8,128)S(1)}, u32[]{:S(2)}, u32[]{:S(2)}) collective-permute-start(f32[128,1024]{1,0:T(8,128)} %collective-permute-done.6), channel_id=1, source_target_pairs={{8,10},{10,8},{12,14},{14,12},{9,11},{11,9},{13,15},{15,13},{24,26... | collective-permute-start | bytes 1572872 | tf_op jit(solution)/shard_map/ppermute | solution.py:21
  93.3 13.2 %collective-permute-start.11 = (f32[128,1024]{1,0:T(8,128)}, f32[128,1024]{1,0:T(8,128)S(1)}, u32[]{:S(2)}, u32[]{:S(2)}) collective-permute-start(f32[128,1024]{1,0:T(8,128)} %collective-permute-done.9), channel_id=1, source_target_pairs={{0,2},{2,0},{1,3},{3,1},{16,18},{18,16},{17,19},{19,17}} | collective-permute-start | bytes 1572872 | tf_op jit(solution)/shard_map/ppermute | solution.py:21
  98.6 15.7 %collective-permute-start.12 = (f32[128,1024]{1,0:T(8,128)}, f32[128,1024]{1,0:T(8,128)S(1)}, u32[]{:S(2)}, u32[]{:S(2)}) collective-permute-start(f32[128,1024]{1,0:T(8,128)} %collective-permute-done.10), channel_id=1, source_target_pairs={{12,14},{14,12},{13,15},{15,13},{28,30},{30,28},{29,31},{31,29}} | collective-permute-start | bytes 1572872 | tf_op jit(solution)/shard_map/ppermute | solution.py:21
  128.3 5.8 %collective-permute-start.25 = (f32[1024,128]{1,0:T(8,128)S(1)}, f32[1024,128]{1,0:T(8,128)S(1)}, u32[]{:S(2)}, u32[]{:S(2)}) collective-permute-start(f32[1024,128]{1,0:T(8,128)S(1)} %fusion), channel_id=1, source_target_pairs={{0,1},{1,0},{2,3},{3,2},{4,5},{5,4},{6,7},{7,6},{8,9},{9,8},{10,11... | collective-permute-start | bytes 1572872 | tf_op jit(solution)/shard_map/ppermute | solution.py:120
  (5 other events, 32.2 us)

commit v2 on v0

v2 whole, which is shorter than its diff:
```python
import jax
import jax.numpy as jnp
from jax import lax
from jax.experimental import pallas as pl
from jax.experimental.pallas import tpu as pltpu
from jax.sharding import PartitionSpec as P

F32, BF16 = jnp.float32, jnp.bfloat16
NT = (((1,), (1,)), ((), ()))
NN = (((1,), (0,)), ((), ()))
WIDTH = 2


def mm(a, b, dims):
    return lax.dot_general(a, b, dims, preferred_element_type=F32)


def halves(x):
    high = x.astype(BF16)
    return high, (x - high.astype(F32)).astype(BF16)


VMEM = pl.BlockSpec(memory_space=pltpu.VMEM)
PARAMS = pltpu.CompilerParams(vmem_limit_bytes=8 << 20)


def in_vmem(*arrays):
    return [pltpu.with_memory_space_constraint(a, pltpu.VMEM) for a in arrays]


def split_kernel(x_ref, high_ref, low_ref):
    high_ref[...], low_ref[...] = halves(x_ref[...])


def split(x, tile=256):
    rows, cols = x.shape
    return pl.pallas_call(
        split_kernel,
        grid=(rows // tile,),
        in_specs=[pl.BlockSpec((tile, cols), lambda i: (i, 0))],
        out_specs=[pl.BlockSpec((tile, cols), lambda i: (i, 0))] * 2,
        out_shape=[pltpu.VMEM(x.shape, BF16)] * 2,
        compiler_params=PARAMS,
        cost_estimate=pl.CostEstimate(flops=4 * rows * cols, bytes_accessed=8 * rows * cols, transcendentals=0),
    )(x)


def gram_kernel(scale, tile, xh_ref, xl_ref, near_ref, far_ref, kh_ref, kl_ref, ph_ref, pl_ref):
    half = near_ref.shape[0]
    ph_ref[:half], pl_ref[:half] = halves(near_ref[...])
    ph_ref[half:], pl_ref[half:] = halves(far_ref[...])
    for r in range(0, kh_ref.shape[0], tile):
        rows = slice(r, r + tile)
        xh, ph = xh_ref[rows], ph_ref[...]
        gram = mm(xh, pl_ref[...], NT) + mm(xl_ref[rows], ph, NT) + mm(xh, ph, NT)
        root = gram * scale + 0.5
        kh_ref[rows], kl_ref[rows] = halves(root * root)


def gram(x_high, x_low, near, far, tile=512):
    rows, feats = x_high.shape
    points = 2 * near.shape[0]
    return pl.pallas_call(
        lambda *refs: gram_kernel(1.0 / feats, tile, *refs),
        in_specs=[VMEM] * 4,
        out_specs=[VMEM] * 2,
        out_shape=[pltpu.VMEM((rows, points), BF16)] * 2,
        scratch_shapes=[pltpu.VMEM((points, feats), BF16)] * 2,
        compiler_params=PARAMS,
        cost_estimate=pl.CostEstimate(
            flops=6 * rows * feats * points, bytes_accessed=4 * rows * (feats + points), transcendentals=0
        ),
    )(*in_vmem(x_high, x_low), near, far)


def apply_kernel(slots, runs, tile, table_ref, *refs):
    highs, lows = refs[:slots], refs[slots:2 * slots]
    same_refs, cross_refs = refs[2 * slots:2 * slots + runs], refs[2 * slots + runs:2 * slots + 2 * runs]
    out_ref, c_ref = refs[2 * slots + 2 * runs:]
    each, half = same_refs[0].shape[:2]
    rhs = out_ref.shape[1]
    cols = pl.ds(pl.multiple_of(table_ref[slots] * rhs, rhs), rhs)
    for j in range(slots):
        place = table_ref[j]
        for i, run_refs in enumerate((same_refs, cross_refs)):
            rows = pl.ds((2 * j + i) * half, half)
            for r, ref in enumerate(run_refs):

                @pl.when((place >= r * each) & (place < (r + 1) * each))
                def _():
                    c_ref[rows, :rhs], c_ref[rows, rhs:] = halves(ref[place - r * each, :, cols])

    for r in range(0, out_ref.shape[0], tile):
        span = slice(r, r + tile)
        total = jnp.zeros((tile, rhs), F32)
        for j in range(slots):
            rows = pl.ds(2 * j * half, 2 * half)
            both = mm(highs[j][span], c_ref[rows, :], NN)
            total += both[:, :rhs] + (both[:, rhs:] + mm(lows[j][span], c_ref[rows, :rhs], NN))
        out_ref[span] = total


def apply(kerns, sames, crosses, table, parts, tile=512):
    slots, runs = len(kerns), len(sames)
    rows, points = kerns[0][0].shape
    rhs = sames[0].shape[2] // parts
    return pl.pallas_call(
        lambda *refs: apply_kernel(slots, runs, tile, *refs),
        in_specs=[pl.BlockSpec(memory_space=pltpu.SMEM)] + [VMEM] * (2 * slots + 2 * runs),
        out_specs=VMEM,
        scratch_shapes=[pltpu.VMEM((slots * points, 2 * rhs), BF16)],
        out_shape=jax.ShapeDtypeStruct((rows, rhs), F32),
        compiler_params=PARAMS,
        cost_estimate=pl.CostEstimate(
            flops=6 * rows * slots * points * rhs, bytes_accessed=4 * rows * slots * points, transcendentals=0
        ),
    )(table, *in_vmem(*[k[0] for k in kerns], *[k[1] for k in kerns]), *sames, *crosses)


def moves(depth):
    steps, held = [], {"own": {z: z for z in range(depth)}}

    def step(name, pairs, source):
        pairs = [(s, d) for s, d in pairs if s in held[source]]
        held[name] = {d: held[source][s] for s, d in pairs}
        steps.append((name, pairs, source))

    if depth == 4:
        inner, outer = [(1, 2), (2, 1)], [(1, 0), (2, 3)]
        step("a", [(0, 1), (1, 0), (2, 3), (3, 2)], "own")
        step("b", inner, "own")
        step("c", inner, "a")
        step("d", outer, "b")
        step("e", outer, "c")
    else:
        up = down = "own"
        for s in range(1, depth):
            step(f"u{s}", [(z, z + 1) for z in range(depth - 1)], up)
            step(f"d{s}", [(z, z - 1) for z in range(1, depth)], down)
            up, down = f"u{s}", f"d{s}"
    order = [name for name, _, _ in steps]
    slots = []
    for z in range(depth):
        slots.append([(name, held[name][z]) for name in order if z in held[name]])
    return steps, slots


def permute(x, pairs):
    return lax.ppermute(x, "row", pairs)


def along(pairs):
    return [(s * WIDTH + y, d * WIDTH + y) for s, d in pairs for y in range(WIDTH)]


def on_device(inverse, features, residual, block_ids):
    n = lax.axis_size("row")
    depth = n // WIDTH
    me, col = lax.axis_index("row"), lax.axis_index("col")
    cols = lax.axis_size("col")
    z, y = lax.shift_right_logical(me, 1), lax.bitwise_and(me, 1)
    across = [(r, r ^ 1) for r in range(n)]
    local_ids = block_ids - me * features.shape[0]
    half = block_ids.shape[0] // cols

    own_ids = lax.dynamic_slice_in_dim(local_ids, col * half, half)
    own = jnp.take(features, own_ids, axis=0, mode="clip")
    steps, slots = moves(depth)

    other = cols - 1 - col
    places, masks = [z], []
    for j in range(depth - 1):
        by_name, place = {}, jnp.int32(0)
        for zz in range(depth):
            by_name.setdefault(slots[zz][j][0], []).append(zz)
            place = jnp.where(z == zz, slots[zz][j][1], place)
        places.append(place)
        masks.append({name: any_of(z, zs) for name, zs in list(by_name.items())})
    ends = [(z == i) | (z == depth - 1 - i) for i in range(depth // 2 - 1)]
    tables = [jnp.stack(places + [c]).astype(jnp.int32) for c in (other, col)]
    own, local_ids, y, masks, ends, tables = lax.optimization_barrier((own, local_ids, y, masks, ends, tables))

    bufs = {"own": own}
    for name, pairs, source in steps:
        bufs[name] = permute(bufs[source], along(pairs))

    block_res = jnp.take(residual, local_ids, axis=0, mode="clip")
    partial = lax.dot_general(
        inverse.reshape(-1, inverse.shape[-1]), block_res, NN,
        precision=lax.Precision.HIGH, preferred_element_type=F32,
    ).reshape(depth, WIDTH, half, -1)
    keep = lax.dynamic_index_in_dim(partial, y, 1, keepdims=False)
    send = lax.dynamic_index_in_dim(partial, 1 - y, 1, keepdims=False)

    sames, crosses = [], []
    for h in range(2):
        run = slice(h * depth // 2, (h + 1) * depth // 2)
        term = keep[run] + permute(send[run], across)
        inward = [[(s, s + 1), (depth - 1 - s, depth - 2 - s)] for s in range(depth // 2 - 1)]
        for pairs in inward:
            term = term + permute(term, along(pairs))
        pairs = [(depth // 2 - 1, depth // 2), (depth // 2, depth // 2 - 1)]
        term = term + permute(term, along(pairs))
        for i, pairs in reversed(list(enumerate(inward))):
            back = permute(term, along([(d, s) for s, d in pairs]))
            term = jnp.where(ends[i], back, term)
        sames.append(term)
        crosses.append(permute(term, across))

    x_high, x_low = split(features)
    kerns = []
    for j in range(depth):
        block = own
        if j > 0:
            block = None
            for name, mask in masks[j - 1].items():
                block = bufs[name] if block is None else jnp.where(mask, bufs[name], block)
        far = permute(block, across)
        kerns.append(gram(x_high, x_low, block, far))

    theirs = apply(kerns, sames, crosses, tables[0], cols)
    got = lax.ppermute(theirs, "col", [(c, cols - 1 - c) for c in range(cols)])
    mine = apply(kerns, sames, crosses, tables[1], cols)
    rhs = mine.shape[1]
    return lax.dynamic_slice_in_dim(residual, col * rhs, rhs, 1) - (mine + got)


def any_of(z, places):
    mask = z == places[0]
    for p in places[1:]:
        mask = mask | (z == p)
    return mask


def solution(mesh):
    return jax.shard_map(
        on_device,
        mesh=mesh,
        in_specs=(
            P("groups", "col", None, "row"),
            P(("groups", "row"), None),
            P(("groups", "row"), None),
            P(("groups", "row")),
        ),
        out_specs=P(("groups", "row"), "col"),
        check_vma=False,
    )
```

time: 195 us -> 99 us (0.51)
  the two profiles are of different devices: /device:TPU:25 before, /device:TPU:9 now
where the time goes in v2:
time: 99 us; the launch traced here: 98.5 us
  waiting for transfers between devices  37.6 us (38%)
  starting transfers between devices  32.8 us (33%)
  Pallas kernels  12.3 us (12%)
  local copies, waits for them, and re-layouts  9.04 us (9%)
  other arithmetic  4.42 us (4%)
  matrix products  2.05 us (2%)
    ppermute x19, waiting for transfers between devices, permute(): return lax.ppermute(x, 'row', pairs)  37.6 us
    ppermute x19, starting transfers between devices, permute(): return lax.ppermute(x, 'row', pairs)  29.5 us
    pallas_call x4, Pallas kernels, gram(): pl.pallas_call(lambda *refs: gram_kernel(1.0 / feats, tile, *refs), in_sp...  7.7 us
    pallas_call x2, Pallas kernels, apply(): pl.pallas_call(lambda *refs: apply_kernel(slots, runs, tile, *refs), in_s...  3.96 us
    ppermute x1, starting transfers between devices, on_device(): got = lax.ppermute(theirs, 'col', [(c, cols - 1 - c) for c in range(cols)])  3.37 us
    gather x1, local copies, waits for them, and re-layouts, on_device(): own = jnp.take(features, own_ids, axis=0, mode='clip')  3.23 us
    unnamed x10, local copies, waits for them, and re-layouts  2.2 us
    dot_general x1, matrix products, on_device(): lax.dot_general(inverse.reshape(-1, inverse.shape[-1]), block_res, NN, pr...  2.05 us
  transfers between devices with their start and end apart: 20, of which 9 were waited for; matrix products, arithmetic and copies ran while one was open for 8% of the time, Pallas kernels for 10%

profile of v2, /device:TPU:9, one launch (start us, length us, event | category | flops | bytes accessed | tf_op | source)
XLA Modules:
  0.0 98.5 jit_solution(3384638799166990648)
XLA Ops:
  1.1 3.2 %gather_fusion = f32[128,1024]{1,0:T(8,128)S(1)} fusion(f32[1024,1024]{1,0:T(8,128)} %x_ref.1, s32[1024]{0:T(1024)S(1)} %pad_clamp_fusion.1), kind=kCustom, calls=%fused_computation | custom fusion | bytes 1049088 | tf_op jit(solution)/shard_map/jit(_take)/gather | solution.py:167
  4.4 4.5 %collective-permute-start.3 = (f32[128,1024]{1,0:T(8,128)S(1)}, f32[128,1024]{1,0:T(8,128)}, u32[]{:S(2)}, u32[]{:S(2)}) collective-permute-start(f32[128,1024]{1,0:T(8,128)S(1)} %gather_fusion), channel_id=1, source_target_pairs={{4,8},{6,10},{8,4},{10,6},{5,9},{7,11},{9,5},{11,7},{20,24},{22,26... | collective-permute-start | bytes 1572872 | tf_op jit(solution)/shard_map/ppermute | solution.py:149
  9.9 2.0 %convolution_bitcast_fusion = f32[1024,256]{0,1:T(8,128)} fusion(f32[256,256]{1,0:T(8,128)S(1)} %gather_fusion.1, f32[1024,256]{1,0:T(8,128)S(1)} %bitcast.34), kind=kOutput, calls=%fused_computation.2 | convolution fusion | flops 402653184 | bytes 2359296 | tf_op jit(solution)/shard_map/dot_general | solution.py:188
  11.9 1.6 %copy.5 = f32[1024,256]{1,0:T(8,128)S(1)} copy(f32[1024,256]{0,1:T(8,128)} %convolution_bitcast_fusion) | data formatting | bytes 2097152 | tf_op jit(solution)/shard_map/dot_general | solution.py:188
  14.4 1.2 %collective-permute-start.13 = (f32[2,128,256]{2,1,0:T(8,128)}, f32[2,128,256]{2,1,0:T(8,128)}, u32[]{:S(2)}, u32[]{:S(2)}) collective-permute-start(f32[2,128,256]{2,1,0:T(8,128)} %get-tuple-element.43), channel_id=1, source_target_pairs={{0,2},{2,0},{4,6},{6,4},{8,10},{10,8},{12,14},{14,12},{1,3},{3,1},... | collective-permute-start | bytes 786440 | tf_op jit(solution)/shard_map/ppermute | solution.py:149
  15.8 1.2 %collective-permute-start = (f32[128,1024]{1,0:T(8,128)S(1)}, f32[128,1024]{1,0:T(8,128)S(1)}, u32[]{:S(2)}, u32[]{:S(2)}) collective-permute-start(f32[128,1024]{1,0:T(8,128)S(1)} %gather_fusion), channel_id=1, source_target_pairs={{0,2},{2,0},{4,6},{6,4},{8,10},{10,8},{12,14},{14,12},{1,3},{3,1},... | collective-permute-start | bytes 1572872 | tf_op jit(solution)/shard_map/ppermute | solution.py:149
  17.3 3.2 %collective-permute-start.6 = (f32[128,1024]{1,0:T(8,128)S(1)}, f32[128,1024]{1,0:T(8,128)S(1)}, u32[]{:S(2)}, u32[]{:S(2)}) collective-permute-start(f32[128,1024]{1,0:T(8,128)S(1)} %collective-permute-done.1.refs_2_), channel_id=1, source_target_pairs={{4,8},{6,10},{8,4},{10,6},{5,9},{7,11},{9,5},{11,7},{20,24},{22,26... | collective-permute-start | bytes 1572872 | tf_op jit(solution)/shard_map/ppermute | solution.py:149
  21.3 5.6 %collective-permute-done.9 = f32[2,128,256]{2,1,0:T(8,128)} collective-permute-done((f32[2,128,256]{2,1,0:T(8,128)S(1)}, f32[2,128,256]{2,1,0:T(8,128)}, u32[]{:S(2)}, u32[]{:S(2)}) %collective-permute-start.9) | collective-permute-done | bytes 262176 | tf_op jit(solution)/shard_map/ppermute | solution.py:149
  26.9 1.3 %fusion = (f32[2,128,256]{2,1,0:T(8,128)S(1)}, f32[2,128,256]{2,1,0:T(8,128)S(1)}) fusion(f32[2,128,256]{2,1,0:T(8,128)} %collective-permute-done.13, f32[4,2,128,256]{3,2,1,0:T(8,128)} %bitcast.36, s32[]{:T(128)S(6)} %add.43, s32[]{:T(128)S(6)} %select_n.92, f32[2,128,256]{2,1,0:T(8,128)} %collective-permute-done.9), kind=kLoop, calls=%fused_computation.6 | loop fusion | flops 131072 | bytes 1572872 | tf_op jit(solution)/shard_map/add | solution.py:198
  28.2 1.3 %collective-permute-start.10 = (f32[2,128,256]{2,1,0:T(8,128)S(1)}, f32[2,128,256]{2,1,0:T(8,128)S(1)}, u32[]{:S(2)}, u32[]{:S(2)}) collective-permute-start(f32[2,128,256]{2,1,0:T(8,128)S(1)} %get-tuple-element.42), channel_id=1, source_target_pairs={{0,4},{2,6},{12,8},{14,10},{1,5},{3,7},{13,9},{15,11},{16,20},{18,... | collective-permute-start | bytes 786440 | tf_op jit(solution)/shard_map/ppermute | solution.py:149
  29.5 1.3 %collective-permute-start.14 = (f32[2,128,256]{2,1,0:T(8,128)S(1)}, f32[2,128,256]{2,1,0:T(8,128)S(1)}, u32[]{:S(2)}, u32[]{:S(2)}) collective-permute-start(f32[2,128,256]{2,1,0:T(8,128)S(1)} %get-tuple-element.41), channel_id=1, source_target_pairs={{0,4},{2,6},{12,8},{14,10},{1,5},{3,7},{13,9},{15,11},{16,20},{18,... | collective-permute-start | bytes 786440 | tf_op jit(solution)/shard_map/ppermute | solution.py:149
  30.8 4.0 %collective-permute-start.4 = (f32[128,1024]{1,0:T(8,128)}, f32[128,1024]{1,0:T(8,128)S(1)}, u32[]{:S(2)}, u32[]{:S(2)}) collective-permute-start(f32[128,1024]{1,0:T(8,128)} %collective-permute-done.3), channel_id=1, source_target_pairs={{4,0},{6,2},{8,12},{10,14},{5,1},{7,3},{9,13},{11,15},{20,16},{22,... | collective-permute-start | bytes 1572872 | tf_op jit(solution)/shard_map/ppermute | solution.py:149
  35.6 2.2 %collective-permute-start.11 = (f32[2,128,256]{2,1,0:T(8,128)S(1)}, f32[2,128,256]{2,1,0:T(8,128)S(1)}, u32[]{:S(2)}, u32[]{:S(2)}) collective-permute-start(f32[2,128,256]{2,1,0:T(8,128)S(1)} %add.37), channel_id=1, source_target_pairs={{4,8},{6,10},{8,4},{10,6},{5,9},{7,11},{9,5},{11,7},{20,24},{22,26... | collective-permute-start | bytes 786440 | tf_op jit(solution)/shard_map/ppermute | solution.py:149
  37.8 1.9 %collective-permute-done.14 = f32[2,128,256]{2,1,0:T(8,128)S(1)} collective-permute-done((f32[2,128,256]{2,1,0:T(8,128)S(1)}, f32[2,128,256]{2,1,0:T(8,128)S(1)}, u32[]{:S(2)}, u32[]{:S(2)}) %collective-permute-start.14) | collective-permute-done | bytes 262176 | tf_op jit(solution)/shard_map/ppermute | solution.py:149
  39.8 2.8 %collective-permute-start.15 = (f32[2,128,256]{2,1,0:T(8,128)S(1)}, f32[2,128,256]{2,1,0:T(8,128)S(1)}, u32[]{:S(2)}, u32[]{:S(2)}) collective-permute-start(f32[2,128,256]{2,1,0:T(8,128)S(1)} %add.40), channel_id=1, source_target_pairs={{4,8},{6,10},{8,4},{10,6},{5,9},{7,11},{9,5},{11,7},{20,24},{22,26... | collective-permute-start | bytes 786440 | tf_op jit(solution)/shard_map/ppermute | solution.py:149
  42.6 2.2 %copy-done.1 = f32[1024,1024]{1,0:T(8,128)S(1)} copy-done((f32[1024,1024]{1,0:T(8,128)S(1)}, f32[1024,1024]{1,0:T(8,128)}, u32[]{:S(2)}) %copy-start.1) | copy-done | bytes 4194328
  45.4 1.3 %collective-permute-start.2 = (f32[128,1024]{1,0:T(8,128)S(1)}, f32[128,1024]{1,0:T(8,128)S(1)}, u32[]{:S(2)}, u32[]{:S(2)}) collective-permute-start(f32[128,1024]{1,0:T(8,128)S(1)} %collective-permute-done.1.refs_2_), channel_id=1, source_target_pairs={{0,2},{2,0},{4,6},{6,4},{8,10},{10,8},{12,14},{14,12},{1,3},{3,1},... | collective-permute-start | bytes 1572872 | tf_op jit(solution)/shard_map/ppermute | solution.py:149
  46.7 1.3 %collective-permute-start.7 = (f32[128,1024]{1,0:T(8,128)S(1)}, f32[128,1024]{1,0:T(8,128)S(1)}, u32[]{:S(2)}, u32[]{:S(2)}) collective-permute-start(f32[128,1024]{1,0:T(8,128)S(1)} %collective-permute-done.6), channel_id=1, source_target_pairs={{4,0},{6,2},{8,12},{10,14},{5,1},{7,3},{9,13},{11,15},{20,16},{22,... | collective-permute-start | bytes 1572872 | tf_op jit(solution)/shard_map/ppermute | solution.py:149
  48.0 1.9 %shard_map.47 = (bf16[1024,256]{1,0:T(8,128)(2,1)S(1)}, bf16[1024,256]{1,0:T(8,128)(2,1)S(1)}) custom-call(bf16[1024,1024]{1,0:T(8,128)(2,1)S(1)} %get-tuple-element.24.refs_0_, bf16[1024,1024]{1,0:T(8,128)(2,1)S(1)} %get-tuple-element.25.refs_1_, f32[128,1024]{1,0:T(8,128)S(1)} %gather_fusion, f32[128,1024]{1,0:T(8,128)S(1)} %collective-permute-done.refs_3_), custom_call_target="tpu_custom_call" | custom-call | flops 1610612736 | bytes 5242880 | tf_op jit(solution)/shard_map/pallas_call | solution.py:63
  50.0 1.3 %collective-permute-start.12 = (f32[2,128,256]{2,1,0:T(8,128)S(1)}, f32[2,128,256]{2,1,0:T(8,128)S(1)}, u32[]{:S(2)}, u32[]{:S(2)}) collective-permute-start(f32[2,128,256]{2,1,0:T(8,128)S(1)} %add.38), channel_id=1, source_target_pairs={{4,0},{6,2},{8,12},{10,14},{5,1},{7,3},{9,13},{11,15},{20,16},{22,... | collective-permute-start | bytes 786440 | tf_op jit(solution)/shard_map/ppermute | solution.py:149
  51.4 1.3 %collective-permute-start.16 = (f32[2,128,256]{2,1,0:T(8,128)S(1)}, f32[2,128,256]{2,1,0:T(8,128)S(1)}, u32[]{:S(2)}, u32[]{:S(2)}) collective-permute-start(f32[2,128,256]{2,1,0:T(8,128)S(1)} %add.41), channel_id=1, source_target_pairs={{4,0},{6,2},{8,12},{10,14},{5,1},{7,3},{9,13},{11,15},{20,16},{22,... | collective-permute-start | bytes 786440 | tf_op jit(solution)/shard_map/ppermute | solution.py:149
  54.1 5.8 %collective-permute-done.12 = f32[2,128,256]{2,1,0:T(8,128)S(1)} collective-permute-done((f32[2,128,256]{2,1,0:T(8,128)S(1)}, f32[2,128,256]{2,1,0:T(8,128)S(1)}, u32[]{:S(2)}, u32[]{:S(2)}) %collective-permute-start.12) | collective-permute-done | bytes 262176 | tf_op jit(solution)/shard_map/ppermute | solution.py:149
  60.3 1.3 %collective-permute-start.8 = (f32[128,1024]{1,0:T(8,128)S(1)}, f32[128,1024]{1,0:T(8,128)S(1)}, u32[]{:S(2)}, u32[]{:S(2)}) collective-permute-start(f32[128,1024]{1,0:T(8,128)S(1)} %broadcast_select_fusion.refs_2_), channel_id=1, source_target_pairs={{0,2},{2,0},{4,6},{6,4},{8,10},{10,8},{12,14},{14,12},{1,3},{3,1},... | collective-permute-start | bytes 1572872 | tf_op jit(solution)/shard_map/ppermute | solution.py:149
  61.6 3.9 %collective-permute-done.16 = f32[2,128,256]{2,1,0:T(8,128)S(1)} collective-permute-done((f32[2,128,256]{2,1,0:T(8,128)S(1)}, f32[2,128,256]{2,1,0:T(8,128)S(1)}, u32[]{:S(2)}, u32[]{:S(2)}) %collective-permute-start.16) | collective-permute-done | bytes 262176 | tf_op jit(solution)/shard_map/ppermute | solution.py:149
  65.9 1.9 %shard_map.48 = (bf16[1024,256]{1,0:T(8,128)(2,1)S(1)}, bf16[1024,256]{1,0:T(8,128)(2,1)S(1)}) custom-call(bf16[1024,1024]{1,0:T(8,128)(2,1)S(1)} %get-tuple-element.24.refs_0_, bf16[1024,1024]{1,0:T(8,128)(2,1)S(1)} %get-tuple-element.25.refs_1_, f32[128,1024]{1,0:T(8,128)S(1)} %collective-permute-done.1.refs_2_, f32[128,1024]{1,0:T(8,128)S(1)} %collective-permute-done.2.refs_3_), custom_call_target="tpu_custom_call" | custom-call | flops 1610612736 | bytes 5242880 | tf_op jit(solution)/shard_map/pallas_call | solution.py:63
  67.8 1.9 %shard_map.49 = (bf16[1024,256]{1,0:T(8,128)(2,1)S(1)}, bf16[1024,256]{1,0:T(8,128)(2,1)S(1)}) custom-call(bf16[1024,1024]{1,0:T(8,128)(2,1)S(1)} %get-tuple-element.24.refs_0_, bf16[1024,1024]{1,0:T(8,128)(2,1)S(1)} %get-tuple-element.25.refs_1_, f32[128,1024]{1,0:T(8,128)S(1)} %broadcast_select_fusion.1.refs_2_, f32[128,1024]{1,0:T(8,128)S(1)} %collective-permute-done.5.refs_3_), custom_call_target="tpu_custom_call" | custom-call | flops 1610612736 | bytes 5242880 | tf_op jit(solution)/shard_map/pallas_call | solution.py:63
  69.7 14.9 %collective-permute-done.8.refs_3_ = f32[128,1024]{1,0:T(8,128)S(1)} collective-permute-done((f32[128,1024]{1,0:T(8,128)S(1)}, f32[128,1024]{1,0:T(8,128)S(1)}, u32[]{:S(2)}, u32[]{:S(2)}) %collective-permute-start.8) | collective-permute-done | bytes 524320 | tf_op jit(solution)/shard_map/ppermute | solution.py:149
  84.6 1.9 %shard_map.50 = (bf16[1024,256]{1,0:T(8,128)(2,1)S(1)}, bf16[1024,256]{1,0:T(8,128)(2,1)S(1)}) custom-call(bf16[1024,1024]{1,0:T(8,128)(2,1)S(1)} %get-tuple-element.24.refs_0_, bf16[1024,1024]{1,0:T(8,128)(2,1)S(1)} %get-tuple-element.25.refs_1_, f32[128,1024]{1,0:T(8,128)S(1)} %broadcast_select_fusion.refs_2_, f32[128,1024]{1,0:T(8,128)S(1)} %collective-permute-done.8.refs_3_), custom_call_target="tpu_custom_call" | custom-call | flops 1610612736 | bytes 5242880 | tf_op jit(solution)/shard_map/pallas_call | solution.py:63
  86.5 3.7 %collective-permute-done.18.refs_12_ = f32[2,128,256]{2,1,0:T(8,128)S(1)} collective-permute-done((f32[2,128,256]{2,1,0:T(8,128)S(1)}, f32[2,128,256]{2,1,0:T(8,128)S(1)}, u32[]{:S(2)}, u32[]{:S(2)}) %collective-permute-start.18) | collective-permute-done | bytes 262176 | tf_op jit(solution)/shard_map/ppermute | solution.py:149
  90.2 2.0 %shard_map.52 = f32[1024,128]{1,0:T(8,128)S(1)} custom-call(s32[5]{0:T(128)S(1)} %stack.33.refs_0_, bf16[1024,256]{1,0:T(8,128)(2,1)S(1)} %get-tuple-element.27.refs_1_, bf16[1024,256]{1,0:T(8,128)(2,1)S(1)} %get-tuple-element.28.refs_2_, bf16[1024,256]{1,0:T(8,128)(2,1)S(1)} %get-tuple-element.30.refs_3_, bf16[1024,256]{1,0:T(8,128)(2,1)S(1)} %get-tuple-element.32.refs_4_, ...), custom_call_target="tpu_custom_call" | custom-call | flops 805306368 | bytes 4194304 | tf_op jit(solution)/shard_map/pallas_call | solution.py:107
  92.2 3.4 %collective-permute-start.19 = (f32[1024,128]{1,0:T(8,128)S(1)}, f32[1024,128]{1,0:T(8,128)S(1)}, u32[]{:S(2)}, u32[]{:S(2)}) collective-permute-start(f32[1024,128]{1,0:T(8,128)S(1)} %shard_map.52), channel_id=1, source_target_pairs={{0,1},{1,0},{2,3},{3,2},{4,5},{5,4},{6,7},{7,6},{8,9},{9,8},{10,11... | collective-permute-start | bytes 1572872 | tf_op jit(solution)/shard_map/ppermute | solution.py:222
  95.6 2.0 %shard_map.51 = f32[1024,128]{1,0:T(8,128)S(1)} custom-call(s32[5]{0:T(128)S(1)} %stack.35.refs_0_, bf16[1024,256]{1,0:T(8,128)(2,1)S(1)} %get-tuple-element.27.refs_1_, bf16[1024,256]{1,0:T(8,128)(2,1)S(1)} %get-tuple-element.28.refs_2_, bf16[1024,256]{1,0:T(8,128)(2,1)S(1)} %get-tuple-element.30.refs_3_, bf16[1024,256]{1,0:T(8,128)(2,1)S(1)} %get-tuple-element.32.refs_4_, ...), custom_call_target="tpu_custom_call" | custom-call | flops 805306368 | bytes 4194304 | tf_op jit(solution)/shard_map/pallas_call | solution.py:107
  (46 shorter events, 8.8 us)
Async XLA Ops:
  0.0 9.9 %copy-start = (f32[8,1,128,256]{3,2,1,0:T(8,128)S(1)}, f32[8,1,128,256]{3,2,1,0:T(8,128)}, u32[]{:S(2)}) copy-start(f32[8,1,128,256]{3,2,1,0:T(8,128)} %param.4) | copy-start | bytes 3145732
  0.0 8.9 %copy-start.2 = (f32[1024,256]{1,0:T(8,128)S(1)}, f32[1024,256]{1,0:T(8,128)}, u32[]{:S(2)}) copy-start(f32[1024,256]{1,0:T(8,128)} %param.6) | copy-start | bytes 3145732
  4.3 13.0 %collective-permute-start.1 = (f32[128,1024]{1,0:T(8,128)S(1)}, f32[128,1024]{1,0:T(8,128)S(1)}, u32[]{:S(2)}, u32[]{:S(2)}) collective-permute-start(f32[128,1024]{1,0:T(8,128)S(1)} %gather_fusion), channel_id=1, source_target_pairs={{0,4},{2,6},{4,0},{6,2},{8,12},{10,14},{12,8},{14,10},{1,5},{3,7},... | collective-permute-start | bytes 1572872 | tf_op jit(solution)/shard_map/ppermute | solution.py:149
  4.4 26.4 %collective-permute-start.3 = (f32[128,1024]{1,0:T(8,128)S(1)}, f32[128,1024]{1,0:T(8,128)}, u32[]{:S(2)}, u32[]{:S(2)}) collective-permute-start(f32[128,1024]{1,0:T(8,128)S(1)} %gather_fusion), channel_id=1, source_target_pairs={{4,8},{6,10},{8,4},{10,6},{5,9},{7,11},{9,5},{11,7},{20,24},{22,26... | collective-permute-start | bytes 1572872 | tf_op jit(solution)/shard_map/ppermute | solution.py:149
  13.5 2.1 %copy-start.4 = (f32[1024,256]{1,0:T(8,128)}, f32[1024,256]{1,0:T(8,128)S(1)}, u32[]{:S(2)}) copy-start(f32[1024,256]{1,0:T(8,128)S(1)} %copy.5) | copy-start | bytes 3145732
  14.4 6.9 %collective-permute-start.13 = (f32[2,128,256]{2,1,0:T(8,128)}, f32[2,128,256]{2,1,0:T(8,128)}, u32[]{:S(2)}, u32[]{:S(2)}) collective-permute-start(f32[2,128,256]{2,1,0:T(8,128)} %get-tuple-element.43), channel_id=1, source_target_pairs={{0,2},{2,0},{4,6},{6,4},{8,10},{10,8},{12,14},{14,12},{1,3},{3,1},... | collective-permute-start | bytes 786440 | tf_op jit(solution)/shard_map/ppermute | solution.py:149
  15.6 11.3 %collective-permute-start.9 = (f32[2,128,256]{2,1,0:T(8,128)S(1)}, f32[2,128,256]{2,1,0:T(8,128)}, u32[]{:S(2)}, u32[]{:S(2)}) collective-permute-start(f32[2,128,256]{2,1,0:T(8,128)S(1)} %get-tuple-element.44), channel_id=1, source_target_pairs={{0,2},{2,0},{4,6},{6,4},{8,10},{10,8},{12,14},{14,12},{1,3},{3,1},... | collective-permute-start | bytes 786440 | tf_op jit(solution)/shard_map/ppermute | solution.py:149
  15.8 29.5 %collective-permute-start = (f32[128,1024]{1,0:T(8,128)S(1)}, f32[128,1024]{1,0:T(8,128)S(1)}, u32[]{:S(2)}, u32[]{:S(2)}) collective-permute-start(f32[128,1024]{1,0:T(8,128)S(1)} %gather_fusion), channel_id=1, source_target_pairs={{0,2},{2,0},{4,6},{6,4},{8,10},{10,8},{12,14},{14,12},{1,3},{3,1},... | collective-permute-start | bytes 1572872 | tf_op jit(solution)/shard_map/ppermute | solution.py:149
  17.3 29.4 %collective-permute-start.6 = (f32[128,1024]{1,0:T(8,128)S(1)}, f32[128,1024]{1,0:T(8,128)S(1)}, u32[]{:S(2)}, u32[]{:S(2)}) collective-permute-start(f32[128,1024]{1,0:T(8,128)S(1)} %collective-permute-done.1.refs_2_), channel_id=1, source_target_pairs={{4,8},{6,10},{8,4},{10,6},{5,9},{7,11},{9,5},{11,7},{20,24},{22,26... | collective-permute-start | bytes 1572872 | tf_op jit(solution)/shard_map/ppermute | solution.py:149
  28.2 7.4 %collective-permute-start.10 = (f32[2,128,256]{2,1,0:T(8,128)S(1)}, f32[2,128,256]{2,1,0:T(8,128)S(1)}, u32[]{:S(2)}, u32[]{:S(2)}) collective-permute-start(f32[2,128,256]{2,1,0:T(8,128)S(1)} %get-tuple-element.42), channel_id=1, source_target_pairs={{0,4},{2,6},{12,8},{14,10},{1,5},{3,7},{13,9},{15,11},{16,20},{18,... | collective-permute-start | bytes 786440 | tf_op jit(solution)/shard_map/ppermute | solution.py:149
  29.5 10.3 %collective-permute-start.14 = (f32[2,128,256]{2,1,0:T(8,128)S(1)}, f32[2,128,256]{2,1,0:T(8,128)S(1)}, u32[]{:S(2)}, u32[]{:S(2)}) collective-permute-start(f32[2,128,256]{2,1,0:T(8,128)S(1)} %get-tuple-element.41), channel_id=1, source_target_pairs={{0,4},{2,6},{12,8},{14,10},{1,5},{3,7},{13,9},{15,11},{16,20},{18,... | collective-permute-start | bytes 786440 | tf_op jit(solution)/shard_map/ppermute | solution.py:149
  30.8 21.9 %collective-permute-start.4 = (f32[128,1024]{1,0:T(8,128)}, f32[128,1024]{1,0:T(8,128)S(1)}, u32[]{:S(2)}, u32[]{:S(2)}) collective-permute-start(f32[128,1024]{1,0:T(8,128)} %collective-permute-done.3), channel_id=1, source_target_pairs={{4,0},{6,2},{8,12},{10,14},{5,1},{7,3},{9,13},{11,15},{20,16},{22,... | collective-permute-start | bytes 1572872 | tf_op jit(solution)/shard_map/ppermute | solution.py:149
  35.6 14.3 %collective-permute-start.11 = (f32[2,128,256]{2,1,0:T(8,128)S(1)}, f32[2,128,256]{2,1,0:T(8,128)S(1)}, u32[]{:S(2)}, u32[]{:S(2)}) collective-permute-start(f32[2,128,256]{2,1,0:T(8,128)S(1)} %add.37), channel_id=1, source_target_pairs={{4,8},{6,10},{8,4},{10,6},{5,9},{7,11},{9,5},{11,7},{20,24},{22,26... | collective-permute-start | bytes 786440 | tf_op jit(solution)/shard_map/ppermute | solution.py:149
  39.8 11.5 %collective-permute-start.15 = (f32[2,128,256]{2,1,0:T(8,128)S(1)}, f32[2,128,256]{2,1,0:T(8,128)S(1)}, u32[]{:S(2)}, u32[]{:S(2)}) collective-permute-start(f32[2,128,256]{2,1,0:T(8,128)S(1)} %add.40), channel_id=1, source_target_pairs={{4,8},{6,10},{8,4},{10,6},{5,9},{7,11},{9,5},{11,7},{20,24},{22,26... | collective-permute-start | bytes 786440 | tf_op jit(solution)/shard_map/ppermute | solution.py:149
  42.6 2.2 %copy-start.1 = (f32[1024,1024]{1,0:T(8,128)S(1)}, f32[1024,1024]{1,0:T(8,128)}, u32[]{:S(2)}) copy-start(f32[1024,1024]{1,0:T(8,128)} %x_ref.1) | copy-start | bytes 12582916
  45.4 20.5 %collective-permute-start.2 = (f32[128,1024]{1,0:T(8,128)S(1)}, f32[128,1024]{1,0:T(8,128)S(1)}, u32[]{:S(2)}, u32[]{:S(2)}) collective-permute-start(f32[128,1024]{1,0:T(8,128)S(1)} %collective-permute-done.1.refs_2_), channel_id=1, source_target_pairs={{0,2},{2,0},{4,6},{6,4},{8,10},{10,8},{12,14},{14,12},{1,3},{3,1},... | collective-permute-start | bytes 1572872 | tf_op jit(solution)/shard_map/ppermute | solution.py:149
  46.7 13.5 %collective-permute-start.7 = (f32[128,1024]{1,0:T(8,128)S(1)}, f32[128,1024]{1,0:T(8,128)S(1)}, u32[]{:S(2)}, u32[]{:S(2)}) collective-permute-start(f32[128,1024]{1,0:T(8,128)S(1)} %collective-permute-done.6), channel_id=1, source_target_pairs={{4,0},{6,2},{8,12},{10,14},{5,1},{7,3},{9,13},{11,15},{20,16},{22,... | collective-permute-start | bytes 1572872 | tf_op jit(solution)/shard_map/ppermute | solution.py:149
  50.0 9.9 %collective-permute-start.12 = (f32[2,128,256]{2,1,0:T(8,128)S(1)}, f32[2,128,256]{2,1,0:T(8,128)S(1)}, u32[]{:S(2)}, u32[]{:S(2)}) collective-permute-start(f32[2,128,256]{2,1,0:T(8,128)S(1)} %add.38), channel_id=1, source_target_pairs={{4,0},{6,2},{8,12},{10,14},{5,1},{7,3},{9,13},{11,15},{20,16},{22,... | collective-permute-start | bytes 786440 | tf_op jit(solution)/shard_map/ppermute | solution.py:149
  51.4 14.1 %collective-permute-start.16 = (f32[2,128,256]{2,1,0:T(8,128)S(1)}, f32[2,128,256]{2,1,0:T(8,128)S(1)}, u32[]{:S(2)}, u32[]{:S(2)}) collective-permute-start(f32[2,128,256]{2,1,0:T(8,128)S(1)} %add.41), channel_id=1, source_target_pairs={{4,0},{6,2},{8,12},{10,14},{5,1},{7,3},{9,13},{11,15},{20,16},{22,... | collective-permute-start | bytes 786440 | tf_op jit(solution)/shard_map/ppermute | solution.py:149
  53.8 14.0 %collective-permute-start.5 = (f32[128,1024]{1,0:T(8,128)S(1)}, f32[128,1024]{1,0:T(8,128)S(1)}, u32[]{:S(2)}, u32[]{:S(2)}) collective-permute-start(f32[128,1024]{1,0:T(8,128)S(1)} %broadcast_select_fusion.1.refs_2_), channel_id=1, source_target_pairs={{0,2},{2,0},{4,6},{6,4},{8,10},{10,8},{12,14},{14,12},{1,3},{3,1},... | collective-permute-start | bytes 1572872 | tf_op jit(solution)/shard_map/ppermute | solution.py:149
  59.9 26.6 %collective-permute-start.17 = (f32[2,128,256]{2,1,0:T(8,128)S(1)}, f32[2,128,256]{2,1,0:T(8,128)S(1)}, u32[]{:S(2)}, u32[]{:S(2)}) collective-permute-start(f32[2,128,256]{2,1,0:T(8,128)S(1)} %broadcast_select_fusion.3.refs_9_), channel_id=1, source_target_pairs={{0,2},{2,0},{4,6},{6,4},{8,10},{10,8},{12,14},{14,12},{1,3},{3,1},... | collective-permute-start | bytes 786440 | tf_op jit(solution)/shard_map/ppermute | solution.py:149
  60.3 24.3 %collective-permute-start.8 = (f32[128,1024]{1,0:T(8,128)S(1)}, f32[128,1024]{1,0:T(8,128)S(1)}, u32[]{:S(2)}, u32[]{:S(2)}) collective-permute-start(f32[128,1024]{1,0:T(8,128)S(1)} %broadcast_select_fusion.refs_2_), channel_id=1, source_target_pairs={{0,2},{2,0},{4,6},{6,4},{8,10},{10,8},{12,14},{14,12},{1,3},{3,1},... | collective-permute-start | bytes 1572872 | tf_op jit(solution)/shard_map/ppermute | solution.py:149
  65.6 24.6 %collective-permute-start.18 = (f32[2,128,256]{2,1,0:T(8,128)S(1)}, f32[2,128,256]{2,1,0:T(8,128)S(1)}, u32[]{:S(2)}, u32[]{:S(2)}) collective-permute-start(f32[2,128,256]{2,1,0:T(8,128)S(1)} %broadcast_select_fusion.2.refs_10_), channel_id=1, source_target_pairs={{0,2},{2,0},{4,6},{6,4},{8,10},{10,8},{12,14},{14,12},{1,3},{3,1},... | collective-permute-start | bytes 786440 | tf_op jit(solution)/shard_map/ppermute | solution.py:149
  92.2 5.4 %copy-start.3 = (f32[1024,256]{1,0:T(8,128)S(1)}, f32[1024,256]{1,0:T(8,128)}, u32[]{:S(2)}) copy-start(f32[1024,256]{1,0:T(8,128)} %param.6) | copy-start | bytes 3145732
  92.2 5.4 %collective-permute-start.19 = (f32[1024,128]{1,0:T(8,128)S(1)}, f32[1024,128]{1,0:T(8,128)S(1)}, u32[]{:S(2)}, u32[]{:S(2)}) collective-permute-start(f32[1024,128]{1,0:T(8,128)S(1)} %shard_map.52), channel_id=1, source_target_pairs={{0,1},{1,0},{2,3},{3,2},{4,5},{5,4},{6,7},{7,6},{8,9},{9,8},{10,11... | collective-permute-start | bytes 1572872 | tf_op jit(solution)/shard_map/ppermute | solution.py:222

commit v3 on v2

--- a/solution.py
+++ b/solution.py
@@ -9,6 +9,7 @@
 NT = (((1,), (1,)), ((), ()))
 NN = (((1,), (0,)), ((), ()))
 WIDTH = 2
+RUNS = 2
 
 
 def mm(a, b, dims):
@@ -43,6 +44,58 @@
         compiler_params=PARAMS,
         cost_estimate=pl.CostEstimate(flops=4 * rows * cols, bytes_accessed=8 * rows * cols, transcendentals=0),
     )(x)
+
+
+def gather_kernel(whole, ids_ref, x_ref, out_ref, sem):
+    count = out_ref.shape[0]
+    first = 0 if whole else lax.axis_index("col") * count
+    base = lax.axis_index("row") * x_ref.shape[0]
+
+    @pl.loop(0, count, unroll=8)
+    def _(i):
+        row = ids_ref[first + i] - base
+        pltpu.make_async_copy(x_ref.at[pl.ds(row, 1)], out_ref.at[pl.ds(i, 1)], sem).start()
+
+    pltpu.make_async_copy(x_ref.at[pl.ds(0, count)], out_ref, sem).wait()
+
+
+def gather(x, ids, count):
+    return pl.pallas_call(
+        lambda *refs: gather_kernel(count == ids.shape[0], *refs),
+        in_specs=[pl.BlockSpec(memory_space=pltpu.SMEM), pl.BlockSpec(memory_space=pltpu.HBM)],
+        out_specs=VMEM,
+        out_shape=jax.ShapeDtypeStruct((count, x.shape[1]), x.dtype),
+        scratch_shapes=[pltpu.SemaphoreType.DMA],
+        compiler_params=PARAMS,
+        cost_estimate=pl.CostEstimate(flops=0, bytes_accessed=8 * count * x.shape[1], transcendentals=0),
+    )(ids, pltpu.with_memory_space_constraint(x, pltpu.HBM))
+
+
+def partial_kernel(runs, inv_ref, res_ref, *out_refs):
+    y = lax.rem(lax.axis_index("row"), WIDTH)
+    high, low = halves(res_ref[...])
+    for i, ref in enumerate(out_refs):
+        run, side = i % runs, i // runs
+        for k in range(ref.shape[0]):
+            place = (run * ref.shape[0] + k) * WIDTH
+            ih, il = halves(inv_ref[place + (y if side else 1 - y)])
+            ref[k] = mm(ih, low, NN) + mm(il, high, NN) + mm(ih, high, NN)
+
+
+def partial(inverse, res, runs):
+    blocks, half, mine = inverse.shape
+    shape = (blocks // WIDTH // runs, half, res.shape[1])
+    outs = pl.pallas_call(
+        lambda *refs: partial_kernel(runs, *refs),
+        in_specs=[VMEM, VMEM],
+        out_specs=[VMEM] * (2 * runs),
+        out_shape=[jax.ShapeDtypeStruct(shape, F32)] * (2 * runs),
+        compiler_params=PARAMS,
+        cost_estimate=pl.CostEstimate(
+            flops=6 * blocks * half * mine * res.shape[1], bytes_accessed=8 * blocks * half * mine, transcendentals=0
+        ),
+    )(inverse, res)
+    return outs[:runs], outs[runs:]
 
 
 def gram_kernel(scale, tile, xh_ref, xl_ref, near_ref, far_ref, kh_ref, kl_ref, ph_ref, pl_ref):
@@ -74,6 +127,9 @@
 
 
 def apply_kernel(slots, runs, tile, table_ref, *refs):
+    base_ref = None
+    if len(refs) > 2 * slots + 2 * runs + 2:
+        base_ref, refs = refs[0], refs[1:]
     highs, lows = refs[:slots], refs[slots:2 * slots]
     same_refs, cross_refs = refs[2 * slots:2 * slots + runs], refs[2 * slots + runs:2 * slots + 2 * runs]
     out_ref, c_ref = refs[2 * slots + 2 * runs:]
@@ -97,16 +153,16 @@
             rows = pl.ds(2 * j * half, 2 * half)
             both = mm(highs[j][span], c_ref[rows, :], NN)
             total += both[:, :rhs] + (both[:, rhs:] + mm(lows[j][span], c_ref[rows, :rhs], NN))
-        out_ref[span] = total
-
-
-def apply(kerns, sames, crosses, table, parts, tile=512):
+        out_ref[span] = total if base_ref is None else base_ref[span, cols] - total
+
+
+def apply(kerns, sames, crosses, table, parts, base=(), tile=512):
     slots, runs = len(kerns), len(sames)
     rows, points = kerns[0][0].shape
     rhs = sames[0].shape[2] // parts
     return pl.pallas_call(
         lambda *refs: apply_kernel(slots, runs, tile, *refs),
-        in_specs=[pl.BlockSpec(memory_space=pltpu.SMEM)] + [VMEM] * (2 * slots + 2 * runs),
+        in_specs=[pl.BlockSpec(memory_space=pltpu.SMEM)] + [VMEM] * (len(base) + 2 * slots + 2 * runs),
         out_specs=VMEM,
         scratch_shapes=[pltpu.VMEM((slots * points, 2 * rhs), BF16)],
         out_shape=jax.ShapeDtypeStruct((rows, rhs), F32),
@@ -114,7 +170,7 @@
         cost_estimate=pl.CostEstimate(
             flops=6 * rows * slots * points * rhs, bytes_accessed=4 * rows * slots * points, transcendentals=0
         ),
-    )(table, *in_vmem(*[k[0] for k in kerns], *[k[1] for k in kerns]), *sames, *crosses)
+    )(table, *base, *in_vmem(*[k[0] for k in kerns], *[k[1] for k in kerns]), *sames, *crosses)
 
 
 def moves(depth):
@@ -156,15 +212,12 @@
 def on_device(inverse, features, residual, block_ids):
     n = lax.axis_size("row")
     depth = n // WIDTH
-    me, col = lax.axis_index("row"), lax.axis_index("col")
-    cols = lax.axis_size("col")
-    z, y = lax.shift_right_logical(me, 1), lax.bitwise_and(me, 1)
+    col, cols = lax.axis_index("col"), lax.axis_size("col")
+    z = lax.shift_right_logical(lax.axis_index("row"), 1)
     across = [(r, r ^ 1) for r in range(n)]
-    local_ids = block_ids - me * features.shape[0]
     half = block_ids.shape[0] // cols
 
-    own_ids = lax.dynamic_slice_in_dim(local_ids, col * half, half)
-    own = jnp.take(features, own_ids, axis=0, mode="clip")
+    own = gather(features, block_ids, half)
     steps, slots = moves(depth)
 
     other = cols - 1 - col
@@ -178,24 +231,18 @@
         masks.append({name: any_of(z, zs) for name, zs in list(by_name.items())})
     ends = [(z == i) | (z == depth - 1 - i) for i in range(depth // 2 - 1)]
     tables = [jnp.stack(places + [c]).astype(jnp.int32) for c in (other, col)]
-    own, local_ids, y, masks, ends, tables = lax.optimization_barrier((own, local_ids, y, masks, ends, tables))
+    own, masks, ends, tables = lax.optimization_barrier((own, masks, ends, tables))
 
     bufs = {"own": own}
     for name, pairs, source in steps:
         bufs[name] = permute(bufs[source], along(pairs))
 
-    block_res = jnp.take(residual, local_ids, axis=0, mode="clip")
-    partial = lax.dot_general(
-        inverse.reshape(-1, inverse.shape[-1]), block_res, NN,
-        precision=lax.Precision.HIGH, preferred_element_type=F32,
-    ).reshape(depth, WIDTH, half, -1)
-    keep = lax.dynamic_index_in_dim(partial, y, 1, keepdims=False)
-    send = lax.dynamic_index_in_dim(partial, 1 - y, 1, keepdims=False)
+    res = gather(residual, block_ids, block_ids.shape[0])
+    send, keep = partial(inverse.reshape(n, half, -1), res, RUNS)
 
     sames, crosses = [], []
-    for h in range(2):
-        run = slice(h * depth // 2, (h + 1) * depth // 2)
-        term = keep[run] + permute(send[run], across)
+    for h in range(RUNS):
+        term = keep[h] + permute(send[h], across)
         inward = [[(s, s + 1), (depth - 1 - s, depth - 2 - s)] for s in range(depth // 2 - 1)]
         for pairs in inward:
             term = term + permute(term, along(pairs))
@@ -220,9 +267,8 @@
 
     theirs = apply(kerns, sames, crosses, tables[0], cols)
     got = lax.ppermute(theirs, "col", [(c, cols - 1 - c) for c in range(cols)])
-    mine = apply(kerns, sames, crosses, tables[1], cols)
-    rhs = mine.shape[1]
-    return lax.dynamic_slice_in_dim(residual, col * rhs, rhs, 1) - (mine + got)
+    mine = apply(kerns, sames, crosses, tables[1], cols, (residual,))
+    return mine - got
 
 
 def any_of(z, places):

time: 99 us -> 88.8 us (0.90)
  the two profiles are of different devices: /device:TPU:9 before, /device:TPU:11 now
where the time goes in v3:
time: 88.8 us; the launch traced here: 88.4 us
  starting transfers between devices  34.6 us (39%)
  waiting for transfers between devices  33.3 us (37%)
  Pallas kernels  18 us (20%)
  other arithmetic  1.28 us (1%)
    ppermute x19, waiting for transfers between devices, permute(): return lax.ppermute(x, 'row', pairs)  33.3 us
    ppermute x19, starting transfers between devices, permute(): return lax.ppermute(x, 'row', pairs)  30.9 us
    pallas_call x4, Pallas kernels, gram(): pl.pallas_call(lambda *refs: gram_kernel(1.0 / feats, tile, *refs), in_sp...  7.78 us
    pallas_call x2, Pallas kernels, gather(): pl.pallas_call(lambda *refs: gather_kernel(count == ids.shape[0], *refs),...  4.97 us
    pallas_call x2, Pallas kernels, apply(): pl.pallas_call(lambda *refs: apply_kernel(slots, runs, tile, *refs), in_s...  4 us
    ppermute x1, starting transfers between devices, on_device(): got = lax.ppermute(theirs, 'col', [(c, cols - 1 - c) for c in range(cols)])  3.78 us
  transfers between devices with their start and end apart: 20, of which 7 were waited for; matrix products, arithmetic and copies ran while one was open for 0% of the time, Pallas kernels for 16%

profile of v3, /device:TPU:11, one launch (start us, length us, event | category | flops | bytes accessed | tf_op | source)
XLA Modules:
  0.0 88.4 jit_solution(4564493551240772829)
XLA Ops:
  0.9 2.2 %shard_map.46.refs_2_ = f32[128,1024]{1,0:T(8,128)S(1)} custom-call(s32[256]{0:T(256)S(1)} %copy-done.2, f32[1024,1024]{1,0:T(8,128)} %x_ref.1), custom_call_target="tpu_custom_call" | custom-call | bytes 1048576 | tf_op jit(solution)/shard_map/pallas_call | solution.py:63
  3.3 4.3 %collective-permute-start.3 = (f32[128,1024]{1,0:T(8,128)S(1)}, f32[128,1024]{1,0:T(8,128)S(1)}, u32[]{:S(2)}, u32[]{:S(2)}) collective-permute-start(f32[128,1024]{1,0:T(8,128)S(1)} %shard_map.46.refs_2_), channel_id=1, source_target_pairs={{4,8},{6,10},{8,4},{10,6},{5,9},{7,11},{9,5},{11,7},{20,24},{22,26... | collective-permute-start | bytes 1572872 | tf_op jit(solution)/shard_map/ppermute | solution.py:205
  7.6 2.8 %shard_map.52.refs_1_ = f32[256,256]{1,0:T(8,128)S(1)} custom-call(s32[256]{0:T(256)S(1)} %copy-done.2, f32[1024,256]{1,0:T(8,128)} %refs_1_.5), custom_call_target="tpu_custom_call" | custom-call | bytes 524288 | tf_op jit(solution)/shard_map/pallas_call | solution.py:63
  11.0 1.3 %collective-permute-start.9 = (f32[2,128,256]{2,1,0:T(8,128)S(1)}, f32[2,128,256]{2,1,0:T(8,128)S(1)}, u32[]{:S(2)}, u32[]{:S(2)}) collective-permute-start(f32[2,128,256]{2,1,0:T(8,128)S(1)} %get-tuple-element.41), channel_id=1, source_target_pairs={{0,2},{2,0},{4,6},{6,4},{8,10},{10,8},{12,14},{14,12},{1,3},{3,1},... | collective-permute-start | bytes 786440 | tf_op jit(solution)/shard_map/ppermute | solution.py:205
  12.5 1.2 %collective-permute-start = (f32[128,1024]{1,0:T(8,128)S(1)}, f32[128,1024]{1,0:T(8,128)S(1)}, u32[]{:S(2)}, u32[]{:S(2)}) collective-permute-start(f32[128,1024]{1,0:T(8,128)S(1)} %shard_map.46.refs_2_), channel_id=1, source_target_pairs={{0,2},{2,0},{4,6},{6,4},{8,10},{10,8},{12,14},{14,12},{1,3},{3,1},... | collective-permute-start | bytes 1572872 | tf_op jit(solution)/shard_map/ppermute | solution.py:205
  13.8 2.1 %collective-permute-done.1.refs_2_ = f32[128,1024]{1,0:T(8,128)S(1)} collective-permute-done((f32[128,1024]{1,0:T(8,128)S(1)}, f32[128,1024]{1,0:T(8,128)S(1)}, u32[]{:S(2)}, u32[]{:S(2)}) %collective-permute-start.1) | collective-permute-done | bytes 524320 | tf_op jit(solution)/shard_map/ppermute | solution.py:205
  15.9 3.2 %collective-permute-start.6 = (f32[128,1024]{1,0:T(8,128)S(1)}, f32[128,1024]{1,0:T(8,128)S(1)}, u32[]{:S(2)}, u32[]{:S(2)}) collective-permute-start(f32[128,1024]{1,0:T(8,128)S(1)} %collective-permute-done.1.refs_2_), channel_id=1, source_target_pairs={{4,8},{6,10},{8,4},{10,6},{5,9},{7,11},{9,5},{11,7},{20,24},{22,26... | collective-permute-start | bytes 1572872 | tf_op jit(solution)/shard_map/ppermute | solution.py:205
  19.1 1.3 %collective-permute-start.10 = (f32[2,128,256]{2,1,0:T(8,128)S(1)}, f32[2,128,256]{2,1,0:T(8,128)S(1)}, u32[]{:S(2)}, u32[]{:S(2)}) collective-permute-start(f32[2,128,256]{2,1,0:T(8,128)S(1)} %add.18), channel_id=1, source_target_pairs={{0,4},{2,6},{12,8},{14,10},{1,5},{3,7},{13,9},{15,11},{16,20},{18,... | collective-permute-start | bytes 786440 | tf_op jit(solution)/shard_map/ppermute | solution.py:205
  20.4 2.9 %collective-permute-done.13 = f32[2,128,256]{2,1,0:T(8,128)S(1)} collective-permute-done((f32[2,128,256]{2,1,0:T(8,128)S(1)}, f32[2,128,256]{2,1,0:T(8,128)S(1)}, u32[]{:S(2)}, u32[]{:S(2)}) %collective-permute-start.13) | collective-permute-done | bytes 262176 | tf_op jit(solution)/shard_map/ppermute | solution.py:205
  23.4 1.3 %collective-permute-start.14 = (f32[2,128,256]{2,1,0:T(8,128)S(1)}, f32[2,128,256]{2,1,0:T(8,128)S(1)}, u32[]{:S(2)}, u32[]{:S(2)}) collective-permute-start(f32[2,128,256]{2,1,0:T(8,128)S(1)} %add.21), channel_id=1, source_target_pairs={{0,4},{2,6},{12,8},{14,10},{1,5},{3,7},{13,9},{15,11},{16,20},{18,... | collective-permute-start | bytes 786440 | tf_op jit(solution)/shard_map/ppermute | solution.py:205
  24.7 4.0 %collective-permute-start.4 = (f32[128,1024]{1,0:T(8,128)S(1)}, f32[128,1024]{1,0:T(8,128)S(1)}, u32[]{:S(2)}, u32[]{:S(2)}) collective-permute-start(f32[128,1024]{1,0:T(8,128)S(1)} %collective-permute-done.3), channel_id=1, source_target_pairs={{4,0},{6,2},{8,12},{10,14},{5,1},{7,3},{9,13},{11,15},{20,16},{22,... | collective-permute-start | bytes 1572872 | tf_op jit(solution)/shard_map/ppermute | solution.py:205
  28.8 2.2 %collective-permute-start.11 = (f32[2,128,256]{2,1,0:T(8,128)S(1)}, f32[2,128,256]{2,1,0:T(8,128)S(1)}, u32[]{:S(2)}, u32[]{:S(2)}) collective-permute-start(f32[2,128,256]{2,1,0:T(8,128)S(1)} %add.19), channel_id=1, source_target_pairs={{4,8},{6,10},{8,4},{10,6},{5,9},{7,11},{9,5},{11,7},{20,24},{22,26... | collective-permute-start | bytes 786440 | tf_op jit(solution)/shard_map/ppermute | solution.py:205
  31.0 1.2 %collective-permute-done.14 = f32[2,128,256]{2,1,0:T(8,128)S(1)} collective-permute-done((f32[2,128,256]{2,1,0:T(8,128)S(1)}, f32[2,128,256]{2,1,0:T(8,128)S(1)}, u32[]{:S(2)}, u32[]{:S(2)}) %collective-permute-start.14) | collective-permute-done | bytes 262176 | tf_op jit(solution)/shard_map/ppermute | solution.py:205
  32.2 2.4 %collective-permute-start.15 = (f32[2,128,256]{2,1,0:T(8,128)S(1)}, f32[2,128,256]{2,1,0:T(8,128)S(1)}, u32[]{:S(2)}, u32[]{:S(2)}) collective-permute-start(f32[2,128,256]{2,1,0:T(8,128)S(1)} %add.22), channel_id=1, source_target_pairs={{4,8},{6,10},{8,4},{10,6},{5,9},{7,11},{9,5},{11,7},{20,24},{22,26... | collective-permute-start | bytes 786440 | tf_op jit(solution)/shard_map/ppermute | solution.py:205
  35.4 1.3 %collective-permute-start.2 = (f32[128,1024]{1,0:T(8,128)S(1)}, f32[128,1024]{1,0:T(8,128)S(1)}, u32[]{:S(2)}, u32[]{:S(2)}) collective-permute-start(f32[128,1024]{1,0:T(8,128)S(1)} %collective-permute-done.1.refs_2_), channel_id=1, source_target_pairs={{0,2},{2,0},{4,6},{6,4},{8,10},{10,8},{12,14},{14,12},{1,3},{3,1},... | collective-permute-start | bytes 1572872 | tf_op jit(solution)/shard_map/ppermute | solution.py:205
  36.7 1.3 %collective-permute-start.7 = (f32[128,1024]{1,0:T(8,128)S(1)}, f32[128,1024]{1,0:T(8,128)S(1)}, u32[]{:S(2)}, u32[]{:S(2)}) collective-permute-start(f32[128,1024]{1,0:T(8,128)S(1)} %collective-permute-done.6), channel_id=1, source_target_pairs={{4,0},{6,2},{8,12},{10,14},{5,1},{7,3},{9,13},{11,15},{20,16},{22,... | collective-permute-start | bytes 1572872 | tf_op jit(solution)/shard_map/ppermute | solution.py:205
  38.0 1.9 %shard_map.48 = (bf16[1024,256]{1,0:T(8,128)(2,1)S(1)}, bf16[1024,256]{1,0:T(8,128)(2,1)S(1)}) custom-call(bf16[1024,1024]{1,0:T(8,128)(2,1)S(1)} %get-tuple-element.26.refs_0_, bf16[1024,1024]{1,0:T(8,128)(2,1)S(1)} %get-tuple-element.27.refs_1_, f32[128,1024]{1,0:T(8,128)S(1)} %shard_map.46.refs_2_, f32[128,1024]{1,0:T(8,128)S(1)} %collective-permute-done.refs_3_), custom_call_target="tpu_custom_call" | custom-call | flops 1610612736 | bytes 5242880 | tf_op jit(solution)/shard_map/pallas_call | solution.py:116
  40.0 1.3 %collective-permute-start.12 = (f32[2,128,256]{2,1,0:T(8,128)S(1)}, f32[2,128,256]{2,1,0:T(8,128)S(1)}, u32[]{:S(2)}, u32[]{:S(2)}) collective-permute-start(f32[2,128,256]{2,1,0:T(8,128)S(1)} %add.20), channel_id=1, source_target_pairs={{4,0},{6,2},{8,12},{10,14},{5,1},{7,3},{9,13},{11,15},{20,16},{22,... | collective-permute-start | bytes 786440 | tf_op jit(solution)/shard_map/ppermute | solution.py:205
  41.3 1.3 %collective-permute-start.16 = (f32[2,128,256]{2,1,0:T(8,128)S(1)}, f32[2,128,256]{2,1,0:T(8,128)S(1)}, u32[]{:S(2)}, u32[]{:S(2)}) collective-permute-start(f32[2,128,256]{2,1,0:T(8,128)S(1)} %add.23), channel_id=1, source_target_pairs={{4,0},{6,2},{8,12},{10,14},{5,1},{7,3},{9,13},{11,15},{20,16},{22,... | collective-permute-start | bytes 786440 | tf_op jit(solution)/shard_map/ppermute | solution.py:205
  42.7 1.1 %collective-permute-start.5 = (f32[128,1024]{1,0:T(8,128)S(1)}, f32[128,1024]{1,0:T(8,128)S(1)}, u32[]{:S(2)}, u32[]{:S(2)}) collective-permute-start(f32[128,1024]{1,0:T(8,128)S(1)} %broadcast_select_fusion.1.refs_2_), channel_id=1, source_target_pairs={{0,2},{2,0},{4,6},{6,4},{8,10},{10,8},{12,14},{14,12},{1,3},{3,1},... | collective-permute-start | bytes 1572872 | tf_op jit(solution)/shard_map/ppermute | solution.py:205
  43.9 10.6 %collective-permute-done.12 = f32[2,128,256]{2,1,0:T(8,128)S(1)} collective-permute-done((f32[2,128,256]{2,1,0:T(8,128)S(1)}, f32[2,128,256]{2,1,0:T(8,128)S(1)}, u32[]{:S(2)}, u32[]{:S(2)}) %collective-permute-start.12) | collective-permute-done | bytes 262176 | tf_op jit(solution)/shard_map/ppermute | solution.py:205
  54.5 1.1 %collective-permute-start.17 = (f32[2,128,256]{2,1,0:T(8,128)S(1)}, f32[2,128,256]{2,1,0:T(8,128)S(1)}, u32[]{:S(2)}, u32[]{:S(2)}) collective-permute-start(f32[2,128,256]{2,1,0:T(8,128)S(1)} %broadcast_select_fusion.3.refs_10_.refs_9_), channel_id=1, source_target_pairs={{0,2},{2,0},{4,6},{6,4},{8,10},{10,8},{12,14},{14,12},{1,3},{3,1},... | collective-permute-start | bytes 786440 | tf_op jit(solution)/shard_map/ppermute | solution.py:205
  56.2 3.9 %collective-permute-done.16 = f32[2,128,256]{2,1,0:T(8,128)S(1)} collective-permute-done((f32[2,128,256]{2,1,0:T(8,128)S(1)}, f32[2,128,256]{2,1,0:T(8,128)S(1)}, u32[]{:S(2)}, u32[]{:S(2)}) %collective-permute-start.16) | collective-permute-done | bytes 262176 | tf_op jit(solution)/shard_map/ppermute | solution.py:205
  60.1 1.1 %collective-permute-start.18 = (f32[2,128,256]{2,1,0:T(8,128)S(1)}, f32[2,128,256]{2,1,0:T(8,128)S(1)}, u32[]{:S(2)}, u32[]{:S(2)}) collective-permute-start(f32[2,128,256]{2,1,0:T(8,128)S(1)} %broadcast_select_fusion.2.refs_11_.refs_10_), channel_id=1, source_target_pairs={{0,2},{2,0},{4,6},{6,4},{8,10},{10,8},{12,14},{14,12},{1,3},{3,1},... | collective-permute-start | bytes 786440 | tf_op jit(solution)/shard_map/ppermute | solution.py:205
  61.2 2.0 %shard_map.49 = (bf16[1024,256]{1,0:T(8,128)(2,1)S(1)}, bf16[1024,256]{1,0:T(8,128)(2,1)S(1)}) custom-call(bf16[1024,1024]{1,0:T(8,128)(2,1)S(1)} %get-tuple-element.26.refs_0_, bf16[1024,1024]{1,0:T(8,128)(2,1)S(1)} %get-tuple-element.27.refs_1_, f32[128,1024]{1,0:T(8,128)S(1)} %collective-permute-done.1.refs_2_, f32[128,1024]{1,0:T(8,128)S(1)} %collective-permute-done.2.refs_3_), custom_call_target="tpu_custom_call" | custom-call | flops 1610612736 | bytes 5242880 | tf_op jit(solution)/shard_map/pallas_call | solution.py:116
  63.2 1.9 %shard_map.50 = (bf16[1024,256]{1,0:T(8,128)(2,1)S(1)}, bf16[1024,256]{1,0:T(8,128)(2,1)S(1)}) custom-call(bf16[1024,1024]{1,0:T(8,128)(2,1)S(1)} %get-tuple-element.26.refs_0_, bf16[1024,1024]{1,0:T(8,128)(2,1)S(1)} %get-tuple-element.27.refs_1_, f32[128,1024]{1,0:T(8,128)S(1)} %broadcast_select_fusion.1.refs_2_, f32[128,1024]{1,0:T(8,128)S(1)} %collective-permute-done.5.refs_3_), custom_call_target="tpu_custom_call" | custom-call | flops 1610612736 | bytes 5242880 | tf_op jit(solution)/shard_map/pallas_call | solution.py:116
  65.2 9.0 %collective-permute-done.8.refs_3_ = f32[128,1024]{1,0:T(8,128)S(1)} collective-permute-done((f32[128,1024]{1,0:T(8,128)S(1)}, f32[128,1024]{1,0:T(8,128)S(1)}, u32[]{:S(2)}, u32[]{:S(2)}) %collective-permute-start.8) | collective-permute-done | bytes 524320 | tf_op jit(solution)/shard_map/ppermute | solution.py:205
  74.1 1.9 %shard_map.51 = (bf16[1024,256]{1,0:T(8,128)(2,1)S(1)}, bf16[1024,256]{1,0:T(8,128)(2,1)S(1)}) custom-call(bf16[1024,1024]{1,0:T(8,128)(2,1)S(1)} %get-tuple-element.26.refs_0_, bf16[1024,1024]{1,0:T(8,128)(2,1)S(1)} %get-tuple-element.27.refs_1_, f32[128,1024]{1,0:T(8,128)S(1)} %broadcast_select_fusion.refs_2_, f32[128,1024]{1,0:T(8,128)S(1)} %collective-permute-done.8.refs_3_), custom_call_target="tpu_custom_call" | custom-call | flops 1610612736 | bytes 5242880 | tf_op jit(solution)/shard_map/pallas_call | solution.py:116
  76.1 3.7 %collective-permute-done.18.refs_13_.refs_12_ = f32[2,128,256]{2,1,0:T(8,128)S(1)} collective-permute-done((f32[2,128,256]{2,1,0:T(8,128)S(1)}, f32[2,128,256]{2,1,0:T(8,128)S(1)}, u32[]{:S(2)}, u32[]{:S(2)}) %collective-permute-start.18) | collective-permute-done | bytes 262176 | tf_op jit(solution)/shard_map/ppermute | solution.py:205
  79.7 2.0 %shard_map.55 = f32[1024,128]{1,0:T(8,128)S(1)} custom-call(s32[5]{0:T(128)S(1)} %stack.33.refs_0_, bf16[1024,256]{1,0:T(8,128)(2,1)S(1)} %get-tuple-element.29.refs_2_.refs_1_, bf16[1024,256]{1,0:T(8,128)(2,1)S(1)} %get-tuple-element.30.refs_3_.refs_2_, bf16[1024,256]{1,0:T(8,128)(2,1)S(1)} %get-tuple-element.32.refs_4_.refs_3_, ...), custom_call_target="tpu_custom_call" | custom-call | flops 805306368 | bytes 4194304 | tf_op jit(solution)/shard_map/pallas_call | solution.py:163
  81.7 3.8 %collective-permute-start.19 = (f32[1024,128]{1,0:T(8,128)S(1)}, f32[1024,128]{1,0:T(8,128)S(1)}, u32[]{:S(2)}, u32[]{:S(2)}) collective-permute-start(f32[1024,128]{1,0:T(8,128)S(1)} %shard_map.55), channel_id=1, source_target_pairs={{0,1},{1,0},{2,3},{3,2},{4,5},{5,4},{6,7},{7,6},{8,9},{9,8},{10,11... | collective-permute-start | bytes 1572872 | tf_op jit(solution)/shard_map/ppermute | solution.py:269
  85.5 2.0 %shard_map.54 = f32[1024,128]{1,0:T(8,128)S(1)} custom-call(s32[5]{0:T(128)S(1)} %stack.35.refs_0_, f32[1024,256]{1,0:T(8,128)S(1)} %copy-done.1, bf16[1024,256]{1,0:T(8,128)(2,1)S(1)} %get-tuple-element.29.refs_2_.refs_1_, bf16[1024,256]{1,0:T(8,128)(2,1)S(1)} %get-tuple-element.30.refs_3_.refs_2_, bf16[1024,256]{1,0:T(8,128)(2,1)S(1)} %get-tuple-element.32.refs_4_.refs_3_, ...), custom_call_target="tpu_custom_call" | custom-call | flops 805306368 | bytes 4194304 | tf_op jit(solution)/shard_map/pallas_call | solution.py:163
  (39 shorter events, 4.3 us)
Async XLA Ops:
  0.2 0.7 copy-start.2
  0.8 9.6 %copy-start.3 = (f32[8,1,128,256]{3,2,1,0:T(8,128)S(1)}, f32[8,1,128,256]{3,2,1,0:T(8,128)}, u32[]{:S(2)}) copy-start(f32[8,1,128,256]{3,2,1,0:T(8,128)} %param.4) | copy-start | bytes 3145732
  3.0 12.9 %collective-permute-start.1 = (f32[128,1024]{1,0:T(8,128)S(1)}, f32[128,1024]{1,0:T(8,128)S(1)}, u32[]{:S(2)}, u32[]{:S(2)}) collective-permute-start(f32[128,1024]{1,0:T(8,128)S(1)} %shard_map.46.refs_2_), channel_id=1, source_target_pairs={{0,4},{2,6},{4,0},{6,2},{8,12},{10,14},{12,8},{14,10},{1,5},{3,7},... | collective-permute-start | bytes 1572872 | tf_op jit(solution)/shard_map/ppermute | solution.py:205
  3.3 21.4 %collective-permute-start.3 = (f32[128,1024]{1,0:T(8,128)S(1)}, f32[128,1024]{1,0:T(8,128)S(1)}, u32[]{:S(2)}, u32[]{:S(2)}) collective-permute-start(f32[128,1024]{1,0:T(8,128)S(1)} %shard_map.46.refs_2_), channel_id=1, source_target_pairs={{4,8},{6,10},{8,4},{10,6},{5,9},{7,11},{9,5},{11,7},{20,24},{22,26... | collective-permute-start | bytes 1572872 | tf_op jit(solution)/shard_map/ppermute | solution.py:205
  10.4 24.3 %copy-start = (f32[1024,1024]{1,0:T(8,128)S(1)}, f32[1024,1024]{1,0:T(8,128)}, u32[]{:S(2)}) copy-start(f32[1024,1024]{1,0:T(8,128)} %x_ref.1) | copy-start | bytes 12582916
  11.0 8.1 %collective-permute-start.9 = (f32[2,128,256]{2,1,0:T(8,128)S(1)}, f32[2,128,256]{2,1,0:T(8,128)S(1)}, u32[]{:S(2)}, u32[]{:S(2)}) collective-permute-start(f32[2,128,256]{2,1,0:T(8,128)S(1)} %get-tuple-element.41), channel_id=1, source_target_pairs={{0,2},{2,0},{4,6},{6,4},{8,10},{10,8},{12,14},{14,12},{1,3},{3,1},... | collective-permute-start | bytes 786440 | tf_op jit(solution)/shard_map/ppermute | solution.py:205
  12.3 11.0 %collective-permute-start.13 = (f32[2,128,256]{2,1,0:T(8,128)S(1)}, f32[2,128,256]{2,1,0:T(8,128)S(1)}, u32[]{:S(2)}, u32[]{:S(2)}) collective-permute-start(f32[2,128,256]{2,1,0:T(8,128)S(1)} %get-tuple-element.43), channel_id=1, source_target_pairs={{0,2},{2,0},{4,6},{6,4},{8,10},{10,8},{12,14},{14,12},{1,3},{3,1},... | collective-permute-start | bytes 786440 | tf_op jit(solution)/shard_map/ppermute | solution.py:205
  12.5 22.8 %collective-permute-start = (f32[128,1024]{1,0:T(8,128)S(1)}, f32[128,1024]{1,0:T(8,128)S(1)}, u32[]{:S(2)}, u32[]{:S(2)}) collective-permute-start(f32[128,1024]{1,0:T(8,128)S(1)} %shard_map.46.refs_2_), channel_id=1, source_target_pairs={{0,2},{2,0},{4,6},{6,4},{8,10},{10,8},{12,14},{14,12},{1,3},{3,1},... | collective-permute-start | bytes 1572872 | tf_op jit(solution)/shard_map/ppermute | solution.py:205
  15.9 20.8 %collective-permute-start.6 = (f32[128,1024]{1,0:T(8,128)S(1)}, f32[128,1024]{1,0:T(8,128)S(1)}, u32[]{:S(2)}, u32[]{:S(2)}) collective-permute-start(f32[128,1024]{1,0:T(8,128)S(1)} %collective-permute-done.1.refs_2_), channel_id=1, source_target_pairs={{4,8},{6,10},{8,4},{10,6},{5,9},{7,11},{9,5},{11,7},{20,24},{22,26... | collective-permute-start | bytes 1572872 | tf_op jit(solution)/shard_map/ppermute | solution.py:205
  19.1 9.6 %collective-permute-start.10 = (f32[2,128,256]{2,1,0:T(8,128)S(1)}, f32[2,128,256]{2,1,0:T(8,128)S(1)}, u32[]{:S(2)}, u32[]{:S(2)}) collective-permute-start(f32[2,128,256]{2,1,0:T(8,128)S(1)} %add.18), channel_id=1, source_target_pairs={{0,4},{2,6},{12,8},{14,10},{1,5},{3,7},{13,9},{15,11},{16,20},{18,... | collective-permute-start | bytes 786440 | tf_op jit(solution)/shard_map/ppermute | solution.py:205
  23.4 8.8 %collective-permute-start.14 = (f32[2,128,256]{2,1,0:T(8,128)S(1)}, f32[2,128,256]{2,1,0:T(8,128)S(1)}, u32[]{:S(2)}, u32[]{:S(2)}) collective-permute-start(f32[2,128,256]{2,1,0:T(8,128)S(1)} %add.21), channel_id=1, source_target_pairs={{0,4},{2,6},{12,8},{14,10},{1,5},{3,7},{13,9},{15,11},{16,20},{18,... | collective-permute-start | bytes 786440 | tf_op jit(solution)/shard_map/ppermute | solution.py:205
  24.7 18.0 %collective-permute-start.4 = (f32[128,1024]{1,0:T(8,128)S(1)}, f32[128,1024]{1,0:T(8,128)S(1)}, u32[]{:S(2)}, u32[]{:S(2)}) collective-permute-start(f32[128,1024]{1,0:T(8,128)S(1)} %collective-permute-done.3), channel_id=1, source_target_pairs={{4,0},{6,2},{8,12},{10,14},{5,1},{7,3},{9,13},{11,15},{20,16},{22,... | collective-permute-start | bytes 1572872 | tf_op jit(solution)/shard_map/ppermute | solution.py:205
  28.8 11.1 %collective-permute-start.11 = (f32[2,128,256]{2,1,0:T(8,128)S(1)}, f32[2,128,256]{2,1,0:T(8,128)S(1)}, u32[]{:S(2)}, u32[]{:S(2)}) collective-permute-start(f32[2,128,256]{2,1,0:T(8,128)S(1)} %add.19), channel_id=1, source_target_pairs={{4,8},{6,10},{8,4},{10,6},{5,9},{7,11},{9,5},{11,7},{20,24},{22,26... | collective-permute-start | bytes 786440 | tf_op jit(solution)/shard_map/ppermute | solution.py:205
  32.2 9.0 %collective-permute-start.15 = (f32[2,128,256]{2,1,0:T(8,128)S(1)}, f32[2,128,256]{2,1,0:T(8,128)S(1)}, u32[]{:S(2)}, u32[]{:S(2)}) collective-permute-start(f32[2,128,256]{2,1,0:T(8,128)S(1)} %add.22), channel_id=1, source_target_pairs={{4,8},{6,10},{8,4},{10,6},{5,9},{7,11},{9,5},{11,7},{20,24},{22,26... | collective-permute-start | bytes 786440 | tf_op jit(solution)/shard_map/ppermute | solution.py:205
  35.4 25.9 %collective-permute-start.2 = (f32[128,1024]{1,0:T(8,128)S(1)}, f32[128,1024]{1,0:T(8,128)S(1)}, u32[]{:S(2)}, u32[]{:S(2)}) collective-permute-start(f32[128,1024]{1,0:T(8,128)S(1)} %collective-permute-done.1.refs_2_), channel_id=1, source_target_pairs={{0,2},{2,0},{4,6},{6,4},{8,10},{10,8},{12,14},{14,12},{1,3},{3,1},... | collective-permute-start | bytes 1572872 | tf_op jit(solution)/shard_map/ppermute | solution.py:205
  36.7 19.0 %collective-permute-start.7 = (f32[128,1024]{1,0:T(8,128)S(1)}, f32[128,1024]{1,0:T(8,128)S(1)}, u32[]{:S(2)}, u32[]{:S(2)}) collective-permute-start(f32[128,1024]{1,0:T(8,128)S(1)} %collective-permute-done.6), channel_id=1, source_target_pairs={{4,0},{6,2},{8,12},{10,14},{5,1},{7,3},{9,13},{11,15},{20,16},{22,... | collective-permute-start | bytes 1572872 | tf_op jit(solution)/shard_map/ppermute | solution.py:205
  40.0 14.5 %collective-permute-start.12 = (f32[2,128,256]{2,1,0:T(8,128)S(1)}, f32[2,128,256]{2,1,0:T(8,128)S(1)}, u32[]{:S(2)}, u32[]{:S(2)}) collective-permute-start(f32[2,128,256]{2,1,0:T(8,128)S(1)} %add.20), channel_id=1, source_target_pairs={{4,0},{6,2},{8,12},{10,14},{5,1},{7,3},{9,13},{11,15},{20,16},{22,... | collective-permute-start | bytes 786440 | tf_op jit(solution)/shard_map/ppermute | solution.py:205
  41.3 18.7 %collective-permute-start.16 = (f32[2,128,256]{2,1,0:T(8,128)S(1)}, f32[2,128,256]{2,1,0:T(8,128)S(1)}, u32[]{:S(2)}, u32[]{:S(2)}) collective-permute-start(f32[2,128,256]{2,1,0:T(8,128)S(1)} %add.23), channel_id=1, source_target_pairs={{4,0},{6,2},{8,12},{10,14},{5,1},{7,3},{9,13},{11,15},{20,16},{22,... | collective-permute-start | bytes 786440 | tf_op jit(solution)/shard_map/ppermute | solution.py:205
  42.7 20.5 %collective-permute-start.5 = (f32[128,1024]{1,0:T(8,128)S(1)}, f32[128,1024]{1,0:T(8,128)S(1)}, u32[]{:S(2)}, u32[]{:S(2)}) collective-permute-start(f32[128,1024]{1,0:T(8,128)S(1)} %broadcast_select_fusion.1.refs_2_), channel_id=1, source_target_pairs={{0,2},{2,0},{4,6},{6,4},{8,10},{10,8},{12,14},{14,12},{1,3},{3,1},... | collective-permute-start | bytes 1572872 | tf_op jit(solution)/shard_map/ppermute | solution.py:205
  54.5 21.6 %collective-permute-start.17 = (f32[2,128,256]{2,1,0:T(8,128)S(1)}, f32[2,128,256]{2,1,0:T(8,128)S(1)}, u32[]{:S(2)}, u32[]{:S(2)}) collective-permute-start(f32[2,128,256]{2,1,0:T(8,128)S(1)} %broadcast_select_fusion.3.refs_10_.refs_9_), channel_id=1, source_target_pairs={{0,2},{2,0},{4,6},{6,4},{8,10},{10,8},{12,14},{14,12},{1,3},{3,1},... | collective-permute-start | bytes 786440 | tf_op jit(solution)/shard_map/ppermute | solution.py:205
  55.7 18.4 %collective-permute-start.8 = (f32[128,1024]{1,0:T(8,128)S(1)}, f32[128,1024]{1,0:T(8,128)S(1)}, u32[]{:S(2)}, u32[]{:S(2)}) collective-permute-start(f32[128,1024]{1,0:T(8,128)S(1)} %broadcast_select_fusion.refs_2_), channel_id=1, source_target_pairs={{0,2},{2,0},{4,6},{6,4},{8,10},{10,8},{12,14},{14,12},{1,3},{3,1},... | collective-permute-start | bytes 1572872 | tf_op jit(solution)/shard_map/ppermute | solution.py:205
  60.1 19.6 %collective-permute-start.18 = (f32[2,128,256]{2,1,0:T(8,128)S(1)}, f32[2,128,256]{2,1,0:T(8,128)S(1)}, u32[]{:S(2)}, u32[]{:S(2)}) collective-permute-start(f32[2,128,256]{2,1,0:T(8,128)S(1)} %broadcast_select_fusion.2.refs_11_.refs_10_), channel_id=1, source_target_pairs={{0,2},{2,0},{4,6},{6,4},{8,10},{10,8},{12,14},{14,12},{1,3},{3,1},... | collective-permute-start | bytes 786440 | tf_op jit(solution)/shard_map/ppermute | solution.py:205
  79.7 5.8 %copy-start.1 = (f32[1024,256]{1,0:T(8,128)S(1)}, f32[1024,256]{1,0:T(8,128)}, u32[]{:S(2)}) copy-start(f32[1024,256]{1,0:T(8,128)} %refs_1_.5) | copy-start | bytes 3145732
  81.7 5.8 %collective-permute-start.19 = (f32[1024,128]{1,0:T(8,128)S(1)}, f32[1024,128]{1,0:T(8,128)S(1)}, u32[]{:S(2)}, u32[]{:S(2)}) collective-permute-start(f32[1024,128]{1,0:T(8,128)S(1)} %shard_map.55), channel_id=1, source_target_pairs={{0,1},{1,0},{2,3},{3,2},{4,5},{5,4},{6,7},{7,6},{8,9},{9,8},{10,11... | collective-permute-start | bytes 1572872 | tf_op jit(solution)/shard_map/ppermute | solution.py:269

commit v4 on v3

--- a/solution.py
+++ b/solution.py
@@ -46,7 +46,10 @@
     )(x)
 
 
-def gather_kernel(whole, ids_ref, x_ref, out_ref, sem):
+def gather_kernel(whole, ids_hbm, x_ref, out_ref, ids_ref, ids_sem, sem):
+    copy = pltpu.make_async_copy(ids_hbm, ids_ref, ids_sem)
+    copy.start()
+    copy.wait()
     count = out_ref.shape[0]
     first = 0 if whole else lax.axis_index("col") * count
     base = lax.axis_index("row") * x_ref.shape[0]
@@ -62,13 +65,13 @@
 def gather(x, ids, count):
     return pl.pallas_call(
         lambda *refs: gather_kernel(count == ids.shape[0], *refs),
-        in_specs=[pl.BlockSpec(memory_space=pltpu.SMEM), pl.BlockSpec(memory_space=pltpu.HBM)],
+        in_specs=[pl.BlockSpec(memory_space=pltpu.HBM)] * 2,
         out_specs=VMEM,
         out_shape=jax.ShapeDtypeStruct((count, x.shape[1]), x.dtype),
-        scratch_shapes=[pltpu.SemaphoreType.DMA],
+        scratch_shapes=[pltpu.SMEM(ids.shape, ids.dtype), pltpu.SemaphoreType.DMA, pltpu.SemaphoreType.DMA],
         compiler_params=PARAMS,
         cost_estimate=pl.CostEstimate(flops=0, bytes_accessed=8 * count * x.shape[1], transcendentals=0),
-    )(ids, pltpu.with_memory_space_constraint(x, pltpu.HBM))
+    )(*[pltpu.with_memory_space_constraint(a, pltpu.HBM) for a in (ids, x)])
 
 
 def partial_kernel(runs, inv_ref, res_ref, *out_refs):
@@ -148,11 +151,10 @@
 
     for r in range(0, out_ref.shape[0], tile):
         span = slice(r, r + tile)
-        total = jnp.zeros((tile, rhs), F32)
-        for j in range(slots):
-            rows = pl.ds(2 * j * half, 2 * half)
-            both = mm(highs[j][span], c_ref[rows, :], NN)
-            total += both[:, :rhs] + (both[:, rhs:] + mm(lows[j][span], c_ref[rows, :rhs], NN))
+        high = jnp.concatenate([ref[span] for ref in highs], 1)
+        low = jnp.concatenate([ref[span] for ref in lows], 1)
+        both = mm(high, c_ref[...], NN)
+        total = both[:, :rhs] + (both[:, rhs:] + mm(low, c_ref[:, :rhs], NN))
         out_ref[span] = total if base_ref is None else base_ref[span, cols] - total
 
 
@@ -255,14 +257,18 @@
         crosses.append(permute(term, across))
 
     x_high, x_low = split(features)
-    kerns = []
+    kerns, fars = [], []
     for j in range(depth):
         block = own
         if j > 0:
             block = None
             for name, mask in masks[j - 1].items():
                 block = bufs[name] if block is None else jnp.where(mask, bufs[name], block)
-        far = permute(block, across)
+        if j == 1 and depth == 4:
+            far = permute(fars[0], along(steps[0][1]))
+        else:
+            far = permute(block, across)
+        fars.append(far)
         kerns.append(gram(x_high, x_low, block, far))
 
     theirs = apply(kerns, sames, crosses, tables[0], cols)

time: 88.8 us -> 97.5 us (1.098)
  the two profiles are of different devices: /device:TPU:11 before, /device:TPU:0 now
where the time goes in v4:
time: 97.5 us; the launch traced here: 97.1 us
  waiting for transfers between devices  39.8 us (41%)
  starting transfers between devices  37.3 us (38%)
  Pallas kernels  18.3 us (19%)
  other arithmetic  1.29 us (1%)
    ppermute x19, waiting for transfers between devices, permute(): return lax.ppermute(x, 'row', pairs)  39.8 us
    ppermute x19, starting transfers between devices, permute(): return lax.ppermute(x, 'row', pairs)  37.2 us
    pallas_call x4, Pallas kernels, gram(): pl.pallas_call(lambda *refs: gram_kernel(1.0 / feats, tile, *refs), in_sp...  7.76 us
    pallas_call x2, Pallas kernels, gather(): pl.pallas_call(lambda *refs: gather_kernel(count == ids.shape[0], *refs),...  5.4 us
    pallas_call x2, Pallas kernels, apply(): pl.pallas_call(lambda *refs: apply_kernel(slots, runs, tile, *refs), in_s...  3.97 us
  transfers between devices with their start and end apart: 20, of which 8 were waited for; matrix products, arithmetic and copies ran while one was open for 0% of the time, Pallas kernels for 14%

profile of v4, /device:TPU:0, one launch (start us, length us, event | category | flops | bytes accessed | tf_op | source)
XLA Modules:
  0.0 97.1 jit_solution(7552205530328606202)
XLA Ops:
  0.2 2.4 %shard_map.46.refs_2_ = f32[128,1024]{1,0:T(8,128)S(1)} custom-call(s32[256]{0:T(256)} %refs_0_.3, f32[1024,1024]{1,0:T(8,128)} %x_ref.1), custom_call_target="tpu_custom_call" | custom-call | bytes 1048576 | tf_op jit(solution)/shard_map/pallas_call | solution.py:66
  2.6 3.1 %collective-permute-start.1 = (f32[128,1024]{1,0:T(8,128)S(1)}, f32[128,1024]{1,0:T(8,128)S(1)}, u32[]{:S(2)}, u32[]{:S(2)}) collective-permute-start(f32[128,1024]{1,0:T(8,128)S(1)} %shard_map.46.refs_2_), channel_id=1, source_target_pairs={{0,4},{2,6},{4,0},{6,2},{8,12},{10,14},{12,8},{14,10},{1,5},{3,7},... | collective-permute-start | bytes 1572872 | tf_op jit(solution)/shard_map/ppermute | solution.py:207
  5.7 0.7 collective-permute-start.3
  6.4 3.0 %shard_map.52.refs_1_ = f32[256,256]{1,0:T(8,128)S(1)} custom-call(s32[256]{0:T(256)} %refs_0_.3, f32[1024,256]{1,0:T(8,128)} %refs_1_.5), custom_call_target="tpu_custom_call" | custom-call | bytes 524288 | tf_op jit(solution)/shard_map/pallas_call | solution.py:66
  10.0 1.6 %collective-permute-start.9 = (f32[2,128,256]{2,1,0:T(8,128)S(1)}, f32[2,128,256]{2,1,0:T(8,128)S(1)}, u32[]{:S(2)}, u32[]{:S(2)}) collective-permute-start(f32[2,128,256]{2,1,0:T(8,128)S(1)} %get-tuple-element.41), channel_id=1, source_target_pairs={{0,2},{2,0},{4,6},{6,4},{8,10},{10,8},{12,14},{14,12},{1,3},{3,1},... | collective-permute-start | bytes 786440 | tf_op jit(solution)/shard_map/ppermute | solution.py:207
  12.1 1.5 %collective-permute-start = (f32[128,1024]{1,0:T(8,128)S(1)}, f32[128,1024]{1,0:T(8,128)S(1)}, u32[]{:S(2)}, u32[]{:S(2)}) collective-permute-start(f32[128,1024]{1,0:T(8,128)S(1)} %shard_map.46.refs_2_), channel_id=1, source_target_pairs={{0,2},{2,0},{4,6},{6,4},{8,10},{10,8},{12,14},{14,12},{1,3},{3,1},... | collective-permute-start | bytes 1572872 | tf_op jit(solution)/shard_map/ppermute | solution.py:207
  13.6 4.0 %collective-permute-done.1.refs_2_ = f32[128,1024]{1,0:T(8,128)S(1)} collective-permute-done((f32[128,1024]{1,0:T(8,128)S(1)}, f32[128,1024]{1,0:T(8,128)S(1)}, u32[]{:S(2)}, u32[]{:S(2)}) %collective-permute-start.1) | collective-permute-done | bytes 524320 | tf_op jit(solution)/shard_map/ppermute | solution.py:207
  17.7 0.7 collective-permute-start.6
  18.3 0.9 collective-permute-done.9
  19.3 6.3 %collective-permute-start.10 = (f32[2,128,256]{2,1,0:T(8,128)S(1)}, f32[2,128,256]{2,1,0:T(8,128)S(1)}, u32[]{:S(2)}, u32[]{:S(2)}) collective-permute-start(f32[2,128,256]{2,1,0:T(8,128)S(1)} %add.18), channel_id=1, source_target_pairs={{0,4},{2,6},{12,8},{14,10},{1,5},{3,7},{13,9},{15,11},{16,20},{18,... | collective-permute-start | bytes 786440 | tf_op jit(solution)/shard_map/ppermute | solution.py:207
  25.6 5.6 %collective-permute-start.14 = (f32[2,128,256]{2,1,0:T(8,128)S(1)}, f32[2,128,256]{2,1,0:T(8,128)S(1)}, u32[]{:S(2)}, u32[]{:S(2)}) collective-permute-start(f32[2,128,256]{2,1,0:T(8,128)S(1)} %add.21), channel_id=1, source_target_pairs={{0,4},{2,6},{12,8},{14,10},{1,5},{3,7},{13,9},{15,11},{16,20},{18,... | collective-permute-start | bytes 786440 | tf_op jit(solution)/shard_map/ppermute | solution.py:207
  31.2 1.3 %collective-permute-start.4 = (f32[128,1024]{1,0:T(8,128)S(1)}, f32[128,1024]{1,0:T(8,128)S(1)}, u32[]{:S(2)}, u32[]{:S(2)}) collective-permute-start(f32[128,1024]{1,0:T(8,128)S(1)} %collective-permute-done.3), channel_id=1, source_target_pairs={{4,0},{6,2},{8,12},{10,14},{5,1},{7,3},{9,13},{11,15},{20,16},{22,... | collective-permute-start | bytes 1572872 | tf_op jit(solution)/shard_map/ppermute | solution.py:207
  32.6 0.7 collective-permute-start.11
  33.2 1.8 %collective-permute-done.14 = f32[2,128,256]{2,1,0:T(8,128)S(1)} collective-permute-done((f32[2,128,256]{2,1,0:T(8,128)S(1)}, f32[2,128,256]{2,1,0:T(8,128)S(1)}, u32[]{:S(2)}, u32[]{:S(2)}) %collective-permute-start.14) | collective-permute-done | bytes 262176 | tf_op jit(solution)/shard_map/ppermute | solution.py:207
  35.1 0.7 collective-permute-start.15
  36.4 5.4 %collective-permute-start.2 = (f32[128,1024]{1,0:T(8,128)S(1)}, f32[128,1024]{1,0:T(8,128)S(1)}, u32[]{:S(2)}, u32[]{:S(2)}) collective-permute-start(f32[128,1024]{1,0:T(8,128)S(1)} %collective-permute-done.refs_3_), channel_id=1, source_target_pairs={{0,4},{2,6},{4,0},{6,2},{8,12},{10,14},{12,8},{14,10},{1,5},{3,7},... | collective-permute-start | bytes 1572872 | tf_op jit(solution)/shard_map/ppermute | solution.py:207
  41.9 1.3 %collective-permute-start.7 = (f32[128,1024]{1,0:T(8,128)S(1)}, f32[128,1024]{1,0:T(8,128)S(1)}, u32[]{:S(2)}, u32[]{:S(2)}) collective-permute-start(f32[128,1024]{1,0:T(8,128)S(1)} %collective-permute-done.6), channel_id=1, source_target_pairs={{4,0},{6,2},{8,12},{10,14},{5,1},{7,3},{9,13},{11,15},{20,16},{22,... | collective-permute-start | bytes 1572872 | tf_op jit(solution)/shard_map/ppermute | solution.py:207
  43.2 1.9 %shard_map.48 = (bf16[1024,256]{1,0:T(8,128)(2,1)S(1)}, bf16[1024,256]{1,0:T(8,128)(2,1)S(1)}) custom-call(bf16[1024,1024]{1,0:T(8,128)(2,1)S(1)} %get-tuple-element.26.refs_0_, bf16[1024,1024]{1,0:T(8,128)(2,1)S(1)} %get-tuple-element.27.refs_1_, f32[128,1024]{1,0:T(8,128)S(1)} %shard_map.46.refs_2_, f32[128,1024]{1,0:T(8,128)S(1)} %collective-permute-done.refs_3_), custom_call_target="tpu_custom_call" | custom-call | flops 1610612736 | bytes 5242880 | tf_op jit(solution)/shard_map/pallas_call | solution.py:119
  45.1 1.3 %collective-permute-start.12 = (f32[2,128,256]{2,1,0:T(8,128)S(1)}, f32[2,128,256]{2,1,0:T(8,128)S(1)}, u32[]{:S(2)}, u32[]{:S(2)}) collective-permute-start(f32[2,128,256]{2,1,0:T(8,128)S(1)} %add.20), channel_id=1, source_target_pairs={{4,0},{6,2},{8,12},{10,14},{5,1},{7,3},{9,13},{11,15},{20,16},{22,... | collective-permute-start | bytes 786440 | tf_op jit(solution)/shard_map/ppermute | solution.py:207
  46.5 1.3 %collective-permute-start.16 = (f32[2,128,256]{2,1,0:T(8,128)S(1)}, f32[2,128,256]{2,1,0:T(8,128)S(1)}, u32[]{:S(2)}, u32[]{:S(2)}) collective-permute-start(f32[2,128,256]{2,1,0:T(8,128)S(1)} %add.23), channel_id=1, source_target_pairs={{4,0},{6,2},{8,12},{10,14},{5,1},{7,3},{9,13},{11,15},{20,16},{22,... | collective-permute-start | bytes 786440 | tf_op jit(solution)/shard_map/ppermute | solution.py:207
  48.0 1.6 %collective-permute-start.5 = (f32[128,1024]{1,0:T(8,128)S(1)}, f32[128,1024]{1,0:T(8,128)S(1)}, u32[]{:S(2)}, u32[]{:S(2)}) collective-permute-start(f32[128,1024]{1,0:T(8,128)S(1)} %broadcast_select_fusion.1.refs_2_), channel_id=1, source_target_pairs={{0,2},{2,0},{4,6},{6,4},{8,10},{10,8},{12,14},{14,12},{1,3},{3,1},... | collective-permute-start | bytes 1572872 | tf_op jit(solution)/shard_map/ppermute | solution.py:207
  49.6 24.7 %collective-permute-done.12 = f32[2,128,256]{2,1,0:T(8,128)S(1)} collective-permute-done((f32[2,128,256]{2,1,0:T(8,128)S(1)}, f32[2,128,256]{2,1,0:T(8,128)S(1)}, u32[]{:S(2)}, u32[]{:S(2)}) %collective-permute-start.12) | collective-permute-done | bytes 262176 | tf_op jit(solution)/shard_map/ppermute | solution.py:207
  74.3 1.6 %collective-permute-start.17 = (f32[2,128,256]{2,1,0:T(8,128)S(1)}, f32[2,128,256]{2,1,0:T(8,128)S(1)}, u32[]{:S(2)}, u32[]{:S(2)}) collective-permute-start(f32[2,128,256]{2,1,0:T(8,128)S(1)} %broadcast_select_fusion.3.refs_10_.refs_9_), channel_id=1, source_target_pairs={{0,2},{2,0},{4,6},{6,4},{8,10},{10,8},{12,14},{14,12},{1,3},{3,1},... | collective-permute-start | bytes 786440 | tf_op jit(solution)/shard_map/ppermute | solution.py:207
  77.1 1.6 %collective-permute-start.18 = (f32[2,128,256]{2,1,0:T(8,128)S(1)}, f32[2,128,256]{2,1,0:T(8,128)S(1)}, u32[]{:S(2)}, u32[]{:S(2)}) collective-permute-start(f32[2,128,256]{2,1,0:T(8,128)S(1)} %broadcast_select_fusion.2.refs_11_.refs_10_), channel_id=1, source_target_pairs={{0,2},{2,0},{4,6},{6,4},{8,10},{10,8},{12,14},{14,12},{1,3},{3,1},... | collective-permute-start | bytes 786440 | tf_op jit(solution)/shard_map/ppermute | solution.py:207
  78.7 2.0 %shard_map.49 = (bf16[1024,256]{1,0:T(8,128)(2,1)S(1)}, bf16[1024,256]{1,0:T(8,128)(2,1)S(1)}) custom-call(bf16[1024,1024]{1,0:T(8,128)(2,1)S(1)} %get-tuple-element.26.refs_0_, bf16[1024,1024]{1,0:T(8,128)(2,1)S(1)} %get-tuple-element.27.refs_1_, f32[128,1024]{1,0:T(8,128)S(1)} %collective-permute-done.1.refs_2_, f32[128,1024]{1,0:T(8,128)S(1)} %collective-permute-done.2.refs_3_), custom_call_target="tpu_custom_call" | custom-call | flops 1610612736 | bytes 5242880 | tf_op jit(solution)/shard_map/pallas_call | solution.py:119
  80.7 1.9 %shard_map.50 = (bf16[1024,256]{1,0:T(8,128)(2,1)S(1)}, bf16[1024,256]{1,0:T(8,128)(2,1)S(1)}) custom-call(bf16[1024,1024]{1,0:T(8,128)(2,1)S(1)} %get-tuple-element.26.refs_0_, bf16[1024,1024]{1,0:T(8,128)(2,1)S(1)} %get-tuple-element.27.refs_1_, f32[128,1024]{1,0:T(8,128)S(1)} %broadcast_select_fusion.1.refs_2_, f32[128,1024]{1,0:T(8,128)S(1)} %collective-permute-done.5.refs_3_), custom_call_target="tpu_custom_call" | custom-call | flops 1610612736 | bytes 5242880 | tf_op jit(solution)/shard_map/pallas_call | solution.py:119
  82.6 6.8 %collective-permute-done.8.refs_3_ = f32[128,1024]{1,0:T(8,128)S(1)} collective-permute-done((f32[128,1024]{1,0:T(8,128)S(1)}, f32[128,1024]{1,0:T(8,128)S(1)}, u32[]{:S(2)}, u32[]{:S(2)}) %collective-permute-start.8) | collective-permute-done | bytes 524320 | tf_op jit(solution)/shard_map/ppermute | solution.py:207
  89.4 1.9 %shard_map.51 = (bf16[1024,256]{1,0:T(8,128)(2,1)S(1)}, bf16[1024,256]{1,0:T(8,128)(2,1)S(1)}) custom-call(bf16[1024,1024]{1,0:T(8,128)(2,1)S(1)} %get-tuple-element.26.refs_0_, bf16[1024,1024]{1,0:T(8,128)(2,1)S(1)} %get-tuple-element.27.refs_1_, f32[128,1024]{1,0:T(8,128)S(1)} %broadcast_select_fusion.refs_2_, f32[128,1024]{1,0:T(8,128)S(1)} %collective-permute-done.8.refs_3_), custom_call_target="tpu_custom_call" | custom-call | flops 1610612736 | bytes 5242880 | tf_op jit(solution)/shard_map/pallas_call | solution.py:119
  91.4 0.8 collective-permute-done.18.refs_13_.refs_12_
  92.2 2.0 %shard_map.55 = f32[1024,128]{1,0:T(8,128)S(1)} custom-call(s32[5]{0:T(128)S(1)} %stack.33.refs_0_, bf16[1024,256]{1,0:T(8,128)(2,1)S(1)} %get-tuple-element.29.refs_2_.refs_1_, bf16[1024,256]{1,0:T(8,128)(2,1)S(1)} %get-tuple-element.30.refs_3_.refs_2_, bf16[1024,256]{1,0:T(8,128)(2,1)S(1)} %get-tuple-element.32.refs_4_.refs_3_, ...), custom_call_target="tpu_custom_call" | custom-call | flops 805306368 | bytes 4194304 | tf_op jit(solution)/shard_map/pallas_call | solution.py:165
  94.3 2.0 %shard_map.54 = f32[1024,128]{1,0:T(8,128)S(1)} custom-call(s32[5]{0:T(128)S(1)} %stack.35.refs_0_, f32[1024,256]{1,0:T(8,128)S(1)} %copy-done.1, bf16[1024,256]{1,0:T(8,128)(2,1)S(1)} %get-tuple-element.29.refs_2_.refs_1_, bf16[1024,256]{1,0:T(8,128)(2,1)S(1)} %get-tuple-element.30.refs_3_.refs_2_, bf16[1024,256]{1,0:T(8,128)(2,1)S(1)} %get-tuple-element.32.refs_4_.refs_3_, ...), custom_call_target="tpu_custom_call" | custom-call | flops 805306368 | bytes 4194304 | tf_op jit(solution)/shard_map/pallas_call | solution.py:165
  96.3 0.8 sub.7
  (37 shorter events, 3.6 us)
Async XLA Ops:
  0.2 9.2 %copy-start.2 = (f32[8,1,128,256]{3,2,1,0:T(8,128)S(1)}, f32[8,1,128,256]{3,2,1,0:T(8,128)}, u32[]{:S(2)}) copy-start(f32[8,1,128,256]{3,2,1,0:T(8,128)} %param.4) | copy-start | bytes 3145732
  2.6 15.0 %collective-permute-start.1 = (f32[128,1024]{1,0:T(8,128)S(1)}, f32[128,1024]{1,0:T(8,128)S(1)}, u32[]{:S(2)}, u32[]{:S(2)}) collective-permute-start(f32[128,1024]{1,0:T(8,128)S(1)} %shard_map.46.refs_2_), channel_id=1, source_target_pairs={{0,4},{2,6},{4,0},{6,2},{8,12},{10,14},{12,8},{14,10},{1,5},{3,7},... | collective-permute-start | bytes 1572872 | tf_op jit(solution)/shard_map/ppermute | solution.py:207
  5.7 25.5 %collective-permute-start.3 = (f32[128,1024]{1,0:T(8,128)S(1)}, f32[128,1024]{1,0:T(8,128)S(1)}, u32[]{:S(2)}, u32[]{:S(2)}) collective-permute-start(f32[128,1024]{1,0:T(8,128)S(1)} %shard_map.46.refs_2_), channel_id=1, source_target_pairs={{4,8},{6,10},{8,4},{10,6},{5,9},{7,11},{9,5},{11,7},{20,24},{22,26... | collective-permute-start | bytes 1572872 | tf_op jit(solution)/shard_map/ppermute | solution.py:207
  9.4 26.4 %copy-start = (f32[1024,1024]{1,0:T(8,128)S(1)}, f32[1024,1024]{1,0:T(8,128)}, u32[]{:S(2)}) copy-start(f32[1024,1024]{1,0:T(8,128)} %x_ref.1) | copy-start | bytes 12582916
  10.0 9.2 %collective-permute-start.9 = (f32[2,128,256]{2,1,0:T(8,128)S(1)}, f32[2,128,256]{2,1,0:T(8,128)S(1)}, u32[]{:S(2)}, u32[]{:S(2)}) collective-permute-start(f32[2,128,256]{2,1,0:T(8,128)S(1)} %get-tuple-element.41), channel_id=1, source_target_pairs={{0,2},{2,0},{4,6},{6,4},{8,10},{10,8},{12,14},{14,12},{1,3},{3,1},... | collective-permute-start | bytes 786440 | tf_op jit(solution)/shard_map/ppermute | solution.py:207
  11.6 14.0 %collective-permute-start.13 = (f32[2,128,256]{2,1,0:T(8,128)S(1)}, f32[2,128,256]{2,1,0:T(8,128)S(1)}, u32[]{:S(2)}, u32[]{:S(2)}) collective-permute-start(f32[2,128,256]{2,1,0:T(8,128)S(1)} %get-tuple-element.43), channel_id=1, source_target_pairs={{0,2},{2,0},{4,6},{6,4},{8,10},{10,8},{12,14},{14,12},{1,3},{3,1},... | collective-permute-start | bytes 786440 | tf_op jit(solution)/shard_map/ppermute | solution.py:207
  12.1 24.3 %collective-permute-start = (f32[128,1024]{1,0:T(8,128)S(1)}, f32[128,1024]{1,0:T(8,128)S(1)}, u32[]{:S(2)}, u32[]{:S(2)}) collective-permute-start(f32[128,1024]{1,0:T(8,128)S(1)} %shard_map.46.refs_2_), channel_id=1, source_target_pairs={{0,2},{2,0},{4,6},{6,4},{8,10},{10,8},{12,14},{14,12},{1,3},{3,1},... | collective-permute-start | bytes 1572872 | tf_op jit(solution)/shard_map/ppermute | solution.py:207
  17.7 24.2 %collective-permute-start.6 = (f32[128,1024]{1,0:T(8,128)S(1)}, f32[128,1024]{1,0:T(8,128)S(1)}, u32[]{:S(2)}, u32[]{:S(2)}) collective-permute-start(f32[128,1024]{1,0:T(8,128)S(1)} %collective-permute-done.1.refs_2_), channel_id=1, source_target_pairs={{4,8},{6,10},{8,4},{10,6},{5,9},{7,11},{9,5},{11,7},{20,24},{22,26... | collective-permute-start | bytes 1572872 | tf_op jit(solution)/shard_map/ppermute | solution.py:207
  19.3 13.2 %collective-permute-start.10 = (f32[2,128,256]{2,1,0:T(8,128)S(1)}, f32[2,128,256]{2,1,0:T(8,128)S(1)}, u32[]{:S(2)}, u32[]{:S(2)}) collective-permute-start(f32[2,128,256]{2,1,0:T(8,128)S(1)} %add.18), channel_id=1, source_target_pairs={{0,4},{2,6},{12,8},{14,10},{1,5},{3,7},{13,9},{15,11},{16,20},{18,... | collective-permute-start | bytes 786440 | tf_op jit(solution)/shard_map/ppermute | solution.py:207
  25.6 9.4 %collective-permute-start.14 = (f32[2,128,256]{2,1,0:T(8,128)S(1)}, f32[2,128,256]{2,1,0:T(8,128)S(1)}, u32[]{:S(2)}, u32[]{:S(2)}) collective-permute-start(f32[2,128,256]{2,1,0:T(8,128)S(1)} %add.21), channel_id=1, source_target_pairs={{0,4},{2,6},{12,8},{14,10},{1,5},{3,7},{13,9},{15,11},{16,20},{18,... | collective-permute-start | bytes 786440 | tf_op jit(solution)/shard_map/ppermute | solution.py:207
  31.2 16.7 %collective-permute-start.4 = (f32[128,1024]{1,0:T(8,128)S(1)}, f32[128,1024]{1,0:T(8,128)S(1)}, u32[]{:S(2)}, u32[]{:S(2)}) collective-permute-start(f32[128,1024]{1,0:T(8,128)S(1)} %collective-permute-done.3), channel_id=1, source_target_pairs={{4,0},{6,2},{8,12},{10,14},{5,1},{7,3},{9,13},{11,15},{20,16},{22,... | collective-permute-start | bytes 1572872 | tf_op jit(solution)/shard_map/ppermute | solution.py:207
  32.6 12.5 %collective-permute-start.11 = (f32[2,128,256]{2,1,0:T(8,128)S(1)}, f32[2,128,256]{2,1,0:T(8,128)S(1)}, u32[]{:S(2)}, u32[]{:S(2)}) collective-permute-start(f32[2,128,256]{2,1,0:T(8,128)S(1)} %add.19), channel_id=1, source_target_pairs={{4,8},{6,10},{8,4},{10,6},{5,9},{7,11},{9,5},{11,7},{20,24},{22,26... | collective-permute-start | bytes 786440 | tf_op jit(solution)/shard_map/ppermute | solution.py:207
  35.1 11.3 %collective-permute-start.15 = (f32[2,128,256]{2,1,0:T(8,128)S(1)}, f32[2,128,256]{2,1,0:T(8,128)S(1)}, u32[]{:S(2)}, u32[]{:S(2)}) collective-permute-start(f32[2,128,256]{2,1,0:T(8,128)S(1)} %add.22), channel_id=1, source_target_pairs={{4,8},{6,10},{8,4},{10,6},{5,9},{7,11},{9,5},{11,7},{20,24},{22,26... | collective-permute-start | bytes 786440 | tf_op jit(solution)/shard_map/ppermute | solution.py:207
  36.4 42.3 %collective-permute-start.2 = (f32[128,1024]{1,0:T(8,128)S(1)}, f32[128,1024]{1,0:T(8,128)S(1)}, u32[]{:S(2)}, u32[]{:S(2)}) collective-permute-start(f32[128,1024]{1,0:T(8,128)S(1)} %collective-permute-done.refs_3_), channel_id=1, source_target_pairs={{0,4},{2,6},{4,0},{6,2},{8,12},{10,14},{12,8},{14,10},{1,5},{3,7},... | collective-permute-start | bytes 1572872 | tf_op jit(solution)/shard_map/ppermute | solution.py:207
  41.9 34.0 %collective-permute-start.7 = (f32[128,1024]{1,0:T(8,128)S(1)}, f32[128,1024]{1,0:T(8,128)S(1)}, u32[]{:S(2)}, u32[]{:S(2)}) collective-permute-start(f32[128,1024]{1,0:T(8,128)S(1)} %collective-permute-done.6), channel_id=1, source_target_pairs={{4,0},{6,2},{8,12},{10,14},{5,1},{7,3},{9,13},{11,15},{20,16},{22,... | collective-permute-start | bytes 1572872 | tf_op jit(solution)/shard_map/ppermute | solution.py:207
  45.1 29.1 %collective-permute-start.12 = (f32[2,128,256]{2,1,0:T(8,128)S(1)}, f32[2,128,256]{2,1,0:T(8,128)S(1)}, u32[]{:S(2)}, u32[]{:S(2)}) collective-permute-start(f32[2,128,256]{2,1,0:T(8,128)S(1)} %add.20), channel_id=1, source_target_pairs={{4,0},{6,2},{8,12},{10,14},{5,1},{7,3},{9,13},{11,15},{20,16},{22,... | collective-permute-start | bytes 786440 | tf_op jit(solution)/shard_map/ppermute | solution.py:207
  46.5 30.6 %collective-permute-start.16 = (f32[2,128,256]{2,1,0:T(8,128)S(1)}, f32[2,128,256]{2,1,0:T(8,128)S(1)}, u32[]{:S(2)}, u32[]{:S(2)}) collective-permute-start(f32[2,128,256]{2,1,0:T(8,128)S(1)} %add.23), channel_id=1, source_target_pairs={{4,0},{6,2},{8,12},{10,14},{5,1},{7,3},{9,13},{11,15},{20,16},{22,... | collective-permute-start | bytes 786440 | tf_op jit(solution)/shard_map/ppermute | solution.py:207
  48.0 32.7 %collective-permute-start.5 = (f32[128,1024]{1,0:T(8,128)S(1)}, f32[128,1024]{1,0:T(8,128)S(1)}, u32[]{:S(2)}, u32[]{:S(2)}) collective-permute-start(f32[128,1024]{1,0:T(8,128)S(1)} %broadcast_select_fusion.1.refs_2_), channel_id=1, source_target_pairs={{0,2},{2,0},{4,6},{6,4},{8,10},{10,8},{12,14},{14,12},{1,3},{3,1},... | collective-permute-start | bytes 1572872 | tf_op jit(solution)/shard_map/ppermute | solution.py:207
  74.3 17.1 %collective-permute-start.17 = (f32[2,128,256]{2,1,0:T(8,128)S(1)}, f32[2,128,256]{2,1,0:T(8,128)S(1)}, u32[]{:S(2)}, u32[]{:S(2)}) collective-permute-start(f32[2,128,256]{2,1,0:T(8,128)S(1)} %broadcast_select_fusion.3.refs_10_.refs_9_), channel_id=1, source_target_pairs={{0,2},{2,0},{4,6},{6,4},{8,10},{10,8},{12,14},{14,12},{1,3},{3,1},... | collective-permute-start | bytes 786440 | tf_op jit(solution)/shard_map/ppermute | solution.py:207
  76.0 13.4 %collective-permute-start.8 = (f32[128,1024]{1,0:T(8,128)S(1)}, f32[128,1024]{1,0:T(8,128)S(1)}, u32[]{:S(2)}, u32[]{:S(2)}) collective-permute-start(f32[128,1024]{1,0:T(8,128)S(1)} %broadcast_select_fusion.refs_2_), channel_id=1, source_target_pairs={{0,2},{2,0},{4,6},{6,4},{8,10},{10,8},{12,14},{14,12},{1,3},{3,1},... | collective-permute-start | bytes 1572872 | tf_op jit(solution)/shard_map/ppermute | solution.py:207
  77.1 15.1 %collective-permute-start.18 = (f32[2,128,256]{2,1,0:T(8,128)S(1)}, f32[2,128,256]{2,1,0:T(8,128)S(1)}, u32[]{:S(2)}, u32[]{:S(2)}) collective-permute-start(f32[2,128,256]{2,1,0:T(8,128)S(1)} %broadcast_select_fusion.2.refs_11_.refs_10_), channel_id=1, source_target_pairs={{0,2},{2,0},{4,6},{6,4},{8,10},{10,8},{12,14},{14,12},{1,3},{3,1},... | collective-permute-start | bytes 786440 | tf_op jit(solution)/shard_map/ppermute | solution.py:207
  92.2 2.1 %copy-start.1 = (f32[1024,256]{1,0:T(8,128)S(1)}, f32[1024,256]{1,0:T(8,128)}, u32[]{:S(2)}) copy-start(f32[1024,256]{1,0:T(8,128)} %refs_1_.5) | copy-start | bytes 3145732
  94.2 2.1 %collective-permute-start.19 = (f32[1024,128]{1,0:T(8,128)S(1)}, f32[1024,128]{1,0:T(8,128)S(1)}, u32[]{:S(2)}, u32[]{:S(2)}) collective-permute-start(f32[1024,128]{1,0:T(8,128)S(1)} %shard_map.55), channel_id=1, source_target_pairs={{0,1},{1,0},{2,3},{3,2},{4,5},{5,4},{6,7},{7,6},{8,9},{9,8},{10,11... | collective-permute-start | bytes 1572872 | tf_op jit(solution)/shard_map/ppermute | solution.py:275

commit v5 on v4

--- a/solution.py
+++ b/solution.py
@@ -129,50 +129,84 @@
     )(*in_vmem(x_high, x_low), near, far)
 
 
-def apply_kernel(slots, runs, tile, table_ref, *refs):
-    base_ref = None
-    if len(refs) > 2 * slots + 2 * runs + 2:
-        base_ref, refs = refs[0], refs[1:]
-    highs, lows = refs[:slots], refs[slots:2 * slots]
-    same_refs, cross_refs = refs[2 * slots:2 * slots + runs], refs[2 * slots + runs:2 * slots + 2 * runs]
-    out_ref, c_ref = refs[2 * slots + 2 * runs:]
-    each, half = same_refs[0].shape[:2]
-    rhs = out_ref.shape[1]
-    cols = pl.ds(pl.multiple_of(table_ref[slots] * rhs, rhs), rhs)
-    for j in range(slots):
-        place = table_ref[j]
-        for i, run_refs in enumerate((same_refs, cross_refs)):
-            rows = pl.ds((2 * j + i) * half, half)
-            for r, ref in enumerate(run_refs):
-
-                @pl.when((place >= r * each) & (place < (r + 1) * each))
-                def _():
-                    c_ref[rows, :rhs], c_ref[rows, rhs:] = halves(ref[place - r * each, :, cols])
-
-    for r in range(0, out_ref.shape[0], tile):
+def fill(c_ref, row, ref, place, cols):
+    half, rhs = ref.shape[1], c_ref.shape[1] // 2 // len(cols)
+    rows = pl.ds(row, half)
+    for i, col in enumerate(cols):
+        span = pl.ds(pl.multiple_of(col * rhs, rhs), rhs)
+        high, low = halves(ref[place, :, span])
+        c_ref[rows, i * rhs:(i + 1) * rhs] = high
+        c_ref[rows, (len(cols) + i) * rhs:(len(cols) + i + 1) * rhs] = low
+
+
+def product(kerns, slots, places, run_refs, cols, c_ref, tile, store):
+    each, half = run_refs[0].shape[:2]
+    for i, slot in enumerate(slots):
+        place = places[slot]
+        for r, ref in enumerate(run_refs):
+
+            @pl.when((place >= r * each) & (place < (r + 1) * each))
+            def _():
+                fill(c_ref, i * half, ref, place - r * each, cols)
+
+    width = c_ref.shape[1] // 2
+    for r in range(0, kerns[0].shape[0], tile):
         span = slice(r, r + tile)
-        high = jnp.concatenate([ref[span] for ref in highs], 1)
-        low = jnp.concatenate([ref[span] for ref in lows], 1)
+        high = jnp.concatenate([ref[span] for ref in kerns[::2]], 1)
+        low = jnp.concatenate([ref[span] for ref in kerns[1::2]], 1)
         both = mm(high, c_ref[...], NN)
-        total = both[:, :rhs] + (both[:, rhs:] + mm(low, c_ref[:, :rhs], NN))
-        out_ref[span] = total if base_ref is None else base_ref[span, cols] - total
-
-
-def apply(kerns, sames, crosses, table, parts, base=(), tile=512):
-    slots, runs = len(kerns), len(sames)
-    rows, points = kerns[0][0].shape
-    rhs = sames[0].shape[2] // parts
+        store(span, both[:, :width] + (both[:, width:] + mm(low, c_ref[:, :width], NN)))
+
+
+def call(kernel, kerns, runs, others, table, outs, scratch, cost):
     return pl.pallas_call(
-        lambda *refs: apply_kernel(slots, runs, tile, *refs),
-        in_specs=[pl.BlockSpec(memory_space=pltpu.SMEM)] + [VMEM] * (len(base) + 2 * slots + 2 * runs),
-        out_specs=VMEM,
-        scratch_shapes=[pltpu.VMEM((slots * points, 2 * rhs), BF16)],
-        out_shape=jax.ShapeDtypeStruct((rows, rhs), F32),
-        compiler_params=PARAMS,
-        cost_estimate=pl.CostEstimate(
-            flops=6 * rows * slots * points * rhs, bytes_accessed=4 * rows * slots * points, transcendentals=0
-        ),
-    )(table, *base, *in_vmem(*[k[0] for k in kerns], *[k[1] for k in kerns]), *sames, *crosses)
+        kernel,
+        in_specs=[pl.BlockSpec(memory_space=pltpu.SMEM)] + [VMEM] * (len(kerns) + len(runs) + len(others)),
+        out_specs=[VMEM] * outs[0],
+        out_shape=[pltpu.VMEM(outs[1], F32)] * outs[0],
+        scratch_shapes=[pltpu.VMEM(scratch, BF16)],
+        compiler_params=PARAMS,
+        cost_estimate=pl.CostEstimate(flops=cost, bytes_accessed=cost // 1024, transcendentals=0),
+    )(table, *in_vmem(*kerns), *runs, *in_vmem(*others))
+
+
+def apply_near(kerns, slots, runs, table, residual, parts, tile=512):
+    rows, count = kerns[0].shape[0], len(kerns)
+    half, rhs = runs[0].shape[1], runs[0].shape[2] // parts
+
+    def kernel(table_ref, *refs):
+        base_ref, theirs_ref, mine_ref, c_ref = refs[count + len(runs):]
+        col = table_ref[len(slots)]
+        span = pl.ds(pl.multiple_of(col * rhs, rhs), rhs)
+
+        def store(at, value):
+            theirs_ref[at] = value[:, :rhs]
+            mine_ref[at] = base_ref[at, span] - value[:, rhs:]
+
+        product(refs[:count], slots, table_ref, refs[count:count + len(runs)], (parts - 1 - col, col), c_ref, tile, store)
+
+    scratch = (len(slots) * half, 4 * rhs)
+    return call(
+        kernel, kerns, runs, [residual], table, (2, (rows, rhs)), scratch, 6 * rows * scratch[0] * 2 * rhs
+    )
+
+
+def apply_far(kerns, slots, runs, table, base, mine, parts, tile=512):
+    rows, count = kerns[0].shape[0], len(kerns)
+    half, rhs = runs[0].shape[1], runs[0].shape[2] // parts
+
+    def kernel(table_ref, *refs):
+        base_ref, out_ref, c_ref = refs[count + len(runs):]
+        col = table_ref[len(slots)]
+
+        def store(at, value):
+            out_ref[at] = base_ref[at] - value if mine else base_ref[at] + value
+
+        cols = (col if mine else parts - 1 - col,)
+        product(refs[:count], slots, table_ref, refs[count:count + len(runs)], cols, c_ref, tile, store)
+
+    scratch = (len(slots) * half, 2 * rhs)
+    return call(kernel, kerns, runs, [base], table, (1, (rows, rhs)), scratch, 6 * rows * scratch[0] * rhs)[0]
 
 
 def moves(depth):
@@ -222,7 +256,6 @@
     own = gather(features, block_ids, half)
     steps, slots = moves(depth)
 
-    other = cols - 1 - col
     places, masks = [z], []
     for j in range(depth - 1):
         by_name, place = {}, jnp.int32(0)
@@ -232,8 +265,8 @@
         places.append(place)
         masks.append({name: any_of(z, zs) for name, zs in list(by_name.items())})
     ends = [(z == i) | (z == depth - 1 - i) for i in range(depth // 2 - 1)]
-    tables = [jnp.stack(places + [c]).astype(jnp.int32) for c in (other, col)]
-    own, masks, ends, tables = lax.optimization_barrier((own, masks, ends, tables))
+    table = jnp.stack(places + [col]).astype(jnp.int32)
+    own, masks, ends, table = lax.optimization_barrier((own, masks, ends, table))
 
     bufs = {"own": own}
     for name, pairs, source in steps:
@@ -257,23 +290,29 @@
         crosses.append(permute(term, across))
 
     x_high, x_low = split(features)
-    kerns, fars = [], []
+    nears, fars = [], []
     for j in range(depth):
         block = own
         if j > 0:
             block = None
             for name, mask in masks[j - 1].items():
                 block = bufs[name] if block is None else jnp.where(mask, bufs[name], block)
+        nears.append(block)
         if j == 1 and depth == 4:
-            far = permute(fars[0], along(steps[0][1]))
+            fars.append(permute(fars[0], along(steps[0][1])))
         else:
-            far = permute(block, across)
-        fars.append(far)
-        kerns.append(gram(x_high, x_low, block, far))
-
-    theirs = apply(kerns, sames, crosses, tables[0], cols)
+            fars.append(permute(block, across))
+    near_slots = list(range(depth))
+    far_slots = [0, 2, 1, 3] if depth == 4 else near_slots
+    near_kerns, far_kerns = [], []
+    for i in range(0, depth, 2):
+        near_kerns += gram(x_high, x_low, *[nears[j] for j in near_slots[i:i + 2]])
+        far_kerns += gram(x_high, x_low, *[fars[j] for j in far_slots[i:i + 2]])
+
+    theirs, mine = apply_near(near_kerns, near_slots, sames, table, residual, cols)
+    theirs = apply_far(far_kerns, far_slots, crosses, table, theirs, False, cols)
     got = lax.ppermute(theirs, "col", [(c, cols - 1 - c) for c in range(cols)])
-    mine = apply(kerns, sames, crosses, tables[1], cols, (residual,))
+    mine = apply_far(far_kerns, far_slots, crosses, table, mine, True, cols)
     return mine - got
 
 

time: 97.5 us -> 93.8 us (0.962)
  waiting for transfers between devices: 39.8 us -> 36.1 us
    ppermute x19, waiting for transfers between devices: 39.8 us -> 35.5 us  [permute(): return lax.ppermute(x, 'row', pairs)]
    pallas_call x2 -> x3, Pallas kernels: 3.97 us -> 4.38 us  [call(): pl.pallas_call(kernel, in_specs=[pl.BlockSpec(memory_space=pltpu.SMEM)] +...]
  transfers between devices with their start and end apart: 20 -> 20, of which waited for: 8 -> 9; matrix products, arithmetic and copies ran while one was open for 0% -> 0% of each run, Pallas kernels for 14% -> 16%
where the time goes in v5:
time: 93.8 us; the launch traced here: 93.5 us
  starting transfers between devices  37.1 us (40%)
  waiting for transfers between devices  36.1 us (38%)
  Pallas kernels  18.7 us (20%)
  other arithmetic  1.25 us (1%)
    ppermute x19, starting transfers between devices, permute(): return lax.ppermute(x, 'row', pairs)  37 us
    ppermute x19, waiting for transfers between devices, permute(): return lax.ppermute(x, 'row', pairs)  35.5 us
    pallas_call x4, Pallas kernels, gram(): pl.pallas_call(lambda *refs: gram_kernel(1.0 / feats, tile, *refs), in_sp...  7.69 us
    pallas_call x2, Pallas kernels, gather(): pl.pallas_call(lambda *refs: gather_kernel(count == ids.shape[0], *refs),...  5.39 us
    pallas_call x3, Pallas kernels, call(): pl.pallas_call(kernel, in_specs=[pl.BlockSpec(memory_space=pltpu.SMEM)] +...  4.38 us
  transfers between devices with their start and end apart: 20, of which 9 were waited for; matrix products, arithmetic and copies ran while one was open for 0% of the time, Pallas kernels for 16%

profile of v5, /device:TPU:0, one launch (start us, length us, event | category | flops | bytes accessed | tf_op | source)
XLA Modules:
  0.0 93.5 jit_solution(6462843927471517255)
XLA Ops:
  0.0 2.4 %shard_map.46.refs_2_ = f32[128,1024]{1,0:T(8,128)S(1)} custom-call(s32[256]{0:T(256)} %refs_0_.3, f32[1024,1024]{1,0:T(8,128)} %x_ref.1), custom_call_target="tpu_custom_call" | custom-call | bytes 1048576 | tf_op jit(solution)/shard_map/pallas_call | solution.py:66
  2.5 3.1 %collective-permute-start.5 = (f32[128,1024]{1,0:T(8,128)S(1)}, f32[128,1024]{1,0:T(8,128)S(1)}, u32[]{:S(2)}, u32[]{:S(2)}) collective-permute-start(f32[128,1024]{1,0:T(8,128)S(1)} %shard_map.46.refs_2_), channel_id=1, source_target_pairs={{0,4},{2,6},{4,0},{6,2},{8,12},{10,14},{12,8},{14,10},{1,5},{3,7},... | collective-permute-start | bytes 1572872 | tf_op jit(solution)/shard_map/ppermute | solution.py:241
  5.6 3.0 %shard_map.50.refs_1_ = f32[256,256]{1,0:T(8,128)S(1)} custom-call(s32[256]{0:T(256)} %refs_0_.3, f32[1024,256]{1,0:T(8,128)} %refs_6_.1), custom_call_target="tpu_custom_call" | custom-call | bytes 524288 | tf_op jit(solution)/shard_map/pallas_call | solution.py:66
  9.2 1.6 %collective-permute-start.14 = (f32[2,128,256]{2,1,0:T(8,128)S(1)}, f32[2,128,256]{2,1,0:T(8,128)S(1)}, u32[]{:S(2)}, u32[]{:S(2)}) collective-permute-start(f32[2,128,256]{2,1,0:T(8,128)S(1)} %get-tuple-element.40), channel_id=1, source_target_pairs={{0,2},{2,0},{4,6},{6,4},{8,10},{10,8},{12,14},{14,12},{1,3},{3,1},... | collective-permute-start | bytes 786440 | tf_op jit(solution)/shard_map/ppermute | solution.py:241
  11.4 0.7 collective-permute-start.9
  12.1 6.3 %collective-permute-done.14 = f32[2,128,256]{2,1,0:T(8,128)S(1)} collective-permute-done((f32[2,128,256]{2,1,0:T(8,128)S(1)}, f32[2,128,256]{2,1,0:T(8,128)S(1)}, u32[]{:S(2)}, u32[]{:S(2)}) %collective-permute-start.14) | collective-permute-done | bytes 262176 | tf_op jit(solution)/shard_map/ppermute | solution.py:241
  18.4 1.3 %collective-permute-start.15 = (f32[2,128,256]{2,1,0:T(8,128)S(1)}, f32[2,128,256]{2,1,0:T(8,128)S(1)}, u32[]{:S(2)}, u32[]{:S(2)}) collective-permute-start(f32[2,128,256]{2,1,0:T(8,128)S(1)} %add.21), channel_id=1, source_target_pairs={{0,4},{2,6},{12,8},{14,10},{1,5},{3,7},{13,9},{15,11},{16,20},{18,... | collective-permute-start | bytes 786440 | tf_op jit(solution)/shard_map/ppermute | solution.py:241
  19.8 2.1 %collective-permute-start = (f32[128,1024]{1,0:T(8,128)S(1)}, f32[128,1024]{1,0:T(8,128)S(1)}, u32[]{:S(2)}, u32[]{:S(2)}) collective-permute-start(f32[128,1024]{1,0:T(8,128)S(1)} %shard_map.46.refs_2_), channel_id=1, source_target_pairs={{0,2},{2,0},{4,6},{6,4},{8,10},{10,8},{12,14},{14,12},{1,3},{3,1},... | collective-permute-start | bytes 1572872 | tf_op jit(solution)/shard_map/ppermute | solution.py:241
  22.5 1.5 %collective-permute-done.9 = f32[2,128,256]{2,1,0:T(8,128)S(1)} collective-permute-done((f32[2,128,256]{2,1,0:T(8,128)S(1)}, f32[2,128,256]{2,1,0:T(8,128)S(1)}, u32[]{:S(2)}, u32[]{:S(2)}) %collective-permute-start.9) | collective-permute-done | bytes 262176 | tf_op jit(solution)/shard_map/ppermute | solution.py:241
  24.1 4.3 %collective-permute-start.10 = (f32[2,128,256]{2,1,0:T(8,128)S(1)}, f32[2,128,256]{2,1,0:T(8,128)S(1)}, u32[]{:S(2)}, u32[]{:S(2)}) collective-permute-start(f32[2,128,256]{2,1,0:T(8,128)S(1)} %add.18), channel_id=1, source_target_pairs={{0,4},{2,6},{12,8},{14,10},{1,5},{3,7},{13,9},{15,11},{16,20},{18,... | collective-permute-start | bytes 786440 | tf_op jit(solution)/shard_map/ppermute | solution.py:241
  29.1 1.3 %collective-permute-start.2 = (f32[128,1024]{1,0:T(8,128)S(1)}, f32[128,1024]{1,0:T(8,128)S(1)}, u32[]{:S(2)}, u32[]{:S(2)}) collective-permute-start(f32[128,1024]{1,0:T(8,128)S(1)} %collective-permute-done.1), channel_id=1, source_target_pairs={{4,0},{6,2},{8,12},{10,14},{5,1},{7,3},{9,13},{11,15},{20,16},{22,... | collective-permute-start | bytes 1572872 | tf_op jit(solution)/shard_map/ppermute | solution.py:241
  30.4 1.8 %collective-permute-done.10 = f32[2,128,256]{2,1,0:T(8,128)S(1)} collective-permute-done((f32[2,128,256]{2,1,0:T(8,128)S(1)}, f32[2,128,256]{2,1,0:T(8,128)S(1)}, u32[]{:S(2)}, u32[]{:S(2)}) %collective-permute-start.10) | collective-permute-done | bytes 262176 | tf_op jit(solution)/shard_map/ppermute | solution.py:241
  33.0 1.3 %collective-permute-start.17 = (f32[2,128,256]{2,1,0:T(8,128)S(1)}, f32[2,128,256]{2,1,0:T(8,128)S(1)}, u32[]{:S(2)}, u32[]{:S(2)}) collective-permute-start(f32[2,128,256]{2,1,0:T(8,128)S(1)} %add.23), channel_id=1, source_target_pairs={{4,0},{6,2},{8,12},{10,14},{5,1},{7,3},{9,13},{11,15},{20,16},{22,... | collective-permute-start | bytes 786440 | tf_op jit(solution)/shard_map/ppermute | solution.py:241
  35.0 12.5 %collective-permute-start.4 = (f32[128,1024]{1,0:T(8,128)S(1)}, f32[128,1024]{1,0:T(8,128)S(1)}, u32[]{:S(2)}, u32[]{:S(2)}) collective-permute-start(f32[128,1024]{1,0:T(8,128)S(1)} %collective-permute-done.refs_2_), channel_id=1, source_target_pairs={{0,4},{2,6},{4,0},{6,2},{8,12},{10,14},{12,8},{14,10},{1,5},{3,7},... | collective-permute-start | bytes 1572872 | tf_op jit(solution)/shard_map/ppermute | solution.py:241
  47.5 1.3 %collective-permute-start.7 = (f32[128,1024]{1,0:T(8,128)S(1)}, f32[128,1024]{1,0:T(8,128)S(1)}, u32[]{:S(2)}, u32[]{:S(2)}) collective-permute-start(f32[128,1024]{1,0:T(8,128)S(1)} %collective-permute-done.6), channel_id=1, source_target_pairs={{4,0},{6,2},{8,12},{10,14},{5,1},{7,3},{9,13},{11,15},{20,16},{22,... | collective-permute-start | bytes 1572872 | tf_op jit(solution)/shard_map/ppermute | solution.py:241
  48.8 1.9 %shard_map.52 = (bf16[1024,256]{1,0:T(8,128)(2,1)S(1)}, bf16[1024,256]{1,0:T(8,128)(2,1)S(1)}) custom-call(bf16[1024,1024]{1,0:T(8,128)(2,1)S(1)} %get-tuple-element.27.refs_0_, bf16[1024,1024]{1,0:T(8,128)(2,1)S(1)} %get-tuple-element.28.refs_1_, f32[128,1024]{1,0:T(8,128)S(1)} %shard_map.46.refs_2_, f32[128,1024]{1,0:T(8,128)S(1)} %collective-permute-done.5.refs_3_), custom_call_target="tpu_custom_call" | custom-call | flops 1610612736 | bytes 5242880 | tf_op jit(solution)/shard_map/pallas_call | solution.py:119
  50.8 1.3 %collective-permute-start.12 = (f32[2,128,256]{2,1,0:T(8,128)S(1)}, f32[2,128,256]{2,1,0:T(8,128)S(1)}, u32[]{:S(2)}, u32[]{:S(2)}) collective-permute-start(f32[2,128,256]{2,1,0:T(8,128)S(1)} %add.20), channel_id=1, source_target_pairs={{4,0},{6,2},{8,12},{10,14},{5,1},{7,3},{9,13},{11,15},{20,16},{22,... | collective-permute-start | bytes 786440 | tf_op jit(solution)/shard_map/ppermute | solution.py:241
  52.1 1.8 %collective-permute-done.17 = f32[2,128,256]{2,1,0:T(8,128)S(1)} collective-permute-done((f32[2,128,256]{2,1,0:T(8,128)S(1)}, f32[2,128,256]{2,1,0:T(8,128)S(1)}, u32[]{:S(2)}, u32[]{:S(2)}) %collective-permute-start.17) | collective-permute-done | bytes 262176 | tf_op jit(solution)/shard_map/ppermute | solution.py:241
  53.9 0.7 collective-permute-start.18
  54.7 1.5 %collective-permute-start.3 = (f32[128,1024]{1,0:T(8,128)S(1)}, f32[128,1024]{1,0:T(8,128)S(1)}, u32[]{:S(2)}, u32[]{:S(2)}) collective-permute-start(f32[128,1024]{1,0:T(8,128)S(1)} %broadcast_select_fusion.1.refs_2_), channel_id=1, source_target_pairs={{0,2},{2,0},{4,6},{6,4},{8,10},{10,8},{12,14},{14,12},{1,3},{3,1},... | collective-permute-start | bytes 1572872 | tf_op jit(solution)/shard_map/ppermute | solution.py:241
  56.2 19.6 %collective-permute-done.7 = f32[128,1024]{1,0:T(8,128)S(1)} collective-permute-done((f32[128,1024]{1,0:T(8,128)S(1)}, f32[128,1024]{1,0:T(8,128)S(1)}, u32[]{:S(2)}, u32[]{:S(2)}) %collective-permute-start.7) | collective-permute-done | bytes 524320 | tf_op jit(solution)/shard_map/ppermute | solution.py:241
  76.5 2.0 %collective-permute-done.12 = f32[2,128,256]{2,1,0:T(8,128)S(1)} collective-permute-done((f32[2,128,256]{2,1,0:T(8,128)S(1)}, f32[2,128,256]{2,1,0:T(8,128)S(1)}, u32[]{:S(2)}, u32[]{:S(2)}) %collective-permute-start.12) | collective-permute-done | bytes 262176 | tf_op jit(solution)/shard_map/ppermute | solution.py:241
  78.6 0.7 collective-permute-start.13
  79.3 1.9 %shard_map.53 = (bf16[1024,256]{1,0:T(8,128)(2,1)S(1)}, bf16[1024,256]{1,0:T(8,128)(2,1)S(1)}) custom-call(bf16[1024,1024]{1,0:T(8,128)(2,1)S(1)} %get-tuple-element.27.refs_0_, bf16[1024,1024]{1,0:T(8,128)(2,1)S(1)} %get-tuple-element.28.refs_1_, f32[128,1024]{1,0:T(8,128)S(1)} %broadcast_select_fusion.1.refs_2_, f32[128,1024]{1,0:T(8,128)S(1)} %broadcast_select_fusion.refs_3_), custom_call_target="tpu_custom_call" | custom-call | flops 1610612736 | bytes 5242880 | tf_op jit(solution)/shard_map/pallas_call | solution.py:119
  81.3 1.9 %shard_map.48 = (bf16[1024,256]{1,0:T(8,128)(2,1)S(1)}, bf16[1024,256]{1,0:T(8,128)(2,1)S(1)}) custom-call(bf16[1024,1024]{1,0:T(8,128)(2,1)S(1)} %get-tuple-element.27.refs_0_, bf16[1024,1024]{1,0:T(8,128)(2,1)S(1)} %get-tuple-element.28.refs_1_, f32[128,1024]{1,0:T(8,128)S(1)} %collective-permute-done.refs_2_, f32[128,1024]{1,0:T(8,128)S(1)} %collective-permute-done.3.refs_3_), custom_call_target="tpu_custom_call" | custom-call | flops 1610612736 | bytes 5242880 | tf_op jit(solution)/shard_map/pallas_call | solution.py:119
  83.2 1.7 %shard_map.54 = (f32[1024,128]{1,0:T(8,128)S(1)}, f32[1024,128]{1,0:T(8,128)S(1)}) custom-call(s32[5]{0:T(128)S(1)} %stack.23.table_ref, bf16[1024,256]{1,0:T(8,128)(2,1)S(1)} %get-tuple-element.41.refs_0_, bf16[1024,256]{1,0:T(8,128)(2,1)S(1)} %get-tuple-element.42.refs_1_, bf16[1024,256]{1,0:T(8,128)(2,1)S(1)} %get-tuple-element.43.refs_2_, ...), custom_call_target="tpu_custom_call" | custom-call | flops 805306368 | bytes 786432 | tf_op jit(solution)/shard_map/pallas_call | solution.py:162
  84.9 1.6 %collective-permute-done.8.refs_3_ = f32[128,1024]{1,0:T(8,128)S(1)} collective-permute-done((f32[128,1024]{1,0:T(8,128)S(1)}, f32[128,1024]{1,0:T(8,128)S(1)}, u32[]{:S(2)}, u32[]{:S(2)}) %collective-permute-start.8) | collective-permute-done | bytes 524320 | tf_op jit(solution)/shard_map/ppermute | solution.py:241
  86.5 1.9 %shard_map.49 = (bf16[1024,256]{1,0:T(8,128)(2,1)S(1)}, bf16[1024,256]{1,0:T(8,128)(2,1)S(1)}) custom-call(bf16[1024,1024]{1,0:T(8,128)(2,1)S(1)} %get-tuple-element.27.refs_0_, bf16[1024,1024]{1,0:T(8,128)(2,1)S(1)} %get-tuple-element.28.refs_1_, f32[128,1024]{1,0:T(8,128)S(1)} %collective-permute-done.4.refs_2_, f32[128,1024]{1,0:T(8,128)S(1)} %collective-permute-done.8.refs_3_), custom_call_target="tpu_custom_call" | custom-call | flops 1610612736 | bytes 5242880 | tf_op jit(solution)/shard_map/pallas_call | solution.py:119
  88.4 0.9 collective-permute-done.13.refs_4_
  89.3 1.4 %shard_map.56 = f32[1024,128]{1,0:T(8,128)S(1)} custom-call(s32[5]{0:T(128)S(1)} %stack.23.table_ref, bf16[1024,256]{1,0:T(8,128)(2,1)S(1)} %get-tuple-element.31.refs_0_, bf16[1024,256]{1,0:T(8,128)(2,1)S(1)} %get-tuple-element.32.refs_1_, bf16[1024,256]{1,0:T(8,128)(2,1)S(1)} %get-tuple-element.34.refs_2_, ...), custom_call_target="tpu_custom_call" | custom-call | flops 402653184 | bytes 393216 | tf_op jit(solution)/shard_map/pallas_call | solution.py:162
  90.7 1.4 %shard_map.55 = f32[1024,128]{1,0:T(8,128)S(1)} custom-call(s32[5]{0:T(128)S(1)} %stack.23.table_ref, bf16[1024,256]{1,0:T(8,128)(2,1)S(1)} %get-tuple-element.31.refs_0_, bf16[1024,256]{1,0:T(8,128)(2,1)S(1)} %get-tuple-element.32.refs_1_, bf16[1024,256]{1,0:T(8,128)(2,1)S(1)} %get-tuple-element.34.refs_2_, ...), custom_call_target="tpu_custom_call" | custom-call | flops 402653184 | bytes 393216 | tf_op jit(solution)/shard_map/pallas_call | solution.py:162
  92.6 0.8 sub.3
  (37 shorter events, 5.8 us)
Async XLA Ops:
  0.0 8.6 %copy-start.2 = (f32[8,1,128,256]{3,2,1,0:T(8,128)S(1)}, f32[8,1,128,256]{3,2,1,0:T(8,128)}, u32[]{:S(2)}) copy-start(f32[8,1,128,256]{3,2,1,0:T(8,128)} %param.4) | copy-start | bytes 3145732
  2.5 19.3 %collective-permute-start.5 = (f32[128,1024]{1,0:T(8,128)S(1)}, f32[128,1024]{1,0:T(8,128)S(1)}, u32[]{:S(2)}, u32[]{:S(2)}) collective-permute-start(f32[128,1024]{1,0:T(8,128)S(1)} %shard_map.46.refs_2_), channel_id=1, source_target_pairs={{0,4},{2,6},{4,0},{6,2},{8,12},{10,14},{12,8},{14,10},{1,5},{3,7},... | collective-permute-start | bytes 1572872 | tf_op jit(solution)/shard_map/ppermute | solution.py:241
  8.6 25.7 %copy-start = (f32[1024,1024]{1,0:T(8,128)S(1)}, f32[1024,1024]{1,0:T(8,128)}, u32[]{:S(2)}) copy-start(f32[1024,1024]{1,0:T(8,128)} %x_ref.1) | copy-start | bytes 12582916
  9.2 9.2 %collective-permute-start.14 = (f32[2,128,256]{2,1,0:T(8,128)S(1)}, f32[2,128,256]{2,1,0:T(8,128)S(1)}, u32[]{:S(2)}, u32[]{:S(2)}) collective-permute-start(f32[2,128,256]{2,1,0:T(8,128)S(1)} %get-tuple-element.40), channel_id=1, source_target_pairs={{0,2},{2,0},{4,6},{6,4},{8,10},{10,8},{12,14},{14,12},{1,3},{3,1},... | collective-permute-start | bytes 786440 | tf_op jit(solution)/shard_map/ppermute | solution.py:241
  10.7 18.4 %collective-permute-start.1 = (f32[128,1024]{1,0:T(8,128)S(1)}, f32[128,1024]{1,0:T(8,128)S(1)}, u32[]{:S(2)}, u32[]{:S(2)}) collective-permute-start(f32[128,1024]{1,0:T(8,128)S(1)} %shard_map.46.refs_2_), channel_id=1, source_target_pairs={{4,8},{6,10},{8,4},{10,6},{5,9},{7,11},{9,5},{11,7},{20,24},{22,26... | collective-permute-start | bytes 1572872 | tf_op jit(solution)/shard_map/ppermute | solution.py:241
  11.4 12.6 %collective-permute-start.9 = (f32[2,128,256]{2,1,0:T(8,128)S(1)}, f32[2,128,256]{2,1,0:T(8,128)S(1)}, u32[]{:S(2)}, u32[]{:S(2)}) collective-permute-start(f32[2,128,256]{2,1,0:T(8,128)S(1)} %get-tuple-element.38), channel_id=1, source_target_pairs={{0,2},{2,0},{4,6},{6,4},{8,10},{10,8},{12,14},{14,12},{1,3},{3,1},... | collective-permute-start | bytes 786440 | tf_op jit(solution)/shard_map/ppermute | solution.py:241
  18.4 9.9 %collective-permute-start.15 = (f32[2,128,256]{2,1,0:T(8,128)S(1)}, f32[2,128,256]{2,1,0:T(8,128)S(1)}, u32[]{:S(2)}, u32[]{:S(2)}) collective-permute-start(f32[2,128,256]{2,1,0:T(8,128)S(1)} %add.21), channel_id=1, source_target_pairs={{0,4},{2,6},{12,8},{14,10},{1,5},{3,7},{13,9},{15,11},{16,20},{18,... | collective-permute-start | bytes 786440 | tf_op jit(solution)/shard_map/ppermute | solution.py:241
  19.8 15.2 %collective-permute-start = (f32[128,1024]{1,0:T(8,128)S(1)}, f32[128,1024]{1,0:T(8,128)S(1)}, u32[]{:S(2)}, u32[]{:S(2)}) collective-permute-start(f32[128,1024]{1,0:T(8,128)S(1)} %shard_map.46.refs_2_), channel_id=1, source_target_pairs={{0,2},{2,0},{4,6},{6,4},{8,10},{10,8},{12,14},{14,12},{1,3},{3,1},... | collective-permute-start | bytes 1572872 | tf_op jit(solution)/shard_map/ppermute | solution.py:241
  21.9 25.6 %collective-permute-start.6 = (f32[128,1024]{1,0:T(8,128)S(1)}, f32[128,1024]{1,0:T(8,128)S(1)}, u32[]{:S(2)}, u32[]{:S(2)}) collective-permute-start(f32[128,1024]{1,0:T(8,128)S(1)} %collective-permute-done.5.refs_3_), channel_id=1, source_target_pairs={{4,8},{6,10},{8,4},{10,6},{5,9},{7,11},{9,5},{11,7},{20,24},{22,26... | collective-permute-start | bytes 1572872 | tf_op jit(solution)/shard_map/ppermute | solution.py:241
  24.1 8.2 %collective-permute-start.10 = (f32[2,128,256]{2,1,0:T(8,128)S(1)}, f32[2,128,256]{2,1,0:T(8,128)S(1)}, u32[]{:S(2)}, u32[]{:S(2)}) collective-permute-start(f32[2,128,256]{2,1,0:T(8,128)S(1)} %add.18), channel_id=1, source_target_pairs={{0,4},{2,6},{12,8},{14,10},{1,5},{3,7},{13,9},{15,11},{16,20},{18,... | collective-permute-start | bytes 786440 | tf_op jit(solution)/shard_map/ppermute | solution.py:241
  28.4 4.5 %collective-permute-start.16 = (f32[2,128,256]{2,1,0:T(8,128)S(1)}, f32[2,128,256]{2,1,0:T(8,128)S(1)}, u32[]{:S(2)}, u32[]{:S(2)}) collective-permute-start(f32[2,128,256]{2,1,0:T(8,128)S(1)} %add.22), channel_id=1, source_target_pairs={{4,8},{6,10},{8,4},{10,6},{5,9},{7,11},{9,5},{11,7},{20,24},{22,26... | collective-permute-start | bytes 786440 | tf_op jit(solution)/shard_map/ppermute | solution.py:241
  29.1 25.5 %collective-permute-start.2 = (f32[128,1024]{1,0:T(8,128)S(1)}, f32[128,1024]{1,0:T(8,128)S(1)}, u32[]{:S(2)}, u32[]{:S(2)}) collective-permute-start(f32[128,1024]{1,0:T(8,128)S(1)} %collective-permute-done.1), channel_id=1, source_target_pairs={{4,0},{6,2},{8,12},{10,14},{5,1},{7,3},{9,13},{11,15},{20,16},{22,... | collective-permute-start | bytes 1572872 | tf_op jit(solution)/shard_map/ppermute | solution.py:241
  32.3 18.5 %collective-permute-start.11 = (f32[2,128,256]{2,1,0:T(8,128)S(1)}, f32[2,128,256]{2,1,0:T(8,128)S(1)}, u32[]{:S(2)}, u32[]{:S(2)}) collective-permute-start(f32[2,128,256]{2,1,0:T(8,128)S(1)} %add.19), channel_id=1, source_target_pairs={{4,8},{6,10},{8,4},{10,6},{5,9},{7,11},{9,5},{11,7},{20,24},{22,26... | collective-permute-start | bytes 786440 | tf_op jit(solution)/shard_map/ppermute | solution.py:241
  33.0 20.9 %collective-permute-start.17 = (f32[2,128,256]{2,1,0:T(8,128)S(1)}, f32[2,128,256]{2,1,0:T(8,128)S(1)}, u32[]{:S(2)}, u32[]{:S(2)}) collective-permute-start(f32[2,128,256]{2,1,0:T(8,128)S(1)} %add.23), channel_id=1, source_target_pairs={{4,0},{6,2},{8,12},{10,14},{5,1},{7,3},{9,13},{11,15},{20,16},{22,... | collective-permute-start | bytes 786440 | tf_op jit(solution)/shard_map/ppermute | solution.py:241
  35.0 49.9 %collective-permute-start.4 = (f32[128,1024]{1,0:T(8,128)S(1)}, f32[128,1024]{1,0:T(8,128)S(1)}, u32[]{:S(2)}, u32[]{:S(2)}) collective-permute-start(f32[128,1024]{1,0:T(8,128)S(1)} %collective-permute-done.refs_2_), channel_id=1, source_target_pairs={{0,4},{2,6},{4,0},{6,2},{8,12},{10,14},{12,8},{14,10},{1,5},{3,7},... | collective-permute-start | bytes 1572872 | tf_op jit(solution)/shard_map/ppermute | solution.py:241
  47.5 28.3 %collective-permute-start.7 = (f32[128,1024]{1,0:T(8,128)S(1)}, f32[128,1024]{1,0:T(8,128)S(1)}, u32[]{:S(2)}, u32[]{:S(2)}) collective-permute-start(f32[128,1024]{1,0:T(8,128)S(1)} %collective-permute-done.6), channel_id=1, source_target_pairs={{4,0},{6,2},{8,12},{10,14},{5,1},{7,3},{9,13},{11,15},{20,16},{22,... | collective-permute-start | bytes 1572872 | tf_op jit(solution)/shard_map/ppermute | solution.py:241
  50.8 27.8 %collective-permute-start.12 = (f32[2,128,256]{2,1,0:T(8,128)S(1)}, f32[2,128,256]{2,1,0:T(8,128)S(1)}, u32[]{:S(2)}, u32[]{:S(2)}) collective-permute-start(f32[2,128,256]{2,1,0:T(8,128)S(1)} %add.20), channel_id=1, source_target_pairs={{4,0},{6,2},{8,12},{10,14},{5,1},{7,3},{9,13},{11,15},{20,16},{22,... | collective-permute-start | bytes 786440 | tf_op jit(solution)/shard_map/ppermute | solution.py:241
  53.9 34.5 %collective-permute-start.18 = (f32[2,128,256]{2,1,0:T(8,128)S(1)}, f32[2,128,256]{2,1,0:T(8,128)S(1)}, u32[]{:S(2)}, u32[]{:S(2)}) collective-permute-start(f32[2,128,256]{2,1,0:T(8,128)S(1)} %broadcast_select_fusion.2.refs_5_), channel_id=1, source_target_pairs={{0,2},{2,0},{4,6},{6,4},{8,10},{10,8},{12,14},{14,12},{1,3},{3,1},... | collective-permute-start | bytes 786440 | tf_op jit(solution)/shard_map/ppermute | solution.py:241
  54.7 26.6 %collective-permute-start.3 = (f32[128,1024]{1,0:T(8,128)S(1)}, f32[128,1024]{1,0:T(8,128)S(1)}, u32[]{:S(2)}, u32[]{:S(2)}) collective-permute-start(f32[128,1024]{1,0:T(8,128)S(1)} %broadcast_select_fusion.1.refs_2_), channel_id=1, source_target_pairs={{0,2},{2,0},{4,6},{6,4},{8,10},{10,8},{12,14},{14,12},{1,3},{3,1},... | collective-permute-start | bytes 1572872 | tf_op jit(solution)/shard_map/ppermute | solution.py:241
  75.9 10.6 %collective-permute-start.8 = (f32[128,1024]{1,0:T(8,128)S(1)}, f32[128,1024]{1,0:T(8,128)S(1)}, u32[]{:S(2)}, u32[]{:S(2)}) collective-permute-start(f32[128,1024]{1,0:T(8,128)S(1)} %broadcast_select_fusion.refs_3_), channel_id=1, source_target_pairs={{0,2},{2,0},{4,6},{6,4},{8,10},{10,8},{12,14},{14,12},{1,3},{3,1},... | collective-permute-start | bytes 1572872 | tf_op jit(solution)/shard_map/ppermute | solution.py:241
  78.6 10.6 %collective-permute-start.13 = (f32[2,128,256]{2,1,0:T(8,128)S(1)}, f32[2,128,256]{2,1,0:T(8,128)S(1)}, u32[]{:S(2)}, u32[]{:S(2)}) collective-permute-start(f32[2,128,256]{2,1,0:T(8,128)S(1)} %broadcast_select_fusion.3.refs_4_), channel_id=1, source_target_pairs={{0,2},{2,0},{4,6},{6,4},{8,10},{10,8},{12,14},{14,12},{1,3},{3,1},... | collective-permute-start | bytes 786440 | tf_op jit(solution)/shard_map/ppermute | solution.py:241
  81.2 1.9 %copy-start.1 = (f32[1024,256]{1,0:T(8,128)S(1)}, f32[1024,256]{1,0:T(8,128)}, u32[]{:S(2)}) copy-start(f32[1024,256]{1,0:T(8,128)} %refs_6_.1) | copy-start | bytes 3145732
  90.6 2.0 %collective-permute-start.19 = (f32[1024,128]{1,0:T(8,128)S(1)}, f32[1024,128]{1,0:T(8,128)S(1)}, u32[]{:S(2)}, u32[]{:S(2)}) collective-permute-start(f32[1024,128]{1,0:T(8,128)S(1)} %shard_map.56), channel_id=1, source_target_pairs={{0,1},{1,0},{2,3},{3,2},{4,5},{5,4},{6,7},{7,6},{8,9},{9,8},{10,11... | collective-permute-start | bytes 1572872 | tf_op jit(solution)/shard_map/ppermute | solution.py:314

commit v6 on v5

--- a/solution.py
+++ b/solution.py
@@ -113,7 +113,7 @@
         kh_ref[rows], kl_ref[rows] = halves(root * root)
 
 
-def gram(x_high, x_low, near, far, tile=512):
+def gram(x_high, x_low, near, far, tile=1024):
     rows, feats = x_high.shape
     points = 2 * near.shape[0]
     return pl.pallas_call(
@@ -170,7 +170,7 @@
     )(table, *in_vmem(*kerns), *runs, *in_vmem(*others))
 
 
-def apply_near(kerns, slots, runs, table, residual, parts, tile=512):
+def apply_near(kerns, slots, runs, table, residual, parts, tile=1024):
     rows, count = kerns[0].shape[0], len(kerns)
     half, rhs = runs[0].shape[1], runs[0].shape[2] // parts
 
@@ -191,7 +191,7 @@
     )
 
 
-def apply_far(kerns, slots, runs, table, base, mine, parts, tile=512):
+def apply_far(kerns, slots, runs, table, base, mine, parts, tile=1024):
     rows, count = kerns[0].shape[0], len(kerns)
     half, rhs = runs[0].shape[1], runs[0].shape[2] // parts
 

time: 93.8 us -> 93.8 us (level)
  no operation moved by 1% of the time
where the time goes in v6:
time: 93.8 us; the launch traced here: 93.5 us
  starting transfers between devices  37.1 us (40%)
  waiting for transfers between devices  36.4 us (39%)
  Pallas kernels  18.3 us (20%)
  other arithmetic  1.25 us (1%)
    ppermute x19, starting transfers between devices, permute(): return lax.ppermute(x, 'row', pairs)  37 us
    ppermute x19, waiting for transfers between devices, permute(): return lax.ppermute(x, 'row', pairs)  35.9 us
    pallas_call x4, Pallas kernels, gram(): pl.pallas_call(lambda *refs: gram_kernel(1.0 / feats, tile, *refs), in_sp...  7.36 us
    pallas_call x2, Pallas kernels, gather(): pl.pallas_call(lambda *refs: gather_kernel(count == ids.shape[0], *refs),...  5.39 us
    pallas_call x3, Pallas kernels, call(): pl.pallas_call(kernel, in_specs=[pl.BlockSpec(memory_space=pltpu.SMEM)] +...  4.37 us
  transfers between devices with their start and end apart: 20, of which 9 were waited for; matrix products, arithmetic and copies ran while one was open for 0% of the time, Pallas kernels for 16%

profile of v6, /device:TPU:0, one launch (start us, length us, event | category | flops | bytes accessed | tf_op | source)
XLA Modules:
  0.0 93.5 jit_solution(8606212721799172093)
XLA Ops:
  0.0 2.4 %shard_map.46.refs_2_ = f32[128,1024]{1,0:T(8,128)S(1)} custom-call(s32[256]{0:T(256)} %refs_0_.3, f32[1024,1024]{1,0:T(8,128)} %x_ref.1), custom_call_target="tpu_custom_call" | custom-call | bytes 1048576 | tf_op jit(solution)/shard_map/pallas_call | solution.py:66
  2.5 3.1 %collective-permute-start.5 = (f32[128,1024]{1,0:T(8,128)S(1)}, f32[128,1024]{1,0:T(8,128)S(1)}, u32[]{:S(2)}, u32[]{:S(2)}) collective-permute-start(f32[128,1024]{1,0:T(8,128)S(1)} %shard_map.46.refs_2_), channel_id=1, source_target_pairs={{0,4},{2,6},{4,0},{6,2},{8,12},{10,14},{12,8},{14,10},{1,5},{3,7},... | collective-permute-start | bytes 1572872 | tf_op jit(solution)/shard_map/ppermute | solution.py:241
  5.6 3.0 %shard_map.50.refs_1_ = f32[256,256]{1,0:T(8,128)S(1)} custom-call(s32[256]{0:T(256)} %refs_0_.3, f32[1024,256]{1,0:T(8,128)} %refs_6_.1), custom_call_target="tpu_custom_call" | custom-call | bytes 524288 | tf_op jit(solution)/shard_map/pallas_call | solution.py:66
  9.2 1.6 %collective-permute-start.14 = (f32[2,128,256]{2,1,0:T(8,128)S(1)}, f32[2,128,256]{2,1,0:T(8,128)S(1)}, u32[]{:S(2)}, u32[]{:S(2)}) collective-permute-start(f32[2,128,256]{2,1,0:T(8,128)S(1)} %get-tuple-element.40), channel_id=1, source_target_pairs={{0,2},{2,0},{4,6},{6,4},{8,10},{10,8},{12,14},{14,12},{1,3},{3,1},... | collective-permute-start | bytes 786440 | tf_op jit(solution)/shard_map/ppermute | solution.py:241
  11.4 0.7 collective-permute-start.9
  12.1 6.3 %collective-permute-done.14 = f32[2,128,256]{2,1,0:T(8,128)S(1)} collective-permute-done((f32[2,128,256]{2,1,0:T(8,128)S(1)}, f32[2,128,256]{2,1,0:T(8,128)S(1)}, u32[]{:S(2)}, u32[]{:S(2)}) %collective-permute-start.14) | collective-permute-done | bytes 262176 | tf_op jit(solution)/shard_map/ppermute | solution.py:241
  18.4 1.3 %collective-permute-start.15 = (f32[2,128,256]{2,1,0:T(8,128)S(1)}, f32[2,128,256]{2,1,0:T(8,128)S(1)}, u32[]{:S(2)}, u32[]{:S(2)}) collective-permute-start(f32[2,128,256]{2,1,0:T(8,128)S(1)} %add.21), channel_id=1, source_target_pairs={{0,4},{2,6},{12,8},{14,10},{1,5},{3,7},{13,9},{15,11},{16,20},{18,... | collective-permute-start | bytes 786440 | tf_op jit(solution)/shard_map/ppermute | solution.py:241
  19.8 2.1 %collective-permute-start = (f32[128,1024]{1,0:T(8,128)S(1)}, f32[128,1024]{1,0:T(8,128)S(1)}, u32[]{:S(2)}, u32[]{:S(2)}) collective-permute-start(f32[128,1024]{1,0:T(8,128)S(1)} %shard_map.46.refs_2_), channel_id=1, source_target_pairs={{0,2},{2,0},{4,6},{6,4},{8,10},{10,8},{12,14},{14,12},{1,3},{3,1},... | collective-permute-start | bytes 1572872 | tf_op jit(solution)/shard_map/ppermute | solution.py:241
  22.5 1.5 %collective-permute-done.9 = f32[2,128,256]{2,1,0:T(8,128)S(1)} collective-permute-done((f32[2,128,256]{2,1,0:T(8,128)S(1)}, f32[2,128,256]{2,1,0:T(8,128)S(1)}, u32[]{:S(2)}, u32[]{:S(2)}) %collective-permute-start.9) | collective-permute-done | bytes 262176 | tf_op jit(solution)/shard_map/ppermute | solution.py:241
  24.1 4.3 %collective-permute-start.10 = (f32[2,128,256]{2,1,0:T(8,128)S(1)}, f32[2,128,256]{2,1,0:T(8,128)S(1)}, u32[]{:S(2)}, u32[]{:S(2)}) collective-permute-start(f32[2,128,256]{2,1,0:T(8,128)S(1)} %add.18), channel_id=1, source_target_pairs={{0,4},{2,6},{12,8},{14,10},{1,5},{3,7},{13,9},{15,11},{16,20},{18,... | collective-permute-start | bytes 786440 | tf_op jit(solution)/shard_map/ppermute | solution.py:241
  29.1 1.3 %collective-permute-start.2 = (f32[128,1024]{1,0:T(8,128)S(1)}, f32[128,1024]{1,0:T(8,128)S(1)}, u32[]{:S(2)}, u32[]{:S(2)}) collective-permute-start(f32[128,1024]{1,0:T(8,128)S(1)} %collective-permute-done.1), channel_id=1, source_target_pairs={{4,0},{6,2},{8,12},{10,14},{5,1},{7,3},{9,13},{11,15},{20,16},{22,... | collective-permute-start | bytes 1572872 | tf_op jit(solution)/shard_map/ppermute | solution.py:241
  30.4 1.8 %collective-permute-done.10 = f32[2,128,256]{2,1,0:T(8,128)S(1)} collective-permute-done((f32[2,128,256]{2,1,0:T(8,128)S(1)}, f32[2,128,256]{2,1,0:T(8,128)S(1)}, u32[]{:S(2)}, u32[]{:S(2)}) %collective-permute-start.10) | collective-permute-done | bytes 262176 | tf_op jit(solution)/shard_map/ppermute | solution.py:241
  33.0 1.3 %collective-permute-start.17 = (f32[2,128,256]{2,1,0:T(8,128)S(1)}, f32[2,128,256]{2,1,0:T(8,128)S(1)}, u32[]{:S(2)}, u32[]{:S(2)}) collective-permute-start(f32[2,128,256]{2,1,0:T(8,128)S(1)} %add.23), channel_id=1, source_target_pairs={{4,0},{6,2},{8,12},{10,14},{5,1},{7,3},{9,13},{11,15},{20,16},{22,... | collective-permute-start | bytes 786440 | tf_op jit(solution)/shard_map/ppermute | solution.py:241
  35.0 12.5 %collective-permute-start.4 = (f32[128,1024]{1,0:T(8,128)S(1)}, f32[128,1024]{1,0:T(8,128)S(1)}, u32[]{:S(2)}, u32[]{:S(2)}) collective-permute-start(f32[128,1024]{1,0:T(8,128)S(1)} %collective-permute-done.refs_2_), channel_id=1, source_target_pairs={{0,4},{2,6},{4,0},{6,2},{8,12},{10,14},{12,8},{14,10},{1,5},{3,7},... | collective-permute-start | bytes 1572872 | tf_op jit(solution)/shard_map/ppermute | solution.py:241
  47.5 1.3 %collective-permute-start.7 = (f32[128,1024]{1,0:T(8,128)S(1)}, f32[128,1024]{1,0:T(8,128)S(1)}, u32[]{:S(2)}, u32[]{:S(2)}) collective-permute-start(f32[128,1024]{1,0:T(8,128)S(1)} %collective-permute-done.6), channel_id=1, source_target_pairs={{4,0},{6,2},{8,12},{10,14},{5,1},{7,3},{9,13},{11,15},{20,16},{22,... | collective-permute-start | bytes 1572872 | tf_op jit(solution)/shard_map/ppermute | solution.py:241
  48.8 1.8 %shard_map.52 = (bf16[1024,256]{1,0:T(8,128)(2,1)S(1)}, bf16[1024,256]{1,0:T(8,128)(2,1)S(1)}) custom-call(bf16[1024,1024]{1,0:T(8,128)(2,1)S(1)} %get-tuple-element.27.refs_0_, bf16[1024,1024]{1,0:T(8,128)(2,1)S(1)} %get-tuple-element.28.refs_1_, f32[128,1024]{1,0:T(8,128)S(1)} %shard_map.46.refs_2_, f32[128,1024]{1,0:T(8,128)S(1)} %collective-permute-done.5.refs_3_), custom_call_target="tpu_custom_call" | custom-call | flops 1610612736 | bytes 5242880 | tf_op jit(solution)/shard_map/pallas_call | solution.py:119
  50.7 1.3 %collective-permute-start.12 = (f32[2,128,256]{2,1,0:T(8,128)S(1)}, f32[2,128,256]{2,1,0:T(8,128)S(1)}, u32[]{:S(2)}, u32[]{:S(2)}) collective-permute-start(f32[2,128,256]{2,1,0:T(8,128)S(1)} %add.20), channel_id=1, source_target_pairs={{4,0},{6,2},{8,12},{10,14},{5,1},{7,3},{9,13},{11,15},{20,16},{22,... | collective-permute-start | bytes 786440 | tf_op jit(solution)/shard_map/ppermute | solution.py:241
  52.0 1.9 %collective-permute-done.17 = f32[2,128,256]{2,1,0:T(8,128)S(1)} collective-permute-done((f32[2,128,256]{2,1,0:T(8,128)S(1)}, f32[2,128,256]{2,1,0:T(8,128)S(1)}, u32[]{:S(2)}, u32[]{:S(2)}) %collective-permute-start.17) | collective-permute-done | bytes 262176 | tf_op jit(solution)/shard_map/ppermute | solution.py:241
  53.9 0.7 collective-permute-start.18
  54.7 1.5 %collective-permute-start.3 = (f32[128,1024]{1,0:T(8,128)S(1)}, f32[128,1024]{1,0:T(8,128)S(1)}, u32[]{:S(2)}, u32[]{:S(2)}) collective-permute-start(f32[128,1024]{1,0:T(8,128)S(1)} %broadcast_select_fusion.1.refs_2_), channel_id=1, source_target_pairs={{0,2},{2,0},{4,6},{6,4},{8,10},{10,8},{12,14},{14,12},{1,3},{3,1},... | collective-permute-start | bytes 1572872 | tf_op jit(solution)/shard_map/ppermute | solution.py:241
  56.2 19.6 %collective-permute-done.7 = f32[128,1024]{1,0:T(8,128)S(1)} collective-permute-done((f32[128,1024]{1,0:T(8,128)S(1)}, f32[128,1024]{1,0:T(8,128)S(1)}, u32[]{:S(2)}, u32[]{:S(2)}) %collective-permute-start.7) | collective-permute-done | bytes 524320 | tf_op jit(solution)/shard_map/ppermute | solution.py:241
  76.5 2.0 %collective-permute-done.12 = f32[2,128,256]{2,1,0:T(8,128)S(1)} collective-permute-done((f32[2,128,256]{2,1,0:T(8,128)S(1)}, f32[2,128,256]{2,1,0:T(8,128)S(1)}, u32[]{:S(2)}, u32[]{:S(2)}) %collective-permute-start.12) | collective-permute-done | bytes 262176 | tf_op jit(solution)/shard_map/ppermute | solution.py:241
  78.6 0.7 collective-permute-start.13
  79.3 1.8 %shard_map.53 = (bf16[1024,256]{1,0:T(8,128)(2,1)S(1)}, bf16[1024,256]{1,0:T(8,128)(2,1)S(1)}) custom-call(bf16[1024,1024]{1,0:T(8,128)(2,1)S(1)} %get-tuple-element.27.refs_0_, bf16[1024,1024]{1,0:T(8,128)(2,1)S(1)} %get-tuple-element.28.refs_1_, f32[128,1024]{1,0:T(8,128)S(1)} %broadcast_select_fusion.1.refs_2_, f32[128,1024]{1,0:T(8,128)S(1)} %broadcast_select_fusion.refs_3_), custom_call_target="tpu_custom_call" | custom-call | flops 1610612736 | bytes 5242880 | tf_op jit(solution)/shard_map/pallas_call | solution.py:119
  81.2 1.8 %shard_map.48 = (bf16[1024,256]{1,0:T(8,128)(2,1)S(1)}, bf16[1024,256]{1,0:T(8,128)(2,1)S(1)}) custom-call(bf16[1024,1024]{1,0:T(8,128)(2,1)S(1)} %get-tuple-element.27.refs_0_, bf16[1024,1024]{1,0:T(8,128)(2,1)S(1)} %get-tuple-element.28.refs_1_, f32[128,1024]{1,0:T(8,128)S(1)} %collective-permute-done.refs_2_, f32[128,1024]{1,0:T(8,128)S(1)} %collective-permute-done.3.refs_3_), custom_call_target="tpu_custom_call" | custom-call | flops 1610612736 | bytes 5242880 | tf_op jit(solution)/shard_map/pallas_call | solution.py:119
  83.0 1.7 %shard_map.54 = (f32[1024,128]{1,0:T(8,128)S(1)}, f32[1024,128]{1,0:T(8,128)S(1)}) custom-call(s32[5]{0:T(128)S(1)} %stack.23.table_ref, bf16[1024,256]{1,0:T(8,128)(2,1)S(1)} %get-tuple-element.41.refs_0_, bf16[1024,256]{1,0:T(8,128)(2,1)S(1)} %get-tuple-element.42.refs_1_, bf16[1024,256]{1,0:T(8,128)(2,1)S(1)} %get-tuple-element.43.refs_2_, ...), custom_call_target="tpu_custom_call" | custom-call | flops 805306368 | bytes 786432 | tf_op jit(solution)/shard_map/pallas_call | solution.py:162
  84.7 1.8 %collective-permute-done.8.refs_3_ = f32[128,1024]{1,0:T(8,128)S(1)} collective-permute-done((f32[128,1024]{1,0:T(8,128)S(1)}, f32[128,1024]{1,0:T(8,128)S(1)}, u32[]{:S(2)}, u32[]{:S(2)}) %collective-permute-start.8) | collective-permute-done | bytes 524320 | tf_op jit(solution)/shard_map/ppermute | solution.py:241
  86.5 1.8 %shard_map.49 = (bf16[1024,256]{1,0:T(8,128)(2,1)S(1)}, bf16[1024,256]{1,0:T(8,128)(2,1)S(1)}) custom-call(bf16[1024,1024]{1,0:T(8,128)(2,1)S(1)} %get-tuple-element.27.refs_0_, bf16[1024,1024]{1,0:T(8,128)(2,1)S(1)} %get-tuple-element.28.refs_1_, f32[128,1024]{1,0:T(8,128)S(1)} %collective-permute-done.4.refs_2_, f32[128,1024]{1,0:T(8,128)S(1)} %collective-permute-done.8.refs_3_), custom_call_target="tpu_custom_call" | custom-call | flops 1610612736 | bytes 5242880 | tf_op jit(solution)/shard_map/pallas_call | solution.py:119
  88.3 0.9 %collective-permute-done.13.refs_4_ = f32[2,128,256]{2,1,0:T(8,128)S(1)} collective-permute-done((f32[2,128,256]{2,1,0:T(8,128)S(1)}, f32[2,128,256]{2,1,0:T(8,128)S(1)}, u32[]{:S(2)}, u32[]{:S(2)}) %collective-permute-start.13) | collective-permute-done | bytes 262176 | tf_op jit(solution)/shard_map/ppermute | solution.py:241
  89.3 1.3 %shard_map.56 = f32[1024,128]{1,0:T(8,128)S(1)} custom-call(s32[5]{0:T(128)S(1)} %stack.23.table_ref, bf16[1024,256]{1,0:T(8,128)(2,1)S(1)} %get-tuple-element.31.refs_0_, bf16[1024,256]{1,0:T(8,128)(2,1)S(1)} %get-tuple-element.32.refs_1_, bf16[1024,256]{1,0:T(8,128)(2,1)S(1)} %get-tuple-element.34.refs_2_, ...), custom_call_target="tpu_custom_call" | custom-call | flops 402653184 | bytes 393216 | tf_op jit(solution)/shard_map/pallas_call | solution.py:162
  90.7 1.4 %shard_map.55 = f32[1024,128]{1,0:T(8,128)S(1)} custom-call(s32[5]{0:T(128)S(1)} %stack.23.table_ref, bf16[1024,256]{1,0:T(8,128)(2,1)S(1)} %get-tuple-element.31.refs_0_, bf16[1024,256]{1,0:T(8,128)(2,1)S(1)} %get-tuple-element.32.refs_1_, bf16[1024,256]{1,0:T(8,128)(2,1)S(1)} %get-tuple-element.34.refs_2_, ...), custom_call_target="tpu_custom_call" | custom-call | flops 402653184 | bytes 393216 | tf_op jit(solution)/shard_map/pallas_call | solution.py:162
  92.6 0.8 sub.3
  (37 shorter events, 5.8 us)
Async XLA Ops:
  0.0 8.6 %copy-start.2 = (f32[8,1,128,256]{3,2,1,0:T(8,128)S(1)}, f32[8,1,128,256]{3,2,1,0:T(8,128)}, u32[]{:S(2)}) copy-start(f32[8,1,128,256]{3,2,1,0:T(8,128)} %param.4) | copy-start | bytes 3145732
  2.5 19.3 %collective-permute-start.5 = (f32[128,1024]{1,0:T(8,128)S(1)}, f32[128,1024]{1,0:T(8,128)S(1)}, u32[]{:S(2)}, u32[]{:S(2)}) collective-permute-start(f32[128,1024]{1,0:T(8,128)S(1)} %shard_map.46.refs_2_), channel_id=1, source_target_pairs={{0,4},{2,6},{4,0},{6,2},{8,12},{10,14},{12,8},{14,10},{1,5},{3,7},... | collective-permute-start | bytes 1572872 | tf_op jit(solution)/shard_map/ppermute | solution.py:241
  8.6 25.7 %copy-start = (f32[1024,1024]{1,0:T(8,128)S(1)}, f32[1024,1024]{1,0:T(8,128)}, u32[]{:S(2)}) copy-start(f32[1024,1024]{1,0:T(8,128)} %x_ref.1) | copy-start | bytes 12582916
  9.2 9.2 %collective-permute-start.14 = (f32[2,128,256]{2,1,0:T(8,128)S(1)}, f32[2,128,256]{2,1,0:T(8,128)S(1)}, u32[]{:S(2)}, u32[]{:S(2)}) collective-permute-start(f32[2,128,256]{2,1,0:T(8,128)S(1)} %get-tuple-element.40), channel_id=1, source_target_pairs={{0,2},{2,0},{4,6},{6,4},{8,10},{10,8},{12,14},{14,12},{1,3},{3,1},... | collective-permute-start | bytes 786440 | tf_op jit(solution)/shard_map/ppermute | solution.py:241
  10.7 18.4 %collective-permute-start.1 = (f32[128,1024]{1,0:T(8,128)S(1)}, f32[128,1024]{1,0:T(8,128)S(1)}, u32[]{:S(2)}, u32[]{:S(2)}) collective-permute-start(f32[128,1024]{1,0:T(8,128)S(1)} %shard_map.46.refs_2_), channel_id=1, source_target_pairs={{4,8},{6,10},{8,4},{10,6},{5,9},{7,11},{9,5},{11,7},{20,24},{22,26... | collective-permute-start | bytes 1572872 | tf_op jit(solution)/shard_map/ppermute | solution.py:241
  11.4 12.6 %collective-permute-start.9 = (f32[2,128,256]{2,1,0:T(8,128)S(1)}, f32[2,128,256]{2,1,0:T(8,128)S(1)}, u32[]{:S(2)}, u32[]{:S(2)}) collective-permute-start(f32[2,128,256]{2,1,0:T(8,128)S(1)} %get-tuple-element.38), channel_id=1, source_target_pairs={{0,2},{2,0},{4,6},{6,4},{8,10},{10,8},{12,14},{14,12},{1,3},{3,1},... | collective-permute-start | bytes 786440 | tf_op jit(solution)/shard_map/ppermute | solution.py:241
  18.4 9.9 %collective-permute-start.15 = (f32[2,128,256]{2,1,0:T(8,128)S(1)}, f32[2,128,256]{2,1,0:T(8,128)S(1)}, u32[]{:S(2)}, u32[]{:S(2)}) collective-permute-start(f32[2,128,256]{2,1,0:T(8,128)S(1)} %add.21), channel_id=1, source_target_pairs={{0,4},{2,6},{12,8},{14,10},{1,5},{3,7},{13,9},{15,11},{16,20},{18,... | collective-permute-start | bytes 786440 | tf_op jit(solution)/shard_map/ppermute | solution.py:241
  19.8 15.2 %collective-permute-start = (f32[128,1024]{1,0:T(8,128)S(1)}, f32[128,1024]{1,0:T(8,128)S(1)}, u32[]{:S(2)}, u32[]{:S(2)}) collective-permute-start(f32[128,1024]{1,0:T(8,128)S(1)} %shard_map.46.refs_2_), channel_id=1, source_target_pairs={{0,2},{2,0},{4,6},{6,4},{8,10},{10,8},{12,14},{14,12},{1,3},{3,1},... | collective-permute-start | bytes 1572872 | tf_op jit(solution)/shard_map/ppermute | solution.py:241
  21.9 25.6 %collective-permute-start.6 = (f32[128,1024]{1,0:T(8,128)S(1)}, f32[128,1024]{1,0:T(8,128)S(1)}, u32[]{:S(2)}, u32[]{:S(2)}) collective-permute-start(f32[128,1024]{1,0:T(8,128)S(1)} %collective-permute-done.5.refs_3_), channel_id=1, source_target_pairs={{4,8},{6,10},{8,4},{10,6},{5,9},{7,11},{9,5},{11,7},{20,24},{22,26... | collective-permute-start | bytes 1572872 | tf_op jit(solution)/shard_map/ppermute | solution.py:241
  24.1 8.2 %collective-permute-start.10 = (f32[2,128,256]{2,1,0:T(8,128)S(1)}, f32[2,128,256]{2,1,0:T(8,128)S(1)}, u32[]{:S(2)}, u32[]{:S(2)}) collective-permute-start(f32[2,128,256]{2,1,0:T(8,128)S(1)} %add.18), channel_id=1, source_target_pairs={{0,4},{2,6},{12,8},{14,10},{1,5},{3,7},{13,9},{15,11},{16,20},{18,... | collective-permute-start | bytes 786440 | tf_op jit(solution)/shard_map/ppermute | solution.py:241
  28.4 4.5 %collective-permute-start.16 = (f32[2,128,256]{2,1,0:T(8,128)S(1)}, f32[2,128,256]{2,1,0:T(8,128)S(1)}, u32[]{:S(2)}, u32[]{:S(2)}) collective-permute-start(f32[2,128,256]{2,1,0:T(8,128)S(1)} %add.22), channel_id=1, source_target_pairs={{4,8},{6,10},{8,4},{10,6},{5,9},{7,11},{9,5},{11,7},{20,24},{22,26... | collective-permute-start | bytes 786440 | tf_op jit(solution)/shard_map/ppermute | solution.py:241
  29.1 25.5 %collective-permute-start.2 = (f32[128,1024]{1,0:T(8,128)S(1)}, f32[128,1024]{1,0:T(8,128)S(1)}, u32[]{:S(2)}, u32[]{:S(2)}) collective-permute-start(f32[128,1024]{1,0:T(8,128)S(1)} %collective-permute-done.1), channel_id=1, source_target_pairs={{4,0},{6,2},{8,12},{10,14},{5,1},{7,3},{9,13},{11,15},{20,16},{22,... | collective-permute-start | bytes 1572872 | tf_op jit(solution)/shard_map/ppermute | solution.py:241
  32.3 18.4 %collective-permute-start.11 = (f32[2,128,256]{2,1,0:T(8,128)S(1)}, f32[2,128,256]{2,1,0:T(8,128)S(1)}, u32[]{:S(2)}, u32[]{:S(2)}) collective-permute-start(f32[2,128,256]{2,1,0:T(8,128)S(1)} %add.19), channel_id=1, source_target_pairs={{4,8},{6,10},{8,4},{10,6},{5,9},{7,11},{9,5},{11,7},{20,24},{22,26... | collective-permute-start | bytes 786440 | tf_op jit(solution)/shard_map/ppermute | solution.py:241
  33.0 20.9 %collective-permute-start.17 = (f32[2,128,256]{2,1,0:T(8,128)S(1)}, f32[2,128,256]{2,1,0:T(8,128)S(1)}, u32[]{:S(2)}, u32[]{:S(2)}) collective-permute-start(f32[2,128,256]{2,1,0:T(8,128)S(1)} %add.23), channel_id=1, source_target_pairs={{4,0},{6,2},{8,12},{10,14},{5,1},{7,3},{9,13},{11,15},{20,16},{22,... | collective-permute-start | bytes 786440 | tf_op jit(solution)/shard_map/ppermute | solution.py:241
  35.0 49.8 %collective-permute-start.4 = (f32[128,1024]{1,0:T(8,128)S(1)}, f32[128,1024]{1,0:T(8,128)S(1)}, u32[]{:S(2)}, u32[]{:S(2)}) collective-permute-start(f32[128,1024]{1,0:T(8,128)S(1)} %collective-permute-done.refs_2_), channel_id=1, source_target_pairs={{0,4},{2,6},{4,0},{6,2},{8,12},{10,14},{12,8},{14,10},{1,5},{3,7},... | collective-permute-start | bytes 1572872 | tf_op jit(solution)/shard_map/ppermute | solution.py:241
  47.5 28.3 %collective-permute-start.7 = (f32[128,1024]{1,0:T(8,128)S(1)}, f32[128,1024]{1,0:T(8,128)S(1)}, u32[]{:S(2)}, u32[]{:S(2)}) collective-permute-start(f32[128,1024]{1,0:T(8,128)S(1)} %collective-permute-done.6), channel_id=1, source_target_pairs={{4,0},{6,2},{8,12},{10,14},{5,1},{7,3},{9,13},{11,15},{20,16},{22,... | collective-permute-start | bytes 1572872 | tf_op jit(solution)/shard_map/ppermute | solution.py:241
  50.7 27.9 %collective-permute-start.12 = (f32[2,128,256]{2,1,0:T(8,128)S(1)}, f32[2,128,256]{2,1,0:T(8,128)S(1)}, u32[]{:S(2)}, u32[]{:S(2)}) collective-permute-start(f32[2,128,256]{2,1,0:T(8,128)S(1)} %add.20), channel_id=1, source_target_pairs={{4,0},{6,2},{8,12},{10,14},{5,1},{7,3},{9,13},{11,15},{20,16},{22,... | collective-permute-start | bytes 786440 | tf_op jit(solution)/shard_map/ppermute | solution.py:241
  53.9 34.4 %collective-permute-start.18 = (f32[2,128,256]{2,1,0:T(8,128)S(1)}, f32[2,128,256]{2,1,0:T(8,128)S(1)}, u32[]{:S(2)}, u32[]{:S(2)}) collective-permute-start(f32[2,128,256]{2,1,0:T(8,128)S(1)} %broadcast_select_fusion.2.refs_5_), channel_id=1, source_target_pairs={{0,2},{2,0},{4,6},{6,4},{8,10},{10,8},{12,14},{14,12},{1,3},{3,1},... | collective-permute-start | bytes 786440 | tf_op jit(solution)/shard_map/ppermute | solution.py:241
  54.7 26.5 %collective-permute-start.3 = (f32[128,1024]{1,0:T(8,128)S(1)}, f32[128,1024]{1,0:T(8,128)S(1)}, u32[]{:S(2)}, u32[]{:S(2)}) collective-permute-start(f32[128,1024]{1,0:T(8,128)S(1)} %broadcast_select_fusion.1.refs_2_), channel_id=1, source_target_pairs={{0,2},{2,0},{4,6},{6,4},{8,10},{10,8},{12,14},{14,12},{1,3},{3,1},... | collective-permute-start | bytes 1572872 | tf_op jit(solution)/shard_map/ppermute | solution.py:241
  75.9 10.6 %collective-permute-start.8 = (f32[128,1024]{1,0:T(8,128)S(1)}, f32[128,1024]{1,0:T(8,128)S(1)}, u32[]{:S(2)}, u32[]{:S(2)}) collective-permute-start(f32[128,1024]{1,0:T(8,128)S(1)} %broadcast_select_fusion.refs_3_), channel_id=1, source_target_pairs={{0,2},{2,0},{4,6},{6,4},{8,10},{10,8},{12,14},{14,12},{1,3},{3,1},... | collective-permute-start | bytes 1572872 | tf_op jit(solution)/shard_map/ppermute | solution.py:241
  78.6 10.6 %collective-permute-start.13 = (f32[2,128,256]{2,1,0:T(8,128)S(1)}, f32[2,128,256]{2,1,0:T(8,128)S(1)}, u32[]{:S(2)}, u32[]{:S(2)}) collective-permute-start(f32[2,128,256]{2,1,0:T(8,128)S(1)} %broadcast_select_fusion.3.refs_4_), channel_id=1, source_target_pairs={{0,2},{2,0},{4,6},{6,4},{8,10},{10,8},{12,14},{14,12},{1,3},{3,1},... | collective-permute-start | bytes 786440 | tf_op jit(solution)/shard_map/ppermute | solution.py:241
  81.2 1.9 %copy-start.1 = (f32[1024,256]{1,0:T(8,128)S(1)}, f32[1024,256]{1,0:T(8,128)}, u32[]{:S(2)}) copy-start(f32[1024,256]{1,0:T(8,128)} %refs_6_.1) | copy-start | bytes 3145732
  90.6 2.0 %collective-permute-start.19 = (f32[1024,128]{1,0:T(8,128)S(1)}, f32[1024,128]{1,0:T(8,128)S(1)}, u32[]{:S(2)}, u32[]{:S(2)}) collective-permute-start(f32[1024,128]{1,0:T(8,128)S(1)} %shard_map.56), channel_id=1, source_target_pairs={{0,1},{1,0},{2,3},{3,2},{4,5},{5,4},{6,7},{7,6},{8,9},{9,8},{10,11... | collective-permute-start | bytes 1572872 | tf_op jit(solution)/shard_map/ppermute | solution.py:314

commit v7 on v6

--- a/solution.py
+++ b/solution.py
@@ -101,10 +101,12 @@
     return outs[:runs], outs[runs:]
 
 
-def gram_kernel(scale, tile, xh_ref, xl_ref, near_ref, far_ref, kh_ref, kl_ref, ph_ref, pl_ref):
-    half = near_ref.shape[0]
-    ph_ref[:half], pl_ref[:half] = halves(near_ref[...])
-    ph_ref[half:], pl_ref[half:] = halves(far_ref[...])
+def gram_kernel(scale, tile, xh_ref, xl_ref, *refs):
+    blocks, (kh_ref, kl_ref, ph_ref, pl_ref) = refs[:-4], refs[-4:]
+    half = blocks[0].shape[0]
+    for i, ref in enumerate(blocks):
+        rows = slice(i * half, (i + 1) * half)
+        ph_ref[rows], pl_ref[rows] = halves(ref[...])
     for r in range(0, kh_ref.shape[0], tile):
         rows = slice(r, r + tile)
         xh, ph = xh_ref[rows], ph_ref[...]
@@ -113,12 +115,12 @@
         kh_ref[rows], kl_ref[rows] = halves(root * root)
 
 
-def gram(x_high, x_low, near, far, tile=1024):
+def gram(x_high, x_low, *blocks, tile=1024):
     rows, feats = x_high.shape
-    points = 2 * near.shape[0]
+    points = len(blocks) * blocks[0].shape[0]
     return pl.pallas_call(
         lambda *refs: gram_kernel(1.0 / feats, tile, *refs),
-        in_specs=[VMEM] * 4,
+        in_specs=[VMEM] * (2 + len(blocks)),
         out_specs=[VMEM] * 2,
         out_shape=[pltpu.VMEM((rows, points), BF16)] * 2,
         scratch_shapes=[pltpu.VMEM((points, feats), BF16)] * 2,
@@ -126,7 +128,7 @@
         cost_estimate=pl.CostEstimate(
             flops=6 * rows * feats * points, bytes_accessed=4 * rows * (feats + points), transcendentals=0
         ),
-    )(*in_vmem(x_high, x_low), near, far)
+    )(*in_vmem(x_high, x_low), *blocks)
 
 
 def fill(c_ref, row, ref, place, cols):
@@ -303,11 +305,13 @@
         else:
             fars.append(permute(block, across))
     near_slots = list(range(depth))
-    far_slots = [0, 2, 1, 3] if depth == 4 else near_slots
+    far_groups = [[0, 2], [3], [1]] if depth == 4 else [[j, j + 1] for j in range(0, depth, 2)]
+    far_slots = sum(far_groups, [])
     near_kerns, far_kerns = [], []
     for i in range(0, depth, 2):
         near_kerns += gram(x_high, x_low, *[nears[j] for j in near_slots[i:i + 2]])
-        far_kerns += gram(x_high, x_low, *[fars[j] for j in far_slots[i:i + 2]])
+    for group in far_groups:
+        far_kerns += gram(x_high, x_low, *[fars[j] for j in group])
 
     theirs, mine = apply_near(near_kerns, near_slots, sames, table, residual, cols)
     theirs = apply_far(far_kerns, far_slots, crosses, table, theirs, False, cols)

time: 93.8 us -> 93.9 us (level)
  Pallas kernels: 18.3 us -> 20.2 us
  waiting for transfers between devices: 36.4 us -> 34.6 us
    ppermute x19, waiting for transfers between devices: 35.9 us -> 34.1 us  [permute(): return lax.ppermute(x, 'row', pairs)]
    pallas_call x4 -> x5, Pallas kernels: 7.36 us -> 9.11 us  [gram(): pl.pallas_call(lambda *refs: gram_kernel(1.0 / feats, tile, *refs), in_sp...]
  transfers between devices with their start and end apart: 20 -> 20, of which waited for: 9 -> 8; matrix products, arithmetic and copies ran while one was open for 0% -> 0% of each run, Pallas kernels for 16% -> 17%
where the time goes in v7:
time: 93.9 us; the launch traced here: 93.5 us
  starting transfers between devices  37.1 us (40%)
  waiting for transfers between devices  34.6 us (37%)
  Pallas kernels  20.2 us (22%)
  other arithmetic  1.26 us (1%)
    ppermute x19, starting transfers between devices, permute(): return lax.ppermute(x, 'row', pairs)  37 us
    ppermute x19, waiting for transfers between devices, permute(): return lax.ppermute(x, 'row', pairs)  34.1 us
    pallas_call x5, Pallas kernels, gram(): pl.pallas_call(lambda *refs: gram_kernel(1.0 / feats, tile, *refs), in_sp...  9.11 us
    pallas_call x2, Pallas kernels, gather(): pl.pallas_call(lambda *refs: gather_kernel(count == ids.shape[0], *refs),...  5.39 us
    pallas_call x3, Pallas kernels, call(): pl.pallas_call(kernel, in_specs=[pl.BlockSpec(memory_space=pltpu.SMEM)] +...  4.44 us
  transfers between devices with their start and end apart: 20, of which 8 were waited for; matrix products, arithmetic and copies ran while one was open for 0% of the time, Pallas kernels for 17%

profile of v7, /device:TPU:0, one launch (start us, length us, event | category | flops | bytes accessed | tf_op | source)
XLA Modules:
  0.0 93.5 jit_solution(636740209652011301)
XLA Ops:
  0.0 2.4 %shard_map.46.refs_2_ = f32[128,1024]{1,0:T(8,128)S(1)} custom-call(s32[256]{0:T(256)} %refs_0_.3, f32[1024,1024]{1,0:T(8,128)} %x_ref.1), custom_call_target="tpu_custom_call" | custom-call | bytes 1048576 | tf_op jit(solution)/shard_map/pallas_call | solution.py:66
  2.5 3.1 %collective-permute-start.4 = (f32[128,1024]{1,0:T(8,128)S(1)}, f32[128,1024]{1,0:T(8,128)S(1)}, u32[]{:S(2)}, u32[]{:S(2)}) collective-permute-start(f32[128,1024]{1,0:T(8,128)S(1)} %shard_map.46.refs_2_), channel_id=1, source_target_pairs={{0,4},{2,6},{4,0},{6,2},{8,12},{10,14},{12,8},{14,10},{1,5},{3,7},... | collective-permute-start | bytes 1572872 | tf_op jit(solution)/shard_map/ppermute | solution.py:243
  5.6 3.0 %shard_map.51.refs_1_ = f32[256,256]{1,0:T(8,128)S(1)} custom-call(s32[256]{0:T(256)} %refs_0_.3, f32[1024,256]{1,0:T(8,128)} %refs_6_.1), custom_call_target="tpu_custom_call" | custom-call | bytes 524288 | tf_op jit(solution)/shard_map/pallas_call | solution.py:66
  9.2 1.6 %collective-permute-start.14 = (f32[2,128,256]{2,1,0:T(8,128)S(1)}, f32[2,128,256]{2,1,0:T(8,128)S(1)}, u32[]{:S(2)}, u32[]{:S(2)}) collective-permute-start(f32[2,128,256]{2,1,0:T(8,128)S(1)} %get-tuple-element.44), channel_id=1, source_target_pairs={{0,2},{2,0},{4,6},{6,4},{8,10},{10,8},{12,14},{14,12},{1,3},{3,1},... | collective-permute-start | bytes 786440 | tf_op jit(solution)/shard_map/ppermute | solution.py:243
  11.4 0.7 collective-permute-start.9
  12.1 6.3 %collective-permute-done.14 = f32[2,128,256]{2,1,0:T(8,128)S(1)} collective-permute-done((f32[2,128,256]{2,1,0:T(8,128)S(1)}, f32[2,128,256]{2,1,0:T(8,128)S(1)}, u32[]{:S(2)}, u32[]{:S(2)}) %collective-permute-start.14) | collective-permute-done | bytes 262176 | tf_op jit(solution)/shard_map/ppermute | solution.py:243
  18.4 1.3 %collective-permute-start.15 = (f32[2,128,256]{2,1,0:T(8,128)S(1)}, f32[2,128,256]{2,1,0:T(8,128)S(1)}, u32[]{:S(2)}, u32[]{:S(2)}) collective-permute-start(f32[2,128,256]{2,1,0:T(8,128)S(1)} %add.21), channel_id=1, source_target_pairs={{0,4},{2,6},{12,8},{14,10},{1,5},{3,7},{13,9},{15,11},{16,20},{18,... | collective-permute-start | bytes 786440 | tf_op jit(solution)/shard_map/ppermute | solution.py:243
  19.8 2.1 %collective-permute-start = (f32[128,1024]{1,0:T(8,128)S(1)}, f32[128,1024]{1,0:T(8,128)S(1)}, u32[]{:S(2)}, u32[]{:S(2)}) collective-permute-start(f32[128,1024]{1,0:T(8,128)S(1)} %shard_map.46.refs_2_), channel_id=1, source_target_pairs={{0,2},{2,0},{4,6},{6,4},{8,10},{10,8},{12,14},{14,12},{1,3},{3,1},... | collective-permute-start | bytes 1572872 | tf_op jit(solution)/shard_map/ppermute | solution.py:243
  22.5 1.5 %collective-permute-done.9 = f32[2,128,256]{2,1,0:T(8,128)S(1)} collective-permute-done((f32[2,128,256]{2,1,0:T(8,128)S(1)}, f32[2,128,256]{2,1,0:T(8,128)S(1)}, u32[]{:S(2)}, u32[]{:S(2)}) %collective-permute-start.9) | collective-permute-done | bytes 262176 | tf_op jit(solution)/shard_map/ppermute | solution.py:243
  24.1 4.3 %collective-permute-start.10 = (f32[2,128,256]{2,1,0:T(8,128)S(1)}, f32[2,128,256]{2,1,0:T(8,128)S(1)}, u32[]{:S(2)}, u32[]{:S(2)}) collective-permute-start(f32[2,128,256]{2,1,0:T(8,128)S(1)} %add.18), channel_id=1, source_target_pairs={{0,4},{2,6},{12,8},{14,10},{1,5},{3,7},{13,9},{15,11},{16,20},{18,... | collective-permute-start | bytes 786440 | tf_op jit(solution)/shard_map/ppermute | solution.py:243
  29.1 1.3 %collective-permute-start.2 = (f32[128,1024]{1,0:T(8,128)S(1)}, f32[128,1024]{1,0:T(8,128)S(1)}, u32[]{:S(2)}, u32[]{:S(2)}) collective-permute-start(f32[128,1024]{1,0:T(8,128)S(1)} %collective-permute-done.1), channel_id=1, source_target_pairs={{4,0},{6,2},{8,12},{10,14},{5,1},{7,3},{9,13},{11,15},{20,16},{22,... | collective-permute-start | bytes 1572872 | tf_op jit(solution)/shard_map/ppermute | solution.py:243
  30.4 1.8 %collective-permute-done.10 = f32[2,128,256]{2,1,0:T(8,128)S(1)} collective-permute-done((f32[2,128,256]{2,1,0:T(8,128)S(1)}, f32[2,128,256]{2,1,0:T(8,128)S(1)}, u32[]{:S(2)}, u32[]{:S(2)}) %collective-permute-start.10) | collective-permute-done | bytes 262176 | tf_op jit(solution)/shard_map/ppermute | solution.py:243
  33.0 1.3 %collective-permute-start.17 = (f32[2,128,256]{2,1,0:T(8,128)S(1)}, f32[2,128,256]{2,1,0:T(8,128)S(1)}, u32[]{:S(2)}, u32[]{:S(2)}) collective-permute-start(f32[2,128,256]{2,1,0:T(8,128)S(1)} %add.23), channel_id=1, source_target_pairs={{4,0},{6,2},{8,12},{10,14},{5,1},{7,3},{9,13},{11,15},{20,16},{22,... | collective-permute-start | bytes 786440 | tf_op jit(solution)/shard_map/ppermute | solution.py:243
  35.0 12.5 %collective-permute-start.8 = (f32[128,1024]{1,0:T(8,128)S(1)}, f32[128,1024]{1,0:T(8,128)S(1)}, u32[]{:S(2)}, u32[]{:S(2)}) collective-permute-start(f32[128,1024]{1,0:T(8,128)S(1)} %collective-permute-done.refs_2_), channel_id=1, source_target_pairs={{0,4},{2,6},{4,0},{6,2},{8,12},{10,14},{12,8},{14,10},{1,5},{3,7},... | collective-permute-start | bytes 1572872 | tf_op jit(solution)/shard_map/ppermute | solution.py:243
  47.5 1.3 %collective-permute-start.6 = (f32[128,1024]{1,0:T(8,128)S(1)}, f32[128,1024]{1,0:T(8,128)S(1)}, u32[]{:S(2)}, u32[]{:S(2)}) collective-permute-start(f32[128,1024]{1,0:T(8,128)S(1)} %collective-permute-done.5), channel_id=1, source_target_pairs={{4,0},{6,2},{8,12},{10,14},{5,1},{7,3},{9,13},{11,15},{20,16},{22,... | collective-permute-start | bytes 1572872 | tf_op jit(solution)/shard_map/ppermute | solution.py:243
  48.8 1.8 %shard_map.53 = (bf16[1024,256]{1,0:T(8,128)(2,1)S(1)}, bf16[1024,256]{1,0:T(8,128)(2,1)S(1)}) custom-call(bf16[1024,1024]{1,0:T(8,128)(2,1)S(1)} %get-tuple-element.29.refs_0_, bf16[1024,1024]{1,0:T(8,128)(2,1)S(1)} %get-tuple-element.30.refs_1_, f32[128,1024]{1,0:T(8,128)S(1)} %shard_map.46.refs_2_, f32[128,1024]{1,0:T(8,128)S(1)} %collective-permute-done.4.refs_3_), custom_call_target="tpu_custom_call" | custom-call | flops 1610612736 | bytes 5242880 | tf_op jit(solution)/shard_map/pallas_call | solution.py:121
  50.7 1.3 %collective-permute-start.12 = (f32[2,128,256]{2,1,0:T(8,128)S(1)}, f32[2,128,256]{2,1,0:T(8,128)S(1)}, u32[]{:S(2)}, u32[]{:S(2)}) collective-permute-start(f32[2,128,256]{2,1,0:T(8,128)S(1)} %add.20), channel_id=1, source_target_pairs={{4,0},{6,2},{8,12},{10,14},{5,1},{7,3},{9,13},{11,15},{20,16},{22,... | collective-permute-start | bytes 786440 | tf_op jit(solution)/shard_map/ppermute | solution.py:243
  52.0 1.9 %collective-permute-done.17 = f32[2,128,256]{2,1,0:T(8,128)S(1)} collective-permute-done((f32[2,128,256]{2,1,0:T(8,128)S(1)}, f32[2,128,256]{2,1,0:T(8,128)S(1)}, u32[]{:S(2)}, u32[]{:S(2)}) %collective-permute-start.17) | collective-permute-done | bytes 262176 | tf_op jit(solution)/shard_map/ppermute | solution.py:243
  53.9 0.7 collective-permute-start.18
  54.7 1.5 %collective-permute-start.3 = (f32[128,1024]{1,0:T(8,128)S(1)}, f32[128,1024]{1,0:T(8,128)S(1)}, u32[]{:S(2)}, u32[]{:S(2)}) collective-permute-start(f32[128,1024]{1,0:T(8,128)S(1)} %broadcast_select_fusion.1.refs_2_), channel_id=1, source_target_pairs={{0,2},{2,0},{4,6},{6,4},{8,10},{10,8},{12,14},{14,12},{1,3},{3,1},... | collective-permute-start | bytes 1572872 | tf_op jit(solution)/shard_map/ppermute | solution.py:243
  56.2 19.6 %collective-permute-done.6 = f32[128,1024]{1,0:T(8,128)S(1)} collective-permute-done((f32[128,1024]{1,0:T(8,128)S(1)}, f32[128,1024]{1,0:T(8,128)S(1)}, u32[]{:S(2)}, u32[]{:S(2)}) %collective-permute-start.6) | collective-permute-done | bytes 524320 | tf_op jit(solution)/shard_map/ppermute | solution.py:243
  75.8 0.7 collective-permute-start.7
  76.5 2.0 %collective-permute-done.12 = f32[2,128,256]{2,1,0:T(8,128)S(1)} collective-permute-done((f32[2,128,256]{2,1,0:T(8,128)S(1)}, f32[2,128,256]{2,1,0:T(8,128)S(1)}, u32[]{:S(2)}, u32[]{:S(2)}) %collective-permute-start.12) | collective-permute-done | bytes 262176 | tf_op jit(solution)/shard_map/ppermute | solution.py:243
  79.3 1.8 %shard_map.50 = (bf16[1024,128]{1,0:T(8,128)(2,1)S(1)}, bf16[1024,128]{1,0:T(8,128)(2,1)S(1)}) custom-call(bf16[1024,1024]{1,0:T(8,128)(2,1)S(1)} %get-tuple-element.29.refs_0_, bf16[1024,1024]{1,0:T(8,128)(2,1)S(1)} %get-tuple-element.30.refs_1_, f32[128,1024]{1,0:T(8,128)S(1)} %collective-permute-done.8.refs_2_), custom_call_target="tpu_custom_call" | custom-call | flops 805306368 | bytes 4718592 | tf_op jit(solution)/shard_map/pallas_call | solution.py:121
  81.1 1.8 %shard_map.54 = (bf16[1024,256]{1,0:T(8,128)(2,1)S(1)}, bf16[1024,256]{1,0:T(8,128)(2,1)S(1)}) custom-call(bf16[1024,1024]{1,0:T(8,128)(2,1)S(1)} %get-tuple-element.29.refs_0_, bf16[1024,1024]{1,0:T(8,128)(2,1)S(1)} %get-tuple-element.30.refs_1_, f32[128,1024]{1,0:T(8,128)S(1)} %broadcast_select_fusion.1.refs_2_, f32[128,1024]{1,0:T(8,128)S(1)} %broadcast_select_fusion.refs_3_), custom_call_target="tpu_custom_call" | custom-call | flops 1610612736 | bytes 5242880 | tf_op jit(solution)/shard_map/pallas_call | solution.py:121
  83.0 1.7 %shard_map.55 = (f32[1024,128]{1,0:T(8,128)S(1)}, f32[1024,128]{1,0:T(8,128)S(1)}) custom-call(s32[5]{0:T(128)S(1)} %stack.23.table_ref, bf16[1024,256]{1,0:T(8,128)(2,1)S(1)} %get-tuple-element.45.refs_0_, bf16[1024,256]{1,0:T(8,128)(2,1)S(1)} %get-tuple-element.46.refs_1_, bf16[1024,256]{1,0:T(8,128)(2,1)S(1)} %get-tuple-element.47.refs_2_, ...), custom_call_target="tpu_custom_call" | custom-call | flops 805306368 | bytes 786432 | tf_op jit(solution)/shard_map/pallas_call | solution.py:164
  84.7 1.8 %shard_map.48 = (bf16[1024,256]{1,0:T(8,128)(2,1)S(1)}, bf16[1024,256]{1,0:T(8,128)(2,1)S(1)}) custom-call(bf16[1024,1024]{1,0:T(8,128)(2,1)S(1)} %get-tuple-element.29.refs_0_, bf16[1024,1024]{1,0:T(8,128)(2,1)S(1)} %get-tuple-element.30.refs_1_, f32[128,1024]{1,0:T(8,128)S(1)} %collective-permute-done.refs_2_, f32[128,1024]{1,0:T(8,128)S(1)} %collective-permute-done.3.refs_3_), custom_call_target="tpu_custom_call" | custom-call | flops 1610612736 | bytes 5242880 | tf_op jit(solution)/shard_map/pallas_call | solution.py:121
  86.5 1.8 %shard_map.49 = (bf16[1024,128]{1,0:T(8,128)(2,1)S(1)}, bf16[1024,128]{1,0:T(8,128)(2,1)S(1)}) custom-call(bf16[1024,1024]{1,0:T(8,128)(2,1)S(1)} %get-tuple-element.29.refs_0_, bf16[1024,1024]{1,0:T(8,128)(2,1)S(1)} %get-tuple-element.30.refs_1_, f32[128,1024]{1,0:T(8,128)S(1)} %collective-permute-done.7.refs_2_), custom_call_target="tpu_custom_call" | custom-call | flops 805306368 | bytes 4718592 | tf_op jit(solution)/shard_map/pallas_call | solution.py:121
  88.3 0.9 collective-permute-done.13.refs_6_
  89.3 1.4 %shard_map.57 = f32[1024,128]{1,0:T(8,128)S(1)} custom-call(s32[5]{0:T(128)S(1)} %stack.23.table_ref, bf16[1024,256]{1,0:T(8,128)(2,1)S(1)} %get-tuple-element.33.refs_0_, bf16[1024,256]{1,0:T(8,128)(2,1)S(1)} %get-tuple-element.34.refs_1_, bf16[1024,128]{1,0:T(8,128)(2,1)S(1)} %get-tuple-element.36.refs_2_, ...), custom_call_target="tpu_custom_call" | custom-call | flops 402653184 | bytes 393216 | tf_op jit(solution)/shard_map/pallas_call | solution.py:164
  90.7 1.4 %shard_map.56 = f32[1024,128]{1,0:T(8,128)S(1)} custom-call(s32[5]{0:T(128)S(1)} %stack.23.table_ref, bf16[1024,256]{1,0:T(8,128)(2,1)S(1)} %get-tuple-element.33.refs_0_, bf16[1024,256]{1,0:T(8,128)(2,1)S(1)} %get-tuple-element.34.refs_1_, bf16[1024,128]{1,0:T(8,128)(2,1)S(1)} %get-tuple-element.36.refs_2_, ...), custom_call_target="tpu_custom_call" | custom-call | flops 402653184 | bytes 393216 | tf_op jit(solution)/shard_map/pallas_call | solution.py:164
  92.6 0.8 sub.3
  (38 shorter events, 5.7 us)
Async XLA Ops:
  0.0 8.6 %copy-start.2 = (f32[8,1,128,256]{3,2,1,0:T(8,128)S(1)}, f32[8,1,128,256]{3,2,1,0:T(8,128)}, u32[]{:S(2)}) copy-start(f32[8,1,128,256]{3,2,1,0:T(8,128)} %param.4) | copy-start | bytes 3145732
  2.5 19.3 %collective-permute-start.4 = (f32[128,1024]{1,0:T(8,128)S(1)}, f32[128,1024]{1,0:T(8,128)S(1)}, u32[]{:S(2)}, u32[]{:S(2)}) collective-permute-start(f32[128,1024]{1,0:T(8,128)S(1)} %shard_map.46.refs_2_), channel_id=1, source_target_pairs={{0,4},{2,6},{4,0},{6,2},{8,12},{10,14},{12,8},{14,10},{1,5},{3,7},... | collective-permute-start | bytes 1572872 | tf_op jit(solution)/shard_map/ppermute | solution.py:243
  8.6 25.7 %copy-start = (f32[1024,1024]{1,0:T(8,128)S(1)}, f32[1024,1024]{1,0:T(8,128)}, u32[]{:S(2)}) copy-start(f32[1024,1024]{1,0:T(8,128)} %x_ref.1) | copy-start | bytes 12582916
  9.2 9.2 %collective-permute-start.14 = (f32[2,128,256]{2,1,0:T(8,128)S(1)}, f32[2,128,256]{2,1,0:T(8,128)S(1)}, u32[]{:S(2)}, u32[]{:S(2)}) collective-permute-start(f32[2,128,256]{2,1,0:T(8,128)S(1)} %get-tuple-element.44), channel_id=1, source_target_pairs={{0,2},{2,0},{4,6},{6,4},{8,10},{10,8},{12,14},{14,12},{1,3},{3,1},... | collective-permute-start | bytes 786440 | tf_op jit(solution)/shard_map/ppermute | solution.py:243
  10.7 18.4 %collective-permute-start.1 = (f32[128,1024]{1,0:T(8,128)S(1)}, f32[128,1024]{1,0:T(8,128)S(1)}, u32[]{:S(2)}, u32[]{:S(2)}) collective-permute-start(f32[128,1024]{1,0:T(8,128)S(1)} %shard_map.46.refs_2_), channel_id=1, source_target_pairs={{4,8},{6,10},{8,4},{10,6},{5,9},{7,11},{9,5},{11,7},{20,24},{22,26... | collective-permute-start | bytes 1572872 | tf_op jit(solution)/shard_map/ppermute | solution.py:243
  11.4 12.6 %collective-permute-start.9 = (f32[2,128,256]{2,1,0:T(8,128)S(1)}, f32[2,128,256]{2,1,0:T(8,128)S(1)}, u32[]{:S(2)}, u32[]{:S(2)}) collective-permute-start(f32[2,128,256]{2,1,0:T(8,128)S(1)} %get-tuple-element.42), channel_id=1, source_target_pairs={{0,2},{2,0},{4,6},{6,4},{8,10},{10,8},{12,14},{14,12},{1,3},{3,1},... | collective-permute-start | bytes 786440 | tf_op jit(solution)/shard_map/ppermute | solution.py:243
  18.4 9.9 %collective-permute-start.15 = (f32[2,128,256]{2,1,0:T(8,128)S(1)}, f32[2,128,256]{2,1,0:T(8,128)S(1)}, u32[]{:S(2)}, u32[]{:S(2)}) collective-permute-start(f32[2,128,256]{2,1,0:T(8,128)S(1)} %add.21), channel_id=1, source_target_pairs={{0,4},{2,6},{12,8},{14,10},{1,5},{3,7},{13,9},{15,11},{16,20},{18,... | collective-permute-start | bytes 786440 | tf_op jit(solution)/shard_map/ppermute | solution.py:243
  19.8 15.2 %collective-permute-start = (f32[128,1024]{1,0:T(8,128)S(1)}, f32[128,1024]{1,0:T(8,128)S(1)}, u32[]{:S(2)}, u32[]{:S(2)}) collective-permute-start(f32[128,1024]{1,0:T(8,128)S(1)} %shard_map.46.refs_2_), channel_id=1, source_target_pairs={{0,2},{2,0},{4,6},{6,4},{8,10},{10,8},{12,14},{14,12},{1,3},{3,1},... | collective-permute-start | bytes 1572872 | tf_op jit(solution)/shard_map/ppermute | solution.py:243
  21.9 25.6 %collective-permute-start.5 = (f32[128,1024]{1,0:T(8,128)S(1)}, f32[128,1024]{1,0:T(8,128)S(1)}, u32[]{:S(2)}, u32[]{:S(2)}) collective-permute-start(f32[128,1024]{1,0:T(8,128)S(1)} %collective-permute-done.4.refs_3_), channel_id=1, source_target_pairs={{4,8},{6,10},{8,4},{10,6},{5,9},{7,11},{9,5},{11,7},{20,24},{22,26... | collective-permute-start | bytes 1572872 | tf_op jit(solution)/shard_map/ppermute | solution.py:243
  24.1 8.2 %collective-permute-start.10 = (f32[2,128,256]{2,1,0:T(8,128)S(1)}, f32[2,128,256]{2,1,0:T(8,128)S(1)}, u32[]{:S(2)}, u32[]{:S(2)}) collective-permute-start(f32[2,128,256]{2,1,0:T(8,128)S(1)} %add.18), channel_id=1, source_target_pairs={{0,4},{2,6},{12,8},{14,10},{1,5},{3,7},{13,9},{15,11},{16,20},{18,... | collective-permute-start | bytes 786440 | tf_op jit(solution)/shard_map/ppermute | solution.py:243
  28.4 4.5 %collective-permute-start.16 = (f32[2,128,256]{2,1,0:T(8,128)S(1)}, f32[2,128,256]{2,1,0:T(8,128)S(1)}, u32[]{:S(2)}, u32[]{:S(2)}) collective-permute-start(f32[2,128,256]{2,1,0:T(8,128)S(1)} %add.22), channel_id=1, source_target_pairs={{4,8},{6,10},{8,4},{10,6},{5,9},{7,11},{9,5},{11,7},{20,24},{22,26... | collective-permute-start | bytes 786440 | tf_op jit(solution)/shard_map/ppermute | solution.py:243
  29.1 25.5 %collective-permute-start.2 = (f32[128,1024]{1,0:T(8,128)S(1)}, f32[128,1024]{1,0:T(8,128)S(1)}, u32[]{:S(2)}, u32[]{:S(2)}) collective-permute-start(f32[128,1024]{1,0:T(8,128)S(1)} %collective-permute-done.1), channel_id=1, source_target_pairs={{4,0},{6,2},{8,12},{10,14},{5,1},{7,3},{9,13},{11,15},{20,16},{22,... | collective-permute-start | bytes 1572872 | tf_op jit(solution)/shard_map/ppermute | solution.py:243
  32.3 18.4 %collective-permute-start.11 = (f32[2,128,256]{2,1,0:T(8,128)S(1)}, f32[2,128,256]{2,1,0:T(8,128)S(1)}, u32[]{:S(2)}, u32[]{:S(2)}) collective-permute-start(f32[2,128,256]{2,1,0:T(8,128)S(1)} %add.19), channel_id=1, source_target_pairs={{4,8},{6,10},{8,4},{10,6},{5,9},{7,11},{9,5},{11,7},{20,24},{22,26... | collective-permute-start | bytes 786440 | tf_op jit(solution)/shard_map/ppermute | solution.py:243
  33.0 20.9 %collective-permute-start.17 = (f32[2,128,256]{2,1,0:T(8,128)S(1)}, f32[2,128,256]{2,1,0:T(8,128)S(1)}, u32[]{:S(2)}, u32[]{:S(2)}) collective-permute-start(f32[2,128,256]{2,1,0:T(8,128)S(1)} %add.23), channel_id=1, source_target_pairs={{4,0},{6,2},{8,12},{10,14},{5,1},{7,3},{9,13},{11,15},{20,16},{22,... | collective-permute-start | bytes 786440 | tf_op jit(solution)/shard_map/ppermute | solution.py:243
  35.0 44.4 %collective-permute-start.8 = (f32[128,1024]{1,0:T(8,128)S(1)}, f32[128,1024]{1,0:T(8,128)S(1)}, u32[]{:S(2)}, u32[]{:S(2)}) collective-permute-start(f32[128,1024]{1,0:T(8,128)S(1)} %collective-permute-done.refs_2_), channel_id=1, source_target_pairs={{0,4},{2,6},{4,0},{6,2},{8,12},{10,14},{12,8},{14,10},{1,5},{3,7},... | collective-permute-start | bytes 1572872 | tf_op jit(solution)/shard_map/ppermute | solution.py:243
  47.5 28.3 %collective-permute-start.6 = (f32[128,1024]{1,0:T(8,128)S(1)}, f32[128,1024]{1,0:T(8,128)S(1)}, u32[]{:S(2)}, u32[]{:S(2)}) collective-permute-start(f32[128,1024]{1,0:T(8,128)S(1)} %collective-permute-done.5), channel_id=1, source_target_pairs={{4,0},{6,2},{8,12},{10,14},{5,1},{7,3},{9,13},{11,15},{20,16},{22,... | collective-permute-start | bytes 1572872 | tf_op jit(solution)/shard_map/ppermute | solution.py:243
  50.7 27.9 %collective-permute-start.12 = (f32[2,128,256]{2,1,0:T(8,128)S(1)}, f32[2,128,256]{2,1,0:T(8,128)S(1)}, u32[]{:S(2)}, u32[]{:S(2)}) collective-permute-start(f32[2,128,256]{2,1,0:T(8,128)S(1)} %add.20), channel_id=1, source_target_pairs={{4,0},{6,2},{8,12},{10,14},{5,1},{7,3},{9,13},{11,15},{20,16},{22,... | collective-permute-start | bytes 786440 | tf_op jit(solution)/shard_map/ppermute | solution.py:243
  53.9 34.4 %collective-permute-start.18 = (f32[2,128,256]{2,1,0:T(8,128)S(1)}, f32[2,128,256]{2,1,0:T(8,128)S(1)}, u32[]{:S(2)}, u32[]{:S(2)}) collective-permute-start(f32[2,128,256]{2,1,0:T(8,128)S(1)} %broadcast_select_fusion.2.refs_5_), channel_id=1, source_target_pairs={{0,2},{2,0},{4,6},{6,4},{8,10},{10,8},{12,14},{14,12},{1,3},{3,1},... | collective-permute-start | bytes 786440 | tf_op jit(solution)/shard_map/ppermute | solution.py:243
  54.7 30.0 %collective-permute-start.3 = (f32[128,1024]{1,0:T(8,128)S(1)}, f32[128,1024]{1,0:T(8,128)S(1)}, u32[]{:S(2)}, u32[]{:S(2)}) collective-permute-start(f32[128,1024]{1,0:T(8,128)S(1)} %broadcast_select_fusion.1.refs_2_), channel_id=1, source_target_pairs={{0,2},{2,0},{4,6},{6,4},{8,10},{10,8},{12,14},{14,12},{1,3},{3,1},... | collective-permute-start | bytes 1572872 | tf_op jit(solution)/shard_map/ppermute | solution.py:243
  75.8 10.7 %collective-permute-start.7 = (f32[128,1024]{1,0:T(8,128)S(1)}, f32[128,1024]{1,0:T(8,128)S(1)}, u32[]{:S(2)}, u32[]{:S(2)}) collective-permute-start(f32[128,1024]{1,0:T(8,128)S(1)} %broadcast_select_fusion.refs_3_), channel_id=1, source_target_pairs={{0,2},{2,0},{4,6},{6,4},{8,10},{10,8},{12,14},{14,12},{1,3},{3,1},... | collective-permute-start | bytes 1572872 | tf_op jit(solution)/shard_map/ppermute | solution.py:243
  78.6 10.7 %collective-permute-start.13 = (f32[2,128,256]{2,1,0:T(8,128)S(1)}, f32[2,128,256]{2,1,0:T(8,128)S(1)}, u32[]{:S(2)}, u32[]{:S(2)}) collective-permute-start(f32[2,128,256]{2,1,0:T(8,128)S(1)} %broadcast_select_fusion.3.refs_4_), channel_id=1, source_target_pairs={{0,2},{2,0},{4,6},{6,4},{8,10},{10,8},{12,14},{14,12},{1,3},{3,1},... | collective-permute-start | bytes 786440 | tf_op jit(solution)/shard_map/ppermute | solution.py:243
  81.1 1.9 %copy-start.1 = (f32[1024,256]{1,0:T(8,128)S(1)}, f32[1024,256]{1,0:T(8,128)}, u32[]{:S(2)}) copy-start(f32[1024,256]{1,0:T(8,128)} %refs_6_.1) | copy-start | bytes 3145732
  90.7 2.0 %collective-permute-start.19 = (f32[1024,128]{1,0:T(8,128)S(1)}, f32[1024,128]{1,0:T(8,128)S(1)}, u32[]{:S(2)}, u32[]{:S(2)}) collective-permute-start(f32[1024,128]{1,0:T(8,128)S(1)} %shard_map.57), channel_id=1, source_target_pairs={{0,1},{1,0},{2,3},{3,2},{4,5},{5,4},{6,7},{7,6},{8,9},{9,8},{10,11... | collective-permute-start | bytes 1572872 | tf_op jit(solution)/shard_map/ppermute | solution.py:318
